TPU v7x, 32 devices: a whole 2x2x4 slice. The times are simulated.
32 devices in a mesh: dp: 8 (over y, x, core), tensor: 4 (over z).
Axes of the slice: x: 2, y: 2, z: 4, core: 2. Of those that a mesh axis runs over, the one named last changes fastest.
Arguments:
- tokens: bfloat16 [8192, 768], P(('dp', 'tensor')), may hold values from -6 to 6
- lengths: int32 [8, 7], P('dp'), may hold values from 0 to 896, as said below
- query_weight: bfloat16 [768, 768], P(None, 'tensor'), may hold values from -0.109375 to 0.109375
- query_bias: float32 [768], P('tensor'), may hold values from -3 to 3
- key_weight: bfloat16 [768, 768], P(None, 'tensor'), may hold values from -0.109375 to 0.109375
- key_bias: float32 [768], P('tensor'), may hold values from -3 to 3
- value_weight: bfloat16 [768, 768], P(None, 'tensor'), may hold values from -0.21875 to 0.21875
- value_bias: float32 [768], P('tensor'), may hold values from -3 to 3
- feature_proj: bfloat16 [12, 64, 256], P('tensor'), may hold values from -4 to 4
- mixer_weight: bfloat16 [768, 768], P('tensor'), may hold values from -0.875 to 0.875
- mixer_bias: float32 [768], replicated, may hold values from -3 to 3
- first_gain: float32 [768], replicated, may hold values from 0.5 to 1.5
- first_shift: float32 [768], replicated, may hold values from -3 to 3
- hidden_weight: bfloat16 [768, 3072], P(None, 'tensor'), may hold values from -0.21875 to 0.21875
- hidden_bias: float32 [3072], P('tensor'), may hold values from -3 to 3
- output_weight: bfloat16 [3072, 768], P('tensor'), may hold values from -0.109375 to 0.109375
- output_bias: float32 [768], replicated, may hold values from -3 to 3
- second_gain: float32 [768], replicated, may hold values from 0.5 to 1.5
- second_shift: float32 [768], replicated, may hold values from -3 to 3
- cotangent: bfloat16 [8192, 768], P(('dp', 'tensor')), may hold values from -6 to 6
Outputs:
- layer_out: bfloat16 [8192, 768], P(('dp', 'tensor'))
- tokens_grad: float32 [8192, 768], P(('dp', 'tensor'))
- grad_query_weight: float32 [768, 768], P('dp', 'tensor')
- grad_query_bias: float32 [768], replicated
- grad_key_weight: float32 [768, 768], P('dp', 'tensor')
- grad_key_bias: float32 [768], replicated
- grad_value_weight: float32 [768, 768], P('dp', 'tensor')
- grad_value_bias: float32 [768], replicated
- grad_mixer_weight: float32 [768, 768], P('tensor', 'dp')
- grad_mixer_bias: float32 [768], replicated
- grad_first_gain: float32 [768], replicated
- grad_first_shift: float32 [768], replicated
- grad_hidden_weight: float32 [768, 3072], P('dp', 'tensor')
- grad_hidden_bias: float32 [3072], replicated
- grad_output_weight: float32 [3072, 768], P('tensor', 'dp')
- grad_output_bias: float32 [768], replicated
- grad_second_gain: float32 [768], replicated
- grad_second_shift: float32 [768], replicated
Inputs may be any that keep to these rules, and one draw needn't show every extreme that they name: lengths[r, 0] to lengths[r, 5] are the lengths of the sequences packed in order into row r (0 is an empty slot) and lengths[r, 6] the padding at the row's end; each row sums to 1024; some row holds a sequence of exactly 896 positions.
All inputs are finite; a program needn't handle non-finite values.
Results may differ from a plain program's by a relative error of at most 0.035.
Values may be sent and summed in bfloat16 or wider, within the bound.
No kernel may reach another device: no remote copies, remote signals or barrier semaphores. Data moves between devices by JAX's collectives and lax.ppermute only.
A program may use at most 192 MiB of HBM per device.

v0:
```python
import functools
import math

import jax
import jax.numpy as jnp
from jax import lax
from jax.experimental import pallas as pl
from jax.experimental.pallas import tpu as pltpu
from jax.sharding import PartitionSpec as P

HEAD_DIM = 64
FEAT = 256
PLANE = 8
VMEM_LIMIT = 60 * 1024 * 1024
COST_RATE = 9e8

eps = 1e-06
bf16 = jnp.bfloat16
f32 = jnp.float32


def dot(left, right):
    return jnp.dot(left, right, preferred_element_type=f32)


def dot_rows(left, right):
    return lax.dot_general(left, right, (((0,), (0,)), ((), ())), preferred_element_type=f32)


def dot_cols(left, right):
    return lax.dot_general(left, right, (((1,), (1,)), ((), ())), preferred_element_type=f32)


def cost(micros):
    return pl.CostEstimate(flops=int(micros * COST_RATE), transcendentals=0, bytes_accessed=0)


def pack_kernel(
    own_ref, bias_ref, tokens_ref, hidden_ref, mixer_ref, output_ref, xt_ref, first_ref, second_ref, held_ref, sems
):
    rows, columns = second_ref.shape
    chip = lax.shift_right_logical(own_ref[0], 1)
    core = lax.bitwise_and(own_ref[0], 1)
    mixer_rows = mixer_ref.shape[0] // (PLANE // 2)

    def copy(source, height, target, sem):
        begin = pl.multiple_of(chip * height, 16)
        return pltpu.make_async_copy(
            source.at[pl.ds(begin, height), lanes(core, columns)], target, sem
        )

    copies = [
        copy(hidden_ref, rows, first_ref.at[0:rows], sems.at[0]),
        copy(mixer_ref, mixer_rows, first_ref.at[rows : rows + mixer_rows], sems.at[1]),
        copy(output_ref, rows, second_ref, sems.at[2]),
    ]
    fetch = pltpu.make_async_copy(tokens_ref, held_ref, sems.at[3])
    fetch.start()
    start_all([copies])
    wide = bias_ref[...]
    parts = []
    for _ in range(3):
        part = wide.astype(bf16).astype(f32)
        wide = wide - part
        parts += [part[:, :columns], part[:, columns:]]
    parts.append(jnp.zeros((10, columns), f32))
    first_ref[rows + mixer_rows :] = jnp.concatenate(parts, axis=0).astype(bf16)
    fetch.wait()
    xt_ref[...] = held_ref[...].T
    wait_all(copies)


def pack(own, tokens, hidden_bias, hidden_weight, mixer_weight, output_weight):
    local, depth = tokens.shape
    chips = PLANE // 2
    columns = depth // 2
    rows = depth // chips
    first_rows = rows + mixer_weight.shape[0] // chips + 16
    vmem = pl.BlockSpec(memory_space=pltpu.VMEM)
    return pl.pallas_call(
        pack_kernel,
        in_specs=[pl.BlockSpec(memory_space=pltpu.SMEM), vmem] + [pl.BlockSpec(memory_space=pltpu.HBM)] * 4,
        out_specs=[vmem] * 3,
        out_shape=[
            jax.ShapeDtypeStruct((depth, local), bf16),
            jax.ShapeDtypeStruct((first_rows, columns), bf16),
            jax.ShapeDtypeStruct((rows, columns), bf16),
        ],
        scratch_shapes=[pltpu.VMEM((local, depth), bf16), pltpu.SemaphoreType.DMA((4,))],
        compiler_params=pltpu.CompilerParams(vmem_limit_bytes=VMEM_LIMIT),
        cost_estimate=cost(3),
        name="pack",
    )(own, hidden_bias, tokens, hidden_weight, mixer_weight, output_weight)


def unpack_bias(entries):
    wide = entries.astype(f32)
    return jnp.concatenate([wide[0:1] + wide[2:3] + wide[4:5], wide[1:2] + wide[3:4] + wide[5:6]], axis=1)


def prepare_kernel(
    query_ref, key_ref, value_ref, query_bias_ref, key_bias_ref, value_bias_ref, proj_ref, joined_ref, turned_ref, bias_ref, proj_t_ref
):
    width = query_ref.shape[1]
    weights = [query_ref[...], key_ref[...], value_ref[...]]
    joined_ref[...] = jnp.concatenate(weights, axis=1)
    for kind, weight in enumerate(weights):
        turned_ref[kind * width : (kind + 1) * width] = weight.T
    for kind, bias in enumerate((query_bias_ref, key_bias_ref, value_bias_ref)):
        bias_ref[kind * width : (kind + 1) * width] = jnp.broadcast_to(bias[...], (8, width)).T
    for h in range(proj_ref.shape[0]):
        proj_t_ref[h] = proj_ref[h].T


def prepare(weights, biases, proj):
    depth, width = weights[0].shape
    heads, head_dim, feat = proj.shape
    vmem = pl.BlockSpec(memory_space=pltpu.VMEM)
    return pl.pallas_call(
        prepare_kernel,
        in_specs=[vmem] * 7,
        out_specs=[vmem] * 4,
        out_shape=[
            jax.ShapeDtypeStruct((depth, 3 * width), bf16),
            jax.ShapeDtypeStruct((3 * width, depth), bf16),
            jax.ShapeDtypeStruct((3 * width, 8), f32),
            jax.ShapeDtypeStruct((heads, feat, head_dim), bf16),
        ],
        compiler_params=pltpu.CompilerParams(vmem_limit_bytes=VMEM_LIMIT),
        cost_estimate=cost(4),
        name="prepare",
    )(*weights, *biases, proj)


def lanes(index, size):
    return pl.ds(pl.multiple_of(index * size, size), size)


def segments(lengths_ref, count, shape):
    places = lax.broadcasted_iota(jnp.int32, shape, len(shape) - 1)
    seg = jnp.zeros(shape, jnp.int32)
    end = jnp.int32(0)
    for s in range(count):
        end = end + lengths_ref[0, s]
        seg = seg + (places >= end).astype(jnp.int32)
    return seg


def masked_copies(seg, entries, count):
    zero = jnp.zeros_like(entries)
    return [jnp.where(seg == s, entries, zero) for s in range(count)]


def one_hot_rows(seg, count):
    rows = lax.broadcasted_iota(jnp.int32, (8, seg.shape[1]), 0)
    return jnp.where((rows == seg) & (rows < count), 1.0, 0.0).astype(f32)


def masked_sum(seg, wide, count):
    height = HEAD_DIM
    total = jnp.zeros((height, wide.shape[1]), f32)
    for s in range(count):
        total = total + jnp.where(seg == s, wide[s * height : (s + 1) * height], 0.0)
    return total


def feature_rows(vectors, proj_t):
    scale = HEAD_DIM ** (-0.25)
    widened = vectors.astype(f32)
    square = (0.5 * scale * scale) * jnp.sum(widened * widened, axis=0, keepdims=True)
    return (jnp.exp(scale * dot(proj_t, vectors) - square) * (1.0 / math.sqrt(FEAT))).astype(bf16)


def attend_kernel(
    count,
    lengths_ref,
    place_ref,
    xt_ref,
    wt_ref,
    bias_ref,
    proj_t_ref,
    qkv_ref,
    qf_ref,
    kf_ref,
    state_ref,
    out_ref,
    den_ref,
    p0_ref,
    p1_ref,
    p2_ref,
    p3_ref,
    mixed_ref,
):
    h = pl.program_id(0)
    shards, _, local = xt_ref.shape
    heads = pl.num_programs(0)
    width = wt_ref.shape[0] // 3
    spread_rows = count * HEAD_DIM

    @pl.when(h == 0)
    def _():
        for s in range(shards):
            qkv_ref[:, s * local : (s + 1) * local] = (
                dot(wt_ref[...], xt_ref[s]) + bias_ref[:, 0:1]
            ).astype(bf16)

    def rows(kind):
        begin = pl.multiple_of(kind * width + h * HEAD_DIM, HEAD_DIM)
        return qkv_ref[pl.ds(begin, HEAD_DIM), :]

    seg = segments(lengths_ref, count, (1, shards * local))
    hot = one_hot_rows(seg, count)
    proj_t = proj_t_ref[0]
    q_feat = feature_rows(rows(0), proj_t)
    k_feat = feature_rows(rows(1), proj_t)
    qf_ref[0] = q_feat
    kf_ref[0] = k_feat
    wide = jnp.concatenate(
        masked_copies(seg, rows(2), count) + [jnp.concatenate([hot, hot], axis=0).astype(bf16)], axis=0
    )
    state = dot_cols(wide, k_feat)
    sums = state[spread_rows : spread_rows + 8]
    high = sums.astype(bf16).astype(f32)
    state_ref[0, :spread_rows] = state[:spread_rows].astype(bf16)
    state_ref[0, spread_rows : spread_rows + 16] = jnp.concatenate([high, high], axis=0).astype(bf16)
    state_ref[0, spread_rows + 16 :] = jnp.concatenate(
        [sums - high, jnp.zeros_like(high)], axis=0
    ).astype(bf16)
    through = dot(state_ref[0], q_feat)
    scores = through[spread_rows : spread_rows + 8] + through[spread_rows + 16 : spread_rows + 24]
    den = jnp.sum(hot * scores, axis=0, keepdims=True) + (seg >= count).astype(f32)
    out = masked_sum(seg, through, count) / den
    out_ref[...] = out
    den_ref[0] = jnp.broadcast_to(den, den_ref.shape[1:])
    mixed_ref[pl.ds(pl.multiple_of(h * HEAD_DIM, HEAD_DIM), HEAD_DIM), :] = out.astype(bf16)

    @pl.when(h == heads - 1)
    def _():
        for s, piece in enumerate((p0_ref, p1_ref, p2_ref, p3_ref)):
            owner = lax.rem(place_ref[0] + s, shards)
            piece[...] = mixed_ref[:, lanes(owner, local)]


def attend(xt, wt, bias, proj_t, lengths, place):
    shards, depth, local = xt.shape
    heads, feat, head_dim = proj_t.shape
    total = shards * local
    count = lengths.shape[1] - 1
    width = heads * head_dim
    state_rows = count * head_dim + 32
    smem = pl.BlockSpec(memory_space=pltpu.SMEM)

    def whole(*shape):
        return pl.BlockSpec(shape, lambda h: (0,) * len(shape))

    def per_head(*shape):
        return pl.BlockSpec((1,) + shape, lambda h: (h,) + (0,) * len(shape))

    return pl.pallas_call(
        functools.partial(attend_kernel, count),
        grid=(heads,),
        in_specs=[
            smem,
            smem,
            whole(shards, depth, local),
            whole(3 * width, depth),
            whole(3 * width, 8),
            per_head(feat, head_dim),
        ],
        out_specs=[
            whole(3 * width, total),
            per_head(feat, total),
            per_head(feat, total),
            per_head(state_rows, feat),
            pl.BlockSpec((head_dim, total), lambda h: (h, 0)),
            per_head(8, total),
        ]
        + [whole(width, local)] * shards,
        out_shape=[
            jax.ShapeDtypeStruct((3 * width, total), bf16),
            jax.ShapeDtypeStruct((heads, feat, total), bf16),
            jax.ShapeDtypeStruct((heads, feat, total), bf16),
            jax.ShapeDtypeStruct((heads, state_rows, feat), bf16),
            jax.ShapeDtypeStruct((width, total), f32),
            jax.ShapeDtypeStruct((heads, 8, total), f32),
        ]
        + [jax.ShapeDtypeStruct((width, local), bf16)] * shards,
        scratch_shapes=[pltpu.VMEM((width, total), bf16)],
        compiler_params=pltpu.CompilerParams(vmem_limit_bytes=VMEM_LIMIT),
        cost_estimate=cost(8),
        name="attend",
    )(lengths, place, xt, wt, bias, proj_t)


def feature_back_rows(grad_feat, feat, vectors, proj_w):
    scale = HEAD_DIM ** (-0.25)
    grad_proj = grad_feat * feat.astype(f32)
    pulled = scale * dot(proj_w, grad_proj.astype(bf16))
    return pulled - (scale * scale) * vectors.astype(f32) * jnp.sum(grad_proj, axis=0, keepdims=True)


def attend_back_kernel(
    count,
    lengths_ref,
    place_ref,
    qkv_ref,
    qf_ref,
    kf_ref,
    state_ref,
    out_ref,
    den_ref,
    g0_ref,
    g1_ref,
    g2_ref,
    g3_ref,
    proj_ref,
    weight_ref,
    sums_ref,
    grad_ref,
    total_ref,
    small_ref,
    heads_ref,
):
    h = pl.program_id(0)
    shards = total_ref.shape[0]
    width, local = g0_ref.shape
    heads = pl.num_programs(0)
    spread_rows = count * HEAD_DIM

    @pl.when(h == 0)
    def _():
        for s, piece in enumerate((g0_ref, g1_ref, g2_ref, g3_ref)):
            owner = lax.rem(place_ref[0] + s, shards)
            heads_ref[:, lanes(owner, local)] = piece[...]

    def at(kind):
        return pl.ds(pl.multiple_of(kind * width + h * HEAD_DIM, HEAD_DIM), HEAD_DIM)

    seg = segments(lengths_ref, count, (1, shards * local))
    hot = one_hot_rows(seg, count)
    query, key, value = qkv_ref[at(0), :], qkv_ref[at(1), :], qkv_ref[at(2), :]
    q_feat, k_feat = qf_ref[0], kf_ref[0]
    grad_head = heads_ref[pl.ds(pl.multiple_of(h * HEAD_DIM, HEAD_DIM), HEAD_DIM), :].astype(f32)
    den = den_ref[0, 0:1, :]
    grad_numer = (grad_head / den).astype(bf16)
    grad_den = -jnp.sum(grad_head * out_ref[...], axis=0, keepdims=True) / den
    marked = hot * grad_den
    high = marked.astype(bf16).astype(f32)
    low = marked - high
    numer_wide = jnp.concatenate(
        masked_copies(seg, grad_numer, count)
        + [
            jnp.concatenate([high, low], axis=0).astype(bf16),
            jnp.concatenate([high, jnp.zeros_like(high)], axis=0).astype(bf16),
        ],
        axis=0,
    )
    grad_state = dot_cols(numer_wide[: spread_rows + 16], q_feat)
    sums = grad_state[spread_rows : spread_rows + 8] + grad_state[spread_rows + 8 : spread_rows + 16]
    sums_high = sums.astype(bf16).astype(f32)
    grad_state = jnp.concatenate(
        [
            grad_state[:spread_rows].astype(bf16),
            jnp.concatenate([sums_high, sums - sums_high], axis=0).astype(bf16),
        ],
        axis=0,
    )
    value_wide = jnp.concatenate(
        masked_copies(seg, value, count) + [jnp.concatenate([hot, hot], axis=0).astype(bf16)], axis=0
    )
    proj_w = proj_ref[0]
    grad_qfeat = dot_rows(state_ref[0], numer_wide)
    grad_ref[at(0), :] = feature_back_rows(grad_qfeat, q_feat, query, proj_w).astype(bf16)
    grad_kfeat = dot_rows(grad_state, value_wide)
    grad_ref[at(1), :] = feature_back_rows(grad_kfeat, k_feat, key, proj_w).astype(bf16)
    grad_ref[at(2), :] = masked_sum(seg, dot(grad_state[:spread_rows], k_feat), count).astype(bf16)

    @pl.when(h == heads - 1)
    def _():
        for d in range(shards):
            total_ref[d] = dot(weight_ref[...], grad_ref[:, d * local : (d + 1) * local]).astype(bf16)
        rows = sums_ref.shape[0]
        small_ref[:rows] = sums_ref[...]
        small_ref[rows:] = jnp.zeros_like(small_ref[rows:])
        ones = jnp.ones((8, shards * local), bf16)
        totals = dot_cols(ones, grad_ref[...])
        for t in range(shards):

            @pl.when(place_ref[0] == t)
            def _():
                for kind in range(3):
                    small_ref[rows + kind : rows + kind + 1, t * width : (t + 1) * width] = totals[
                        0:1, kind * width : (kind + 1) * width
                    ]


def attend_back(saved, pieces, proj, weight, sums, lengths, place):
    qkv, qf, kf, state, out, den = saved
    heads, feat, total = qf.shape
    width, local = pieces[0].shape
    shards = total // local
    depth = weight.shape[0]
    count = lengths.shape[1] - 1
    state_rows = state.shape[1]
    smem = pl.BlockSpec(memory_space=pltpu.SMEM)

    def whole(*shape):
        return pl.BlockSpec(shape, lambda h: (0,) * len(shape))

    def per_head(*shape):
        return pl.BlockSpec((1,) + shape, lambda h: (h,) + (0,) * len(shape))

    return pl.pallas_call(
        functools.partial(attend_back_kernel, count),
        grid=(heads,),
        in_specs=[
            smem,
            smem,
            whole(3 * width, total),
            per_head(feat, total),
            per_head(feat, total),
            per_head(state_rows, feat),
            pl.BlockSpec((HEAD_DIM, total), lambda h: (h, 0)),
            per_head(8, total),
        ]
        + [whole(width, local)] * shards
        + [per_head(HEAD_DIM, feat), whole(depth, 3 * width), whole(*sums.shape)],
        out_specs=[
            whole(3 * width, total),
            whole(shards, depth, local),
            whole(sums.shape[0] + 8, depth),
        ],
        out_shape=[
            jax.ShapeDtypeStruct((3 * width, total), bf16),
            jax.ShapeDtypeStruct((shards, depth, local), bf16),
            jax.ShapeDtypeStruct((sums.shape[0] + 8, depth), f32),
        ],
        scratch_shapes=[pltpu.VMEM((width, total), bf16)],
        compiler_params=pltpu.CompilerParams(vmem_limit_bytes=VMEM_LIMIT),
        cost_estimate=cost(9),
        name="attend_back",
    )(lengths, place, qkv, qf, kf, state, out, den, *pieces, proj, weight, sums)


def write_blocks(grads, hold_ref, begin=0):
    slots, height, _ = hold_ref.shape
    count = grads.shape[1]
    hold_ref[:, :, begin : begin + count] = grads.astype(bf16).reshape(slots, height, count)


def slot_place(slot, half):
    k = slot // 2
    if half == 0:
        return 1 - k % 2, k // 2
    return 1 - k // 2, k % 2


def emit_blocks(own, hold_ref, even_ref, odd_ref, half):
    for slot in range(hold_ref.shape[0]):
        target = odd_ref if slot % 2 else even_ref
        target[(0,) + slot_place(slot, half) + (0,)] = hold_ref[lax.bitwise_xor(own, slot)]


def emit_half(own, hold_ref, even_ref, odd_ref, second):
    for half in range(2):

        @pl.when(second == half)
        def _():
            emit_blocks(own, hold_ref, even_ref, odd_ref, half)


def output_grad_kernel(own_ref, grad_ffn_ref, act_ref, even_ref, odd_ref, hold_ref):
    write_blocks(dot_rows(grad_ffn_ref[...], act_ref[0]), hold_ref)
    emit_half(own_ref[0], hold_ref, even_ref, odd_ref, pl.program_id(0) // 2)


def block_outputs(slots, shards, height, count):
    spec = pl.BlockSpec((1, 2, 2, 1, height, count), lambda s: (s // 2, 0, 0, s % 2, 0, 0))
    shape = jax.ShapeDtypeStruct((2, 2, slots // 4, shards // 2, height, count), bf16)
    return [spec, spec], [shape, shape]


def output_grad(own, slots, grad_ffn, acts):
    shards, rows, hidden = acts.shape
    depth = grad_ffn.shape[1]
    specs, shapes = block_outputs(slots, shards, depth // slots, hidden)
    return pl.pallas_call(
        output_grad_kernel,
        grid=(shards,),
        in_specs=[
            pl.BlockSpec(memory_space=pltpu.SMEM),
            pl.BlockSpec((rows, depth), lambda s: (0, 0)),
            pl.BlockSpec((1, rows, hidden), lambda s: (s, 0, 0)),
        ],
        out_specs=specs,
        out_shape=shapes,
        scratch_shapes=[pltpu.VMEM((slots, depth // slots, hidden), bf16)],
        compiler_params=pltpu.CompilerParams(vmem_limit_bytes=VMEM_LIMIT),
        cost_estimate=cost(4),
        name="output_grad",
    )(own, grad_ffn, acts)


def hidden_grad_kernel(
    own_ref, first_ref, grad_pre_ref, grad_branch_ref, p0_ref, p1_ref, p2_ref, p3_ref, even_ref, odd_ref, hold_ref
):
    s = pl.program_id(0)
    hidden = grad_pre_ref.shape[2]
    write_blocks(dot_rows(first_ref[...], grad_pre_ref[0]), hold_ref)
    for index, piece in enumerate((p0_ref, p1_ref, p2_ref, p3_ref)):

        @pl.when(s == index)
        def _():
            grads = lax.dot_general(
                grad_branch_ref[...], piece[...], (((0,), (1,)), ((), ())), preferred_element_type=f32
            )
            write_blocks(grads, hold_ref, hidden)

    emit_half(own_ref[0], hold_ref, even_ref, odd_ref, s // 2)


def hidden_grad(own, slots, first_low, grad_pre, grad_branch, pieces):
    shards, rows, hidden = grad_pre.shape
    depth = first_low.shape[1]
    width = pieces[0].shape[0]
    specs, shapes = block_outputs(slots, shards, depth // slots, hidden + width)
    return pl.pallas_call(
        hidden_grad_kernel,
        grid=(shards,),
        in_specs=[
            pl.BlockSpec(memory_space=pltpu.SMEM),
            pl.BlockSpec((rows, depth), lambda s: (0, 0)),
            pl.BlockSpec((1, rows, hidden), lambda s: (s, 0, 0)),
            pl.BlockSpec((rows, depth), lambda s: (0, 0)),
        ]
        + [pl.BlockSpec((width, rows), lambda s: (0, 0))] * shards,
        out_specs=specs,
        out_shape=shapes,
        scratch_shapes=[pltpu.VMEM((slots, depth // slots, hidden + width), bf16)],
        compiler_params=pltpu.CompilerParams(vmem_limit_bytes=VMEM_LIMIT),
        cost_estimate=cost(5),
        name="hidden_grad",
    )(own, first_low, grad_pre, grad_branch, *pieces)


def qkv_grad_kernel(own_ref, xt_ref, grad_ref, even_ref, odd_ref, hold_ref):
    shards, _, local = xt_ref.shape
    grads = sum(
        dot_cols(xt_ref[d], grad_ref[:, d * local : (d + 1) * local]) for d in range(shards)
    )
    write_blocks(grads, hold_ref)
    rows = even_ref.shape[4]
    for slot in range(hold_ref.shape[0]):
        target = odd_ref if slot % 2 else even_ref
        block = hold_ref[lax.bitwise_xor(own_ref[0], slot)]
        for half in range(2):
            target[(half,) + slot_place(slot, half) + (0,)] = block[half * rows : (half + 1) * rows]


def qkv_grad(own, slots, xt, grads):
    shards, depth, local = xt.shape
    count = grads.shape[0]
    vmem = pl.BlockSpec(memory_space=pltpu.VMEM)
    shape = jax.ShapeDtypeStruct((2, 2, slots // 4, 1, depth // slots // 2, count), bf16)
    return pl.pallas_call(
        qkv_grad_kernel,
        in_specs=[pl.BlockSpec(memory_space=pltpu.SMEM), vmem, vmem],
        out_specs=[vmem, vmem],
        out_shape=[shape, shape],
        scratch_shapes=[pltpu.VMEM((slots, depth // slots, count), bf16)],
        compiler_params=pltpu.CompilerParams(vmem_limit_bytes=VMEM_LIMIT),
        cost_estimate=cost(2),
        name="qkv_grad",
    )(own, xt, grads)


def norm_rows(resid):
    center = resid - jnp.mean(resid, axis=-1, keepdims=True)
    inverse = lax.rsqrt(jnp.mean(center * center, axis=-1, keepdims=True) + eps)
    return center * inverse, inverse


HELD = [((0, 2), 0), ((4, 6), 0), ((0, 4), 2), ((2, 6), 2)]
HELD = HELD + [((low ^ 1, high ^ 1), shard) for (low, high), shard in HELD]


def place_copies(own, held, begin, rows, target, sems):
    columns = held[0].shape[2]
    copies = [[] for _ in range(target.shape[0])]
    for piece, (masks, shard) in zip(held, HELD):
        for index in range(4):
            mask, s = masks[index // 2], shard + index % 2
            source = lax.bitwise_xor(own, mask)
            chip = lax.shift_right_logical(source, 1)
            core = lax.bitwise_and(source, 1)
            copies[s].append(
                pltpu.make_async_copy(
                    piece.at[index, pl.ds(begin, rows), :],
                    target.at[s, chip, :, lanes(core, columns)],
                    sems.at[s, mask],
                )
            )
    return copies


def start_all(copies):
    for entries in copies:
        for copy in entries:
            copy.start()


def wait_all(entries):
    for copy in entries:
        copy.wait()


def ffn_up_kernel(
    own_ref,
    tokens_ref,
    p0_ref,
    p1_ref,
    p2_ref,
    p3_ref,
    mixer_bias_ref,
    gain_ref,
    shift_ref,
    hidden_bias_ref,
    *refs,
):
    held = refs[:PLANE]
    normed_ref, inverse_ref, first_ref, act_ref, slope_ref, mixer_ref, hidden_ref, mixer_sem, hidden_sem = refs[PLANE:]
    own = own_ref[0]
    shards, chips, mixer_rows, depth = mixer_ref.shape
    hidden_rows = hidden_ref.shape[2]
    mixer_copies = place_copies(own, held, hidden_rows, mixer_rows, mixer_ref, mixer_sem)
    hidden_copies = place_copies(own, held, 0, hidden_rows, hidden_ref, hidden_sem)
    start_all(mixer_copies)
    start_all(hidden_copies)
    resid = tokens_ref[...].astype(f32) + mixer_bias_ref[...]
    for s, piece in enumerate((p0_ref, p1_ref, p2_ref, p3_ref)):
        wait_all(mixer_copies[s])
        resid = resid + dot_rows(piece[...], mixer_ref[s].reshape(chips * mixer_rows, depth))
    normed, inverse = norm_rows(resid)
    normed_ref[...] = normed
    inverse_ref[...] = jnp.broadcast_to(inverse, inverse_ref.shape)
    first_low = (normed * gain_ref[...] + shift_ref[...]).astype(bf16)
    first_ref[...] = first_low
    for s in range(shards):
        wait_all(hidden_copies[s])
        bias = unpack_bias(hidden_bias_ref[s])
        pre = dot(first_low, hidden_ref[s].reshape(chips * hidden_rows, hidden_ref.shape[3])) + bias
        phi = 0.5 * (1.0 + lax.erf(pre * math.sqrt(0.5)))
        act_ref[s] = (pre * phi).astype(bf16)
        slope_ref[s] = (
            phi + pre * jnp.exp(-0.5 * pre * pre) * (1.0 / math.sqrt(2.0 * math.pi))
        ).astype(bf16)


def ffn_up(own, tokens, pieces, mixer_bias, gain, shift_by, hidden_bias, held, mixer_rows):
    rows, depth = tokens.shape
    shards = len(pieces)
    chips = PLANE // 2
    hidden = 2 * hidden_bias.shape[-1]
    hidden_rows = held[0].shape[1] - mixer_rows
    vmem = pl.BlockSpec(memory_space=pltpu.VMEM)
    return pl.pallas_call(
        ffn_up_kernel,
        in_specs=[pl.BlockSpec(memory_space=pltpu.SMEM)]
        + [vmem] * (1 + shards + 4)
        + [pl.BlockSpec(memory_space=pltpu.HBM)] * PLANE,
        out_specs=[vmem] * 5,
        out_shape=[
            jax.ShapeDtypeStruct((rows, depth), f32),
            jax.ShapeDtypeStruct((rows, 128), f32),
            jax.ShapeDtypeStruct((rows, depth), bf16),
            jax.ShapeDtypeStruct((shards, rows, hidden), bf16),
            jax.ShapeDtypeStruct((shards, rows, hidden), bf16),
        ],
        scratch_shapes=[
            pltpu.VMEM((shards, chips, mixer_rows, depth), bf16),
            pltpu.VMEM((shards, chips, hidden_rows, hidden), bf16),
            pltpu.SemaphoreType.DMA((shards, PLANE)),
            pltpu.SemaphoreType.DMA((shards, PLANE)),
        ],
        compiler_params=pltpu.CompilerParams(vmem_limit_bytes=VMEM_LIMIT),
        cost_estimate=cost(8),
        name="ffn_up",
    )(own, tokens, *pieces, mixer_bias, gain, shift_by, hidden_bias, *held)


def norm_rows_back(scaled, normed, inverse):
    return inverse * (
        scaled
        - jnp.mean(scaled, axis=-1, keepdims=True)
        - normed * jnp.mean(scaled * normed, axis=-1, keepdims=True)
    )


def column_sum(entries):
    return jnp.sum(entries, axis=0, keepdims=True)


def ffn_down_kernel(
    own_ref,
    normed_ref,
    inverse_ref,
    act_ref,
    slope_ref,
    cotangent_ref,
    first_gain_ref,
    first_shift_ref,
    output_bias_ref,
    gain_ref,
    shift_ref,
    *refs,
):
    held, refs = refs[:PLANE], refs[PLANE:]
    held_out, refs = refs[:PLANE], refs[PLANE:]
    (
        layer_ref,
        resid_ref,
        b0_ref,
        b1_ref,
        b2_ref,
        b3_ref,
        grad_ffn_ref,
        grad_pre_ref,
        grad_branch_ref,
        sums_ref,
        mixer_ref,
        hidden_ref,
        output_ref,
        mixer_sem,
        hidden_sem,
        output_sem,
    ) = refs
    own, place = own_ref[0], own_ref[1]
    shards, chips, mixer_rows, depth = mixer_ref.shape
    hidden_rows = hidden_ref.shape[2]
    hidden = hidden_ref.shape[3]
    output_copies = place_copies(own, held_out, 0, output_ref.shape[2], output_ref, output_sem)
    hidden_copies = place_copies(own, held, 0, hidden_rows, hidden_ref, hidden_sem)
    mixer_copies = place_copies(own, held, hidden_rows, mixer_rows, mixer_ref, mixer_sem)
    start_all(output_copies)
    start_all(hidden_copies)
    start_all(mixer_copies)
    normed_one = normed_ref[...]
    resid = normed_one * first_gain_ref[...] + first_shift_ref[...] + output_bias_ref[...]
    for s in range(shards):
        wait_all(output_copies[s])
        resid = resid + dot(act_ref[s], output_ref[s].reshape(hidden, depth))
    normed, inverse = norm_rows(resid)
    layer_ref[...] = (normed * gain_ref[...] + shift_ref[...]).astype(bf16)
    grad_out = cotangent_ref[...].astype(f32)
    sums_ref[0:1] = column_sum(grad_out * normed)
    sums_ref[1:2] = column_sum(grad_out)
    grad_two = norm_rows_back(grad_out * gain_ref[...], normed, inverse)
    grad_ffn = grad_two.astype(bf16)
    grad_ffn_ref[...] = grad_ffn
    sums_ref[2:3] = column_sum(grad_ffn.astype(f32))
    grad_first = grad_two
    for s in range(shards):
        grad_pre = (
            dot_cols(grad_ffn, output_ref[s].reshape(hidden, depth)) * slope_ref[s].astype(f32)
        ).astype(bf16)
        grad_pre_ref[s] = grad_pre
        sums_ref[pl.ds(8 + lax.rem(place - s + shards, shards), 1)] = column_sum(grad_pre.astype(f32))
        wait_all(hidden_copies[s])
        grad_first = grad_first + dot_cols(grad_pre, hidden_ref[s].reshape(depth, hidden))
    sums_ref[3:4] = column_sum(grad_first * normed_one)
    sums_ref[4:5] = column_sum(grad_first)
    grad_one = norm_rows_back(grad_first * first_gain_ref[...], normed_one, inverse_ref[:, 0:1])
    resid_ref[...] = grad_one
    grad_branch = grad_one.astype(bf16)
    grad_branch_ref[...] = grad_branch
    sums_ref[5:6] = column_sum(grad_branch.astype(f32))
    sums_ref[6:8] = jnp.zeros((2, depth), f32)
    sums_ref[8 + shards :] = jnp.zeros((8 - shards, depth), f32)
    for s, back in enumerate((b0_ref, b1_ref, b2_ref, b3_ref)):
        wait_all(mixer_copies[s])
        back[...] = dot_cols(mixer_ref[s].reshape(chips * mixer_rows, depth), grad_branch).astype(bf16)


def ffn_down(own, normed, inverse, acts, slopes, cotangent, vectors, held, held_out, mixer_rows):
    rows, depth = normed.shape
    shards, _, hidden = acts.shape
    chips = PLANE // 2
    hidden_rows = held[0].shape[1] - mixer_rows
    output_rows = held_out[0].shape[1]
    vmem = pl.BlockSpec(memory_space=pltpu.VMEM)
    width = chips * mixer_rows
    return pl.pallas_call(
        ffn_down_kernel,
        in_specs=[pl.BlockSpec(memory_space=pltpu.SMEM)]
        + [vmem] * 10
        + [pl.BlockSpec(memory_space=pltpu.HBM)] * (2 * PLANE),
        out_specs=[vmem] * (6 + shards),
        out_shape=[
            jax.ShapeDtypeStruct((rows, depth), bf16),
            jax.ShapeDtypeStruct((rows, depth), f32),
        ]
        + [jax.ShapeDtypeStruct((width, rows), bf16)] * shards
        + [
            jax.ShapeDtypeStruct((rows, depth), bf16),
            jax.ShapeDtypeStruct((shards, rows, hidden), bf16),
            jax.ShapeDtypeStruct((rows, depth), bf16),
            jax.ShapeDtypeStruct((16, depth), f32),
        ],
        scratch_shapes=[
            pltpu.VMEM((shards, chips, mixer_rows, depth), bf16),
            pltpu.VMEM((shards, chips, hidden_rows, hidden), bf16),
            pltpu.VMEM((shards, chips, output_rows, depth), bf16),
            pltpu.SemaphoreType.DMA((shards, PLANE)),
            pltpu.SemaphoreType.DMA((shards, PLANE)),
            pltpu.SemaphoreType.DMA((shards, PLANE)),
        ],
        compiler_params=pltpu.CompilerParams(vmem_limit_bytes=VMEM_LIMIT),
        cost_estimate=cost(15),
        name="ffn_down",
    )(own, normed, inverse, acts, slopes, cotangent, *vectors, *held, *held_out)


def swap(values, mask):
    size = lax.axis_size("dp")
    return lax.ppermute(values, "dp", [(i, i ^ mask) for i in range(size)])


def shift(values, step):
    size = lax.axis_size("tensor")
    return lax.ppermute(values, "tensor", [(i, (i + step) % size) for i in range(size)])


def after(values, *others):
    return lax.optimization_barrier((values, others))[0]


def spread_shards(payload):
    return [payload] + [shift(payload, s) for s in range(1, lax.axis_size("tensor"))]


def spread_plane(parts, before=(), between=()):
    low, high = after((jnp.stack(parts[:2]), jnp.stack(parts[2:])), *before)
    low_far, high_far = after((swap(low, 2), swap(high, 4)), *between)
    low = jnp.concatenate([low, low_far])
    high = jnp.concatenate([high, high_far])
    return low, swap(low, 4), high, swap(high, 2)


def both_cores(held):
    return list(held) + [swap(entry, 1) for entry in held]


def add_low(*entries):
    return sum(entry.astype(f32) for entry in entries).astype(bf16)


def sum_cores(even, odd):
    far = swap(odd, 1)
    return [[add_low(even[half, part], far[half, part]) for part in range(2)] for half in range(2)]


def sum_first(near, *before):
    (send_low, keep_low), (send_high, keep_high) = near
    send_low, send_high = after((send_low, send_high), *before)
    low, high = swap(send_low, 2), swap(send_high, 4)
    return (
        [add_low(keep_low[0], low[0]), add_low(keep_high[0], high[0])],
        [add_low(keep_low[1], low[1]), add_low(keep_high[1], high[1])],
    )


def sum_second(stay, send):
    low, high = swap(send[0], 4), swap(send[1], 2)
    return [add_low(stay[0], low), add_low(stay[1], high)]


def scatter_all(even, odd):
    order = [[(half, slot) for slot in range(PLANE)] for half in range(2)]
    halves = []
    for half in range(2):
        blocks = [
            (odd if slot % 2 else even)[(half,) + slot_place(slot, half)] for half, slot in order[half]
        ]
        halves.append(jnp.stack(blocks, axis=1))
    return halves


def scatter_shards(grads):
    total = grads[0].astype(f32)
    for s in range(1, len(grads)):
        total = total + shift(grads[s], -s).astype(f32)
    return total


def small_sum(values):
    size = lax.axis_size("dp")
    if size != PLANE:
        return lax.psum(values, ("dp", "tensor"))
    values = values + swap(values, 1)
    values = values + swap(values, 2) + swap(values, 4) + swap(values, 6)
    total = values
    for s in range(1, lax.axis_size("tensor")):
        total = total + shift(values, s)
    return total


def body(
    tokens,
    lengths,
    query_weight,
    query_bias,
    key_weight,
    key_bias,
    value_weight,
    value_bias,
    feature_proj,
    mixer_weight,
    mixer_bias,
    first_gain,
    first_shift,
    hidden_weight,
    hidden_bias,
    output_weight,
    output_bias,
    second_gain,
    second_shift,
    cotangent,
):
    depth = tokens.shape[1]
    shards = lax.axis_size("tensor")
    place = lax.axis_index("tensor").astype(jnp.int32)
    plane = (lax.axis_index("dp") % PLANE).astype(jnp.int32)
    width = query_weight.shape[1]
    hidden = hidden_weight.shape[1]
    mixer_rows = mixer_weight.shape[0] // (PLANE // 2)
    own = jnp.stack([plane, place])
    slot_of = plane[None] if lax.axis_size("dp") == PLANE else jnp.zeros((1,), jnp.int32)

    def row(vector):
        return vector.reshape(1, -1)

    own_xt, payload, payload_out = pack(
        own, tokens, row(hidden_bias), hidden_weight, mixer_weight, output_weight
    )
    parts = spread_shards(payload)
    weights = after((query_weight, key_weight, value_weight), payload)
    qkv_weight, qkv_turned, qkv_bias, proj_t = prepare(
        weights, [row(query_bias), row(key_bias), row(value_bias)], feature_proj
    )
    xt = lax.all_gather(after(own_xt, qkv_bias), "tensor", axis=0, tiled=False)
    rows = payload.shape[0] - 16
    around = spread_plane([part[:rows] for part in parts])
    all_bias = jnp.stack([part[rows:] for part in parts])
    parts_out = spread_shards(after(payload_out, *parts))
    held = both_cores(around)
    *saved, p0, p1, p2, p3 = attend(
        after(xt, *around), qkv_turned, qkv_bias, proj_t, lengths, place[None]
    )
    around_out = spread_plane(parts_out, around, (p0,))
    held_out = both_cores(around_out)
    pieces = [p0] + [shift(p, s) for s, p in ((1, p1), (2, p2), (3, p3))]
    normed, inverse, first_low, acts, slopes = ffn_up(
        own, tokens, pieces, row(mixer_bias), row(first_gain), row(first_shift), all_bias, held, mixer_rows
    )
    vectors = [row(v) for v in (first_gain, first_shift, output_bias, second_gain, second_shift)]
    layer_out, grad_resid, b0, b1, b2, b3, grad_ffn, grad_pre, grad_branch, sums = ffn_down(
        own, normed, inverse, acts, slopes, cotangent, vectors, held, held_out, mixer_rows
    )
    back = [b0] + [shift(b, -s) for s, b in ((1, b1), (2, b2), (3, b3))]
    output_blocks = output_grad(slot_of, PLANE, grad_ffn, acts)
    hidden_blocks = hidden_grad(slot_of, PLANE, first_low, grad_pre, grad_branch, pieces)
    fast = lax.axis_size("dp") == PLANE
    if fast:
        near_output = sum_cores(*output_blocks)
        stay_output, send_output = sum_first(near_output)
        back = after(back, near_output)
    grad_qkv, total, small = attend_back(
        saved, back, feature_proj, qkv_weight, sums, lengths, place[None]
    )
    through = lax.psum_scatter(total, "tensor", scatter_dimension=0, tiled=True)
    tokens_grad = grad_resid + through[0].T.astype(f32)
    if fast:
        near_hidden = sum_cores(*hidden_blocks)
        grad_qkv = after(grad_qkv, send_output, near_hidden)
    qkv_blocks = qkv_grad(slot_of, PLANE, xt, grad_qkv)
    if fast:
        near_qkv = sum_cores(*qkv_blocks)
        grad_output = sum_second(stay_output, send_output)
        stay_hidden, send_hidden = sum_first(near_hidden, send_output)
        grad_hidden = sum_second(stay_hidden, send_hidden)
        stay_qkv, send_qkv = sum_first(near_qkv, send_hidden)
        grad_weight = jnp.concatenate([half[0] for half in sum_second(stay_qkv, send_qkv)])
    else:

        def scatter(halves, axis, dim):
            blocks = jnp.concatenate(halves, axis=axis)
            blocks = blocks.reshape(blocks.shape[:1] + (-1,) + blocks.shape[-1:])
            return lax.psum_scatter(blocks, "dp", scatter_dimension=1, tiled=True)

        grad_output = [scatter(scatter_all(*output_blocks), 0, 0)]
        grad_hidden = [scatter(scatter_all(*hidden_blocks), 0, 0)]
        grad_weight = scatter(scatter_all(*qkv_blocks), 2, 0)[0]
    grad_weight = grad_weight.astype(f32)
    small = small_sum(small)
    grad_output = scatter_shards([entry[s] for entry in grad_output for s in range(entry.shape[0])]).T
    grad_hidden = scatter_shards([entry[s] for entry in grad_hidden for s in range(entry.shape[0])])
    return (
        layer_out,
        tokens_grad,
        grad_weight[:, :width],
        small[16],
        grad_weight[:, width : 2 * width],
        small[17],
        grad_weight[:, 2 * width :],
        small[18],
        grad_hidden[:, hidden:].T,
        small[5],
        small[3],
        small[4],
        grad_hidden[:, :hidden],
        small[8 : 8 + shards].reshape(-1),
        grad_output,
        small[2],
        small[0],
        small[1],
    )


def solution(mesh):
    placed = (
        P(("dp", "tensor"), None),
        P("dp", None),
        P(None, "tensor"),
        P("tensor"),
        P(None, "tensor"),
        P("tensor"),
        P(None, "tensor"),
        P("tensor"),
        P("tensor", None, None),
        P("tensor", None),
        P(),
        P(),
        P(),
        P(None, "tensor"),
        P("tensor"),
        P("tensor", None),
        P(),
        P(),
        P(),
        P(("dp", "tensor"), None),
    )
    return jax.shard_map(
        body,
        mesh=mesh,
        in_specs=placed,
        out_specs=(
            P(("dp", "tensor"), None),
            P(("dp", "tensor"), None),
            P("dp", "tensor"),
            P(),
            P("dp", "tensor"),
            P(),
            P("dp", "tensor"),
            P(),
            P("tensor", "dp"),
            P(),
            P(),
            P(),
            P("dp", "tensor"),
            P(),
            P("tensor", "dp"),
            P(),
            P(),
            P(),
        ),
        check_vma=False,
    )
```

profile of v0, /device:TPU:0, one launch (start us, length us, event | category | flops | bytes accessed | tf_op | source)
XLA Modules:
  0.0 286.7 jit_solution(4619793858955581594)
XLA Ops:
  12.0 5.1 %collective-permute-start.2 = (bf16[256,384]{1,0:T(8,128)(2,1)}, bf16[256,384]{1,0:T(8,128)(2,1)S(1)}, u32[]{:S(2)}, u32[]{:S(2)}) collective-permute-start(bf16[256,384]{1,0:T(8,128)(2,1)} %get-tuple-element.85), channel_id=1, source_target_pairs={{0,3},{1,0},{2,1},{3,2},{4,7},{5,4},{6,5},{7,6},{8,11},{9,8},{10,9... | collective-permute-start | bytes 589832 | tf_op jit(solution)/shard_map/ppermute | solution.py:830
  23.9 10.1 %collective-permute-done.1 = bf16[256,384]{1,0:T(8,128)(2,1)S(1)} collective-permute-done((bf16[256,384]{1,0:T(8,128)(2,1)}, bf16[256,384]{1,0:T(8,128)(2,1)S(1)}, u32[]{:S(2)}, u32[]{:S(2)}) %collective-permute-start.1) | collective-permute-done | bytes 196640 | tf_op jit(solution)/shard_map/ppermute | solution.py:830
  37.4 6.6 %collective-permute-done.3 = bf16[2,240,384]{2,1,0:T(8,128)(2,1)S(1)} collective-permute-done((bf16[2,240,384]{2,1,0:T(8,128)(2,1)S(1)}, bf16[2,240,384]{2,1,0:T(8,128)(2,1)S(1)}, u32[]{:S(2)}, u32[]{:S(2)}) %collective-permute-start.3) | collective-permute-done | bytes 368672 | tf_op jit(solution)/shard_map/ppermute | solution.py:825
  47.5 5.2 %collective-permute-start.15 = (bf16[192,384]{1,0:T(8,128)(2,1)S(1)}, bf16[192,384]{1,0:T(8,128)(2,1)S(1)}, u32[]{:S(2)}, u32[]{:S(2)}) collective-permute-start(bf16[192,384]{1,0:T(8,128)(2,1)S(1)} %copy-done.10), channel_id=1, source_target_pairs={{0,2},{1,3},{2,0},{3,1},{4,6},{5,7},{6,4},{7,5},{8,10},{9,11},{10,... | collective-permute-start | bytes 442376 | tf_op jit(solution)/shard_map/ppermute | solution.py:830
  61.0 12.8 %collective-permute-done.15 = bf16[192,384]{1,0:T(8,128)(2,1)S(1)} collective-permute-done((bf16[192,384]{1,0:T(8,128)(2,1)S(1)}, bf16[192,384]{1,0:T(8,128)(2,1)S(1)}, u32[]{:S(2)}, u32[]{:S(2)}) %collective-permute-start.15) | collective-permute-done | bytes 147488 | tf_op jit(solution)/shard_map/ppermute | solution.py:830
  78.9 9.1 %attend.1 = (bf16[576,1024]{1,0:T(8,128)(2,1)}, bf16[3,256,1024]{2,1,0:T(8,128)(2,1)}, bf16[3,256,1024]{2,1,0:T(8,128)(2,1)}, bf16[3,416,256]{2,1,0:T(8,128)(2,1...) custom-call(s32[1,7]{1,0:T(1,128)} %lengths_ref.3, ...), custom_call_target="tpu_custom_call" | custom-call | flops 7200000000 | tf_op jit(solution)/shard_map/attend/pallas_call | solution.py:259
  92.3 3.1 %collective-permute-start.9 = (bf16[192,256]{1,0:T(8,128)(2,1)}, bf16[192,256]{1,0:T(8,128)(2,1)S(1)}, u32[]{:S(2)}, u32[]{:S(2)}) collective-permute-start(bf16[192,256]{1,0:T(8,128)(2,1)} %get-tuple-element.101), channel_id=1, source_target_pairs={{0,3},{1,0},{2,1},{3,2},{4,7},{5,4},{6,5},{7,6},{8,11},{9,8},{10,9... | collective-permute-start | bytes 294920 | tf_op jit(solution)/shard_map/ppermute | solution.py:830
  96.0 3.0 %collective-permute-done.7.p1_ref = bf16[192,256]{1,0:T(8,128)(2,1)S(1)} collective-permute-done((bf16[192,256]{1,0:T(8,128)(2,1)}, bf16[192,256]{1,0:T(8,128)(2,1)S(1)}, u32[]{:S(2)}, u32[]{:S(2)}) %collective-permute-start.7) | collective-permute-done | bytes 98336 | tf_op jit(solution)/shard_map/ppermute | solution.py:830
  106.6 9.3 %ffn_up.1 = (f32[256,768]{1,0:T(8,128)}, f32[256,128]{1,0:T(8,128)}, bf16[256,768]{1,0:T(8,128)(2,1)}, bf16[4,256,768]{2,1,0:T(8,128)(2,1)}, bf16[4,256,768]{2,1,0:T(8,128)(2,1)}) custom-call(s32[2]{0:T(128)} %pad_add_fusion.own_ref, bf16[256,768]{1,0:T(8,128)(2,1)} %tokens_ref.3, bf16[192,256]{1,0:T(8,128)(2,1)} %get-tuple-element.98.p0_ref, ...), custom_call_target="tpu_custom_call" | custom-call | flops 7200000000 | tf_op jit(solution)/shard_map/ffn_up/pallas_call | solution.py:666
  117.4 15.6 %ffn_down.1 = (bf16[256,768]{1,0:T(8,128)(2,1)}, f32[256,768]{1,0:T(8,128)}, bf16[192,256]{1,0:T(8,128)(2,1)}, bf16[192,256]{1,0:T(8,128)(2,1)}, bf16[192,256]{1...) custom-call(s32[2]{0:T(128)} %pad_add_fusion.own_ref, ...), custom_call_target="tpu_custom_call" | custom-call | flops 13500000256 | tf_op jit(solution)/shard_map/ffn_down/pallas_call | solution.py:792
  133.0 5.7 %output_grad.1 = (bf16[2,2,2,2,96,768]{5,4,3,2,1,0:T(8,128)(2,1)}, bf16[2,2,2,2,96,768]{5,4,3,2,1,0:T(8,128)(2,1)}) custom-call(s32[1]{0:T(128)} %bitcast.own_ref, bf16[256,768]{1,0:T(8,128)(2,1)} %get-tuple-element.124.grad_ffn_ref, bf16[4,256,768]{2,1,0:T(8,128)(2,1)} %get-tuple-element.104.act_ref), custom_call_target="tpu_custom_call" | custom-call | flops 3600000000 | tf_op jit(solution)/shard_map/output_grad/pallas_call | solution.py:487
  139.1 7.1 %hidden_grad.1 = (bf16[2,2,2,2,96,960]{5,4,3,2,1,0:T(8,128)(2,1)}, bf16[2,2,2,2,96,960]{5,4,3,2,1,0:T(8,128)(2,1)}) custom-call(s32[1]{0:T(128)} %bitcast.own_ref, bf16[256,768]{1,0:T(8,128)(2,1)} %get-tuple-element.137.first_ref, bf16[4,256,768]{2,1,0:T(8,128)(2,1)} %get-tuple-element.138.grad_pre_ref, bf16[256,768]{1,0:T(8,128)(2,1)} %get-tuple-element.139.grad_branch_ref, ...), custom_call_target="tpu_custom_call" | custom-call | flops 4499999744 | tf_op jit(solution)/shard_map/hidden_grad/pallas_call | solution.py:527
  149.3 3.3 %add_convert_fusion.4 = (bf16[1,1,2,2,96,768]{5,4,3,2,1,0:T(8,128)(2,1)S(1)}, bf16[1,1,2,2,96,768]{5,4,3,2,1,0:T(8,128)(2,1)S(1)}, bf16[2,2,96,768]{3,2,1,0:T(8,128)(2,1)}, bf16[2,2,96,768]{3,2,1,0:T(8,128)(2,1)}) fusion(bf16[2,2,2,2,96,768]{5,4,3,2,1,0:T(8,128)(2,1)} %collective-permute-done.28, bf16[2,2,2,2,96,768]{5,4,3,2,1,0:T(8,128)(2,1)S(1)} %copy-done), kind=kLoop, calls=%fused_computation.4 | loop fusion | flops 4718592 | bytes 7077888 | tf_op jit(solution)/shard_map/convert_element_type | solution.py:854
  152.7 4.2 %collective-permute-done.26.g2_ref = bf16[192,256]{1,0:T(8,128)(2,1)S(1)} collective-permute-done((bf16[192,256]{1,0:T(8,128)(2,1)S(1)}, bf16[192,256]{1,0:T(8,128)(2,1)S(1)}, u32[]{:S(2)}, u32[]{:S(2)}) %collective-permute-start.26) | collective-permute-done | bytes 98336 | tf_op jit(solution)/shard_map/ppermute | solution.py:830
  158.5 10.6 %attend_back.1 = (bf16[576,1024]{1,0:T(8,128)(2,1)}, bf16[4,768,256]{2,1,0:T(8,128)(2,1)}, f32[24,768]{1,0:T(8,128)}) custom-call(s32[1,7]{1,0:T(1,128)} %lengths_ref.3, s32[1]{0:T(128)} %bitcast.1.place_ref, bf16[576,1024]{1,0:T(8,128)(2,1)} %get-tuple-element.114.qkv_ref, bf16[3,256,1024]{2,1,0:T(8,128)(2,1)} %get-tuple-element.115.qf_ref, ...), custom_call_target="tpu_custom_call" | custom-call | flops 8099999744 | tf_op jit(solution)/shard_map/attend_back/pallas_call | solution.py:413
  177.9 12.7 %collective-permute-done.41 = f32[24,768]{1,0:T(8,128)} collective-permute-done((f32[24,768]{1,0:T(8,128)S(1)}, f32[24,768]{1,0:T(8,128)}, u32[]{:S(2)}, u32[]{:S(2)}) %collective-permute-start.41) | collective-permute-done | bytes 73760 | tf_op jit(solution)/shard_map/ppermute | solution.py:825
  200.2 5.6 %add_convert_fusion = (bf16[1,1,2,2,96,960]{5,4,3,2,1,0:T(8,128)(2,1)S(1)}, bf16[1,1,2,2,96,960]{5,4,3,2,1,0:T(8,128)(2,1)S(1)}, bf16[2,2,96,960]{3,2,1,0:T(8,128)(2,1)}, bf16[2,2,96,960]{3,2,1,0:T(8,128)(2,1)}) fusion(bf16[2,2,2,2,96,960]{5,4,3,2,1,0:T(8,128)(2,1)} %collective-permute-done.31, bf16[2,2,2,2,96,960]{5,4,3,2,1,0:T(8,128)(2,1)} %get-tuple-element.140), kind=kLoop, calls=%fused_computation | loop fusion | flops 5898240 | bytes 8847360 | tf_op jit(solution)/shard_map/convert_element_type | solution.py:854
  205.8 4.1 %qkv_grad.1 = (bf16[2,2,2,1,48,576]{5,4,3,2,1,0:T(8,128)(2,1)}, bf16[2,2,2,1,48,576]{5,4,3,2,1,0:T(8,128)(2,1)}) custom-call(s32[1]{0:T(128)} %bitcast.own_ref, bf16[4,768,256]{2,1,0:T(8,128)(2,1)} %bitcast.189, bf16[576,1024]{1,0:T(8,128)(2,1)} %get-tuple-element.142.grad_ref), custom_call_target="tpu_custom_call" | custom-call | flops 1800000000 | tf_op jit(solution)/shard_map/qkv_grad/pallas_call | solution.py:565
  221.5 8.2 %collective-permute-done.54 = bf16[96,768]{1,0:T(8,128)(2,1)S(1)} collective-permute-done((bf16[96,768]{1,0:T(8,128)(2,1)}, bf16[96,768]{1,0:T(8,128)(2,1)S(1)}, u32[]{:S(2)}, u32[]{:S(2)}) %collective-permute-start.54) | collective-permute-done | bytes 147488 | tf_op jit(solution)/shard_map/ppermute | solution.py:830
  233.2 6.4 %collective-permute-done.34 = bf16[2,2,96,960]{3,2,1,0:T(8,128)(2,1)S(1)} collective-permute-done((bf16[2,2,96,960]{3,2,1,0:T(8,128)(2,1)}, bf16[2,2,96,960]{3,2,1,0:T(8,128)(2,1)S(1)}, u32[]{:S(2)}, u32[]{:S(2)}) %collective-permute-start.34) | collective-permute-done | bytes 737312 | tf_op jit(solution)/shard_map/ppermute | solution.py:825
  247.0 7.0 %collective-permute-done.37 = bf16[2,1,48,576]{3,2,1,0:T(8,128)(2,1)S(1)} collective-permute-done((bf16[2,1,48,576]{3,2,1,0:T(8,128)(2,1)S(1)}, bf16[2,1,48,576]{3,2,1,0:T(8,128)(2,1)S(1)}, u32[]{:S(2)}, u32[]{:S(2)}) %collective-permute-start.37) | collective-permute-done | bytes 110624 | tf_op jit(solution)/shard_map/ppermute | solution.py:825
  259.5 3.1 %collective-permute-start.47 = (bf16[96,960]{1,0:T(8,128)(2,1)S(1)}, bf16[96,960]{1,0:T(8,128)(2,1)S(1)}, u32[]{:S(2)}, u32[]{:S(2)}) collective-permute-start(bf16[96,960]{1,0:T(8,128)(2,1)S(1)} %slice_bitcast_fusion.10), channel_id=1, source_target_pairs={{0,3},{1,0},{2,1},{3,2},{4,7},{5,4},{6,5},{7,6},{8,11},{9,8},{10,9... | collective-permute-start | bytes 552968 | tf_op jit(solution)/shard_map/ppermute | solution.py:830
  264.3 4.1 %collective-permute-done.47 = bf16[96,960]{1,0:T(8,128)(2,1)S(1)} collective-permute-done((bf16[96,960]{1,0:T(8,128)(2,1)S(1)}, bf16[96,960]{1,0:T(8,128)(2,1)S(1)}, u32[]{:S(2)}, u32[]{:S(2)}) %collective-permute-start.47) | collective-permute-done | bytes 184352 | tf_op jit(solution)/shard_map/ppermute | solution.py:830
  268.4 7.6 %collective-permute-done.49 = bf16[96,960]{1,0:T(8,128)(2,1)S(1)} collective-permute-done((bf16[96,960]{1,0:T(8,128)(2,1)S(1)}, bf16[96,960]{1,0:T(8,128)(2,1)S(1)}, u32[]{:S(2)}, u32[]{:S(2)}) %collective-permute-start.49) | collective-permute-done | bytes 184352 | tf_op jit(solution)/shard_map/ppermute | solution.py:830
  (239 shorter events, 102.4 us)
Async XLA Ops:
  7.2 71.7 %all-gather.3.cloned.1.call-start = ((), (), s32[]{:S(2)}) async-start(), calls=%async_computation.2 | async-start | bytes 1966080 | tf_op jit(solution)/shard_map/all_gather | solution.py:950
  17.1 16.9 %collective-permute-start.1 = (bf16[256,384]{1,0:T(8,128)(2,1)}, bf16[256,384]{1,0:T(8,128)(2,1)S(1)}, u32[]{:S(2)}, u32[]{:S(2)}) collective-permute-start(bf16[256,384]{1,0:T(8,128)(2,1)} %get-tuple-element.85), channel_id=1, source_target_pairs={{0,2},{1,3},{2,0},{3,1},{4,6},{5,7},{6,4},{7,5},{8,10},{9,11},{10,... | collective-permute-start | bytes 589832 | tf_op jit(solution)/shard_map/ppermute | solution.py:830
  17.1 17.0 %collective-permute-start = (bf16[256,384]{1,0:T(8,128)(2,1)}, bf16[256,384]{1,0:T(8,128)(2,1)S(1)}, u32[]{:S(2)}, u32[]{:S(2)}) collective-permute-start(bf16[256,384]{1,0:T(8,128)(2,1)} %get-tuple-element.85), channel_id=1, source_target_pairs={{0,1},{1,2},{2,3},{3,0},{4,5},{5,6},{6,7},{7,4},{8,9},{9,10},{10,1... | collective-permute-start | bytes 589832 | tf_op jit(solution)/shard_map/ppermute | solution.py:830
  23.8 253.8 %reduce-scatter.2.cloned.1.call-start = ((), (), s32[]{:S(2)}) async-start(), calls=%async_computation.1 | async-start | bytes 1966080 | tf_op jit(solution)/shard_map/reduce_scatter | solution.py:980
  45.2 29.2 %collective-permute-start.6 = (bf16[4,240,384]{2,1,0:T(8,128)(2,1)S(1)}, bf16[4,240,384]{2,1,0:T(8,128)(2,1)}, u32[]{:S(2)}, u32[]{:S(2)}) collective-permute-start(bf16[4,240,384]{2,1,0:T(8,128)(2,1)S(1)} %constant_dynamic-update-slice_fusion.2.refs_2_), channel_id=1, source_target_pairs={{0,8},{4,12},{8,0},{12,4},{16,24},{20,28},{24,16},{28,20},{1,9},{5... | collective-permute-start | bytes 2211848 | tf_op jit(solution)/shard_map/ppermute | solution.py:825
  45.9 28.5 %collective-permute-start.5 = (bf16[4,240,384]{2,1,0:T(8,128)(2,1)S(1)}, bf16[4,240,384]{2,1,0:T(8,128)(2,1)S(1)}, u32[]{:S(2)}, u32[]{:S(2)}) collective-permute-start(bf16[4,240,384]{2,1,0:T(8,128)(2,1)S(1)} %constant_dynamic-update-slice_fusion.refs_0_), channel_id=1, source_target_pairs={{0,16},{4,20},{8,24},{12,28},{16,0},{20,4},{24,8},{28,12},{1,17},{... | collective-permute-start | bytes 2211848 | tf_op jit(solution)/shard_map/ppermute | solution.py:825
  47.5 26.3 %collective-permute-start.15 = (bf16[192,384]{1,0:T(8,128)(2,1)S(1)}, bf16[192,384]{1,0:T(8,128)(2,1)S(1)}, u32[]{:S(2)}, u32[]{:S(2)}) collective-permute-start(bf16[192,384]{1,0:T(8,128)(2,1)S(1)} %copy-done.10), channel_id=1, source_target_pairs={{0,2},{1,3},{2,0},{3,1},{4,6},{5,7},{6,4},{7,5},{8,10},{9,11},{10,... | collective-permute-start | bytes 442376 | tf_op jit(solution)/shard_map/ppermute | solution.py:830
  52.7 21.1 %collective-permute-start.14 = (bf16[192,384]{1,0:T(8,128)(2,1)S(1)}, bf16[192,384]{1,0:T(8,128)(2,1)S(1)}, u32[]{:S(2)}, u32[]{:S(2)}) collective-permute-start(bf16[192,384]{1,0:T(8,128)(2,1)S(1)} %copy-done.10), channel_id=1, source_target_pairs={{0,1},{1,2},{2,3},{3,0},{4,5},{5,6},{6,7},{7,4},{8,9},{9,10},{10,1... | collective-permute-start | bytes 442376 | tf_op jit(solution)/shard_map/ppermute | solution.py:830
  73.8 16.8 %collective-permute-start.12 = (bf16[4,240,384]{2,1,0:T(8,128)(2,1)S(1)}, bf16[4,240,384]{2,1,0:T(8,128)(2,1)}, u32[]{:S(2)}, u32[]{:S(2)}) collective-permute-start(bf16[4,240,384]{2,1,0:T(8,128)(2,1)S(1)} %constant_dynamic-update-slice_fusion.2.refs_2_), channel_id=1, source_target_pairs={{0,4},{4,0},{8,12},{12,8},{16,20},{20,16},{24,28},{28,24},{1,5},{5... | collective-permute-start | bytes 2211848 | tf_op jit(solution)/shard_map/ppermute | solution.py:825
  73.9 17.3 %collective-permute-start.10 = (bf16[4,240,384]{2,1,0:T(8,128)(2,1)S(1)}, bf16[4,240,384]{2,1,0:T(8,128)(2,1)}, u32[]{:S(2)}, u32[]{:S(2)}) collective-permute-start(bf16[4,240,384]{2,1,0:T(8,128)(2,1)S(1)} %constant_dynamic-update-slice_fusion.refs_0_), channel_id=1, source_target_pairs={{0,4},{4,0},{8,12},{12,8},{16,20},{20,16},{24,28},{28,24},{1,5},{5... | collective-permute-start | bytes 2211848 | tf_op jit(solution)/shard_map/ppermute | solution.py:825
  89.4 15.5 %collective-permute-start.20 = (bf16[4,192,384]{2,1,0:T(8,128)(2,1)}, bf16[4,192,384]{2,1,0:T(8,128)(2,1)S(1)}, u32[]{:S(2)}, u32[]{:S(2)}) collective-permute-start(bf16[4,192,384]{2,1,0:T(8,128)(2,1)} %constant_dynamic-update-slice_fusion.6.refs_10_), channel_id=1, source_target_pairs={{0,8},{4,12},{8,0},{12,4},{16,24},{20,28},{24,16},{28,20},{1,9},{5... | collective-permute-start | bytes 1769480 | tf_op jit(solution)/shard_map/ppermute | solution.py:825
  99.0 16.9 %collective-permute-start.23 = (bf16[4,192,384]{2,1,0:T(8,128)(2,1)}, bf16[4,192,384]{2,1,0:T(8,128)(2,1)S(1)}, u32[]{:S(2)}, u32[]{:S(2)}) collective-permute-start(bf16[4,192,384]{2,1,0:T(8,128)(2,1)} %constant_dynamic-update-slice_fusion.6.refs_10_), channel_id=1, source_target_pairs={{0,4},{4,0},{8,12},{12,8},{16,20},{20,16},{24,28},{28,24},{1,5},{5... | collective-permute-start | bytes 1769480 | tf_op jit(solution)/shard_map/ppermute | solution.py:825
  146.2 53.4 %collective-permute-start.31 = (bf16[2,2,2,2,96,960]{5,4,3,2,1,0:T(8,128)(2,1)}, bf16[2,2,2,2,96,960]{5,4,3,2,1,0:T(8,128)(2,1)}, u32[]{:S(2)}, u32[]{:S(2)}) collective-permute-start(bf16[2,2,2,2,96,960]{5,4,3,2,1,0:T(8,128)(2,1)} %get-tuple-element.141), channel_id=1, source_target_pairs={{0,4},{4,0},{8,12},{12,8},{16,20},{20,16},{24,28},{28,24},{1,5},{5... | collective-permute-start | bytes 8847368 | tf_op jit(solution)/shard_map/ppermute | solution.py:825
  156.9 36.7 %collective-permute-start.29 = (bf16[2,2,96,768]{3,2,1,0:T(8,128)(2,1)}, bf16[2,2,96,768]{3,2,1,0:T(8,128)(2,1)}, u32[]{:S(2)}, u32[]{:S(2)}) collective-permute-start(bf16[2,2,96,768]{3,2,1,0:T(8,128)(2,1)} %get-tuple-element.135), channel_id=1, source_target_pairs={{0,8},{4,12},{8,0},{12,4},{16,24},{20,28},{24,16},{28,20},{1,9},{5... | collective-permute-start | bytes 1769480 | tf_op jit(solution)/shard_map/ppermute | solution.py:825
  172.2 24.4 %collective-permute-start.30 = (bf16[2,2,96,768]{3,2,1,0:T(8,128)(2,1)S(1)}, bf16[2,2,96,768]{3,2,1,0:T(8,128)(2,1)}, u32[]{:S(2)}, u32[]{:S(2)}) collective-permute-start(bf16[2,2,96,768]{3,2,1,0:T(8,128)(2,1)S(1)} %copy-done.2), channel_id=1, source_target_pairs={{0,16},{4,20},{8,24},{12,28},{16,0},{20,4},{24,8},{28,12},{1,17},{... | collective-permute-start | bytes 1769480 | tf_op jit(solution)/shard_map/ppermute | solution.py:825
  173.7 16.9 %collective-permute-start.41 = (f32[24,768]{1,0:T(8,128)S(1)}, f32[24,768]{1,0:T(8,128)}, u32[]{:S(2)}, u32[]{:S(2)}) collective-permute-start(f32[24,768]{1,0:T(8,128)S(1)} %add.250), channel_id=1, source_target_pairs={{0,16},{4,20},{8,24},{12,28},{16,0},{20,4},{24,8},{28,12},{1,17},{... | collective-permute-start | bytes 221192 | tf_op jit(solution)/shard_map/ppermute | solution.py:825
  191.5 22.9 %collective-permute-start.45 = (f32[24,768]{1,0:T(8,128)S(1)}, f32[24,768]{1,0:T(8,128)S(1)}, u32[]{:S(2)}, u32[]{:S(2)}) collective-permute-start(f32[24,768]{1,0:T(8,128)S(1)} %add_add_fusion.1), channel_id=1, source_target_pairs={{0,3},{1,0},{2,1},{3,2},{4,7},{5,4},{6,5},{7,6},{8,11},{9,8},{10,9... | collective-permute-start | bytes 221192 | tf_op jit(solution)/shard_map/ppermute | solution.py:830
  192.5 23.9 %collective-permute-start.44 = (f32[24,768]{1,0:T(8,128)S(1)}, f32[24,768]{1,0:T(8,128)S(1)}, u32[]{:S(2)}, u32[]{:S(2)}) collective-permute-start(f32[24,768]{1,0:T(8,128)S(1)} %add_add_fusion.1), channel_id=1, source_target_pairs={{0,2},{1,3},{2,0},{3,1},{4,6},{5,7},{6,4},{7,5},{8,10},{9,11},{10,... | collective-permute-start | bytes 221192 | tf_op jit(solution)/shard_map/ppermute | solution.py:830
  193.6 22.7 %collective-permute-start.43 = (f32[24,768]{1,0:T(8,128)S(1)}, f32[24,768]{1,0:T(8,128)}, u32[]{:S(2)}, u32[]{:S(2)}) collective-permute-start(f32[24,768]{1,0:T(8,128)S(1)} %add_add_fusion.1), channel_id=1, source_target_pairs={{0,1},{1,2},{2,3},{3,0},{4,5},{5,6},{6,7},{7,4},{8,9},{9,10},{10,1... | collective-permute-start | bytes 221192 | tf_op jit(solution)/shard_map/ppermute | solution.py:830
  210.0 20.6 %collective-permute-start.32 = (bf16[2,2,2,1,48,576]{5,4,3,2,1,0:T(8,128)(2,1)}, bf16[2,2,2,1,48,576]{5,4,3,2,1,0:T(8,128)(2,1)}, u32[]{:S(2)}, u32[]{:S(2)}) collective-permute-start(bf16[2,2,2,1,48,576]{5,4,3,2,1,0:T(8,128)(2,1)} %get-tuple-element.144), channel_id=1, source_target_pairs={{0,4},{4,0},{8,12},{12,8},{16,20},{20,16},{24,28},{28,24},{1,5},{5... | collective-permute-start | bytes 1327112 | tf_op jit(solution)/shard_map/ppermute | solution.py:825
  211.8 20.3 %collective-permute-start.33 = (bf16[2,2,96,960]{3,2,1,0:T(8,128)(2,1)}, bf16[2,2,96,960]{3,2,1,0:T(8,128)(2,1)}, u32[]{:S(2)}, u32[]{:S(2)}) collective-permute-start(bf16[2,2,96,960]{3,2,1,0:T(8,128)(2,1)} %get-tuple-element.145), channel_id=1, source_target_pairs={{0,8},{4,12},{8,0},{12,4},{16,24},{20,28},{24,16},{28,20},{1,9},{5... | collective-permute-start | bytes 2211848 | tf_op jit(solution)/shard_map/ppermute | solution.py:825
  220.7 18.9 %collective-permute-start.34 = (bf16[2,2,96,960]{3,2,1,0:T(8,128)(2,1)}, bf16[2,2,96,960]{3,2,1,0:T(8,128)(2,1)S(1)}, u32[]{:S(2)}, u32[]{:S(2)}) collective-permute-start(bf16[2,2,96,960]{3,2,1,0:T(8,128)(2,1)} %get-tuple-element.146), channel_id=1, source_target_pairs={{0,16},{4,20},{8,24},{12,28},{16,0},{20,4},{24,8},{28,12},{1,17},{... | collective-permute-start | bytes 2211848 | tf_op jit(solution)/shard_map/ppermute | solution.py:825
  241.5 16.8 %collective-permute-start.46 = (bf16[2,96,960]{2,1,0:T(8,128)(2,1)S(1)}, bf16[2,96,960]{2,1,0:T(8,128)(2,1)S(1)}, u32[]{:S(2)}, u32[]{:S(2)}) collective-permute-start(bf16[2,96,960]{2,1,0:T(8,128)(2,1)S(1)} %fusion.17), channel_id=1, source_target_pairs={{0,16},{4,20},{8,24},{12,28},{16,0},{20,4},{24,8},{28,12},{1,17},{... | collective-permute-start | bytes 1105928 | tf_op jit(solution)/shard_map/ppermute | solution.py:825
  243.0 19.6 %collective-permute-start.48 = (bf16[2,96,960]{2,1,0:T(8,128)(2,1)S(1)}, bf16[2,96,960]{2,1,0:T(8,128)(2,1)S(1)}, u32[]{:S(2)}, u32[]{:S(2)}) collective-permute-start(bf16[2,96,960]{2,1,0:T(8,128)(2,1)S(1)} %fusion.18), channel_id=1, source_target_pairs={{0,8},{4,12},{8,0},{12,4},{16,24},{20,28},{24,16},{28,20},{1,9},{5... | collective-permute-start | bytes 1105928 | tf_op jit(solution)/shard_map/ppermute | solution.py:825
  (68 other events, 733.0 us)
Sparse Core Ops, SparseCore 0:
  23.9 49.2 all-gather.2
  178.0 38.5 reduce-scatter.1
where the time goes:
time: 288 us; the launch traced here: 287 us
  waiting for transfers between devices  103 us (36%)
  Pallas kernels  67.3 us (23%)
  starting transfers between devices  57.8 us (20%)
  other arithmetic  25.1 us (9%)
  local copies, waits for them, and re-layouts  18.7 us (6%)
  between operations  14.7 us (5%)
    ppermute x21, waiting for transfers between devices, shift(): lax.ppermute(values, 'tensor', [(i, (i + step) % size) for i in range(siz...  56.8 us
    ppermute x35, waiting for transfers between devices, swap(): return lax.ppermute(values, 'dp', [(i, i ^ mask) for i in range(size)])  46.3 us
    ppermute x21, starting transfers between devices, shift(): lax.ppermute(values, 'tensor', [(i, (i + step) % size) for i in range(siz...  31.3 us
    ppermute x35, starting transfers between devices, swap(): return lax.ppermute(values, 'dp', [(i, i ^ mask) for i in range(size)])  26.5 us
    convert_element_type x14, other arithmetic, add_low(): return sum((entry.astype(f32) for entry in entries)).astype(bf16)  18.9 us
    pallas_call x1, Pallas kernels, ffn_down(): pl.pallas_call(ffn_down_kernel, in_specs=[pl.BlockSpec(memory_space=pltpu...  15.6 us
    pallas_call x1, Pallas kernels, attend_back(): pl.pallas_call(functools.partial(attend_back_kernel, count), grid=(heads,...  10.6 us
    pallas_call x1, Pallas kernels, ffn_up(): pl.pallas_call(ffn_up_kernel, in_specs=[pl.BlockSpec(memory_space=pltpu.S...  9.3 us
  transfers between devices with their start and end apart: 58, of which 23 were waited for; matrix products, arithmetic and copies ran while one was open for 13% of the time, Pallas kernels for 15%

commit v1 on v0

v1 whole, which is shorter than its diff:
```python
import functools
import math

import jax
import jax.numpy as jnp
from jax import lax
from jax.experimental import pallas as pl
from jax.experimental.pallas import tpu as pltpu
from jax.sharding import PartitionSpec as P

HEAD_DIM = 64
FEAT = 256
PLANE = 8
COST_RATE = 9e9

eps = 1e-06
bf16 = jnp.bfloat16
f32 = jnp.float32


def dot(left, right):
    return jnp.dot(left, right, preferred_element_type=f32)


def dot_rows(left, right):
    return lax.dot_general(left, right, (((0,), (0,)), ((), ())), preferred_element_type=f32)


def dot_cols(left, right):
    return lax.dot_general(left, right, (((1,), (1,)), ((), ())), preferred_element_type=f32)


def cost(micros):
    return pl.CostEstimate(flops=int(micros * COST_RATE), transcendentals=0, bytes_accessed=0)


def pack_kernel(
    own_ref, bias_ref, tokens_ref, hidden_ref, mixer_ref, output_ref, xt_ref, first_ref, second_ref, held_ref, sems
):
    rows, columns = second_ref.shape
    chip = lax.shift_right_logical(own_ref[0], 1)
    core = lax.bitwise_and(own_ref[0], 1)
    mixer_rows = mixer_ref.shape[0] // (PLANE // 2)

    def copy(source, height, target, sem):
        begin = pl.multiple_of(chip * height, 16)
        return pltpu.make_async_copy(
            source.at[pl.ds(begin, height), lanes(core, columns)], target, sem
        )

    copies = [
        copy(hidden_ref, rows, first_ref.at[0:rows], sems.at[0]),
        copy(mixer_ref, mixer_rows, first_ref.at[rows : rows + mixer_rows], sems.at[1]),
        copy(output_ref, rows, second_ref, sems.at[2]),
    ]
    fetch = pltpu.make_async_copy(tokens_ref, held_ref, sems.at[3])
    fetch.start()
    start_all([copies])
    wide = jnp.concatenate([bias_ref[...], jnp.zeros((16 - bias_ref.shape[0], 128), f32)], axis=0)
    for index in range(3):
        part = wide.astype(bf16)
        wide = wide - part.astype(f32)
        first_ref[rows + mixer_rows :, index * 128 : (index + 1) * 128] = part
    fetch.wait()
    xt_ref[...] = held_ref[...].T
    wait_all(copies)


def pack(own, tokens, hidden_bias, hidden_weight, mixer_weight, output_weight):
    local, depth = tokens.shape
    chips = PLANE // 2
    columns = depth // 2
    rows = depth // chips
    first_rows = rows + mixer_weight.shape[0] // chips + 16
    vmem = pl.BlockSpec(memory_space=pltpu.VMEM)
    return pl.pallas_call(
        pack_kernel,
        in_specs=[pl.BlockSpec(memory_space=pltpu.SMEM), vmem] + [pl.BlockSpec(memory_space=pltpu.HBM)] * 4,
        out_specs=[vmem] * 3,
        out_shape=[
            jax.ShapeDtypeStruct((depth, local), bf16),
            jax.ShapeDtypeStruct((first_rows, columns), bf16),
            jax.ShapeDtypeStruct((rows, columns), bf16),
        ],
        scratch_shapes=[pltpu.VMEM((local, depth), bf16), pltpu.SemaphoreType.DMA((4,))],
        compiler_params=pltpu.CompilerParams(vmem_limit_bytes=60 << 20),
        cost_estimate=cost(3),
        name="pack",
    )(own, hidden_bias, tokens, hidden_weight, mixer_weight, output_weight)


def unpack_bias(entries):
    wide = entries.astype(f32)
    wide = wide[:, :128] + wide[:, 128:256] + wide[:, 256:384]
    return jnp.concatenate([wide[index : index + 1] for index in range(6)], axis=1)


def prepare_kernel(query_ref, key_ref, value_ref, joined_ref):
    joined_ref[...] = jnp.concatenate([query_ref[...].T, key_ref[...].T, value_ref[...].T], axis=1)


def prepare(weights):
    width, depth = weights[0].shape
    vmem = pl.BlockSpec(memory_space=pltpu.VMEM)
    return pl.pallas_call(
        prepare_kernel,
        in_specs=[vmem] * 3,
        out_specs=vmem,
        out_shape=jax.ShapeDtypeStruct((depth, 3 * width), bf16),
        compiler_params=pltpu.CompilerParams(vmem_limit_bytes=60 << 20),
        cost_estimate=cost(4),
        name="prepare",
    )(*weights)


def lanes(index, size):
    return pl.ds(pl.multiple_of(index * size, size), size)


def segments(lengths_ref, count, shape):
    places = lax.broadcasted_iota(jnp.int32, shape, len(shape) - 1)
    seg = jnp.zeros(shape, jnp.int32)
    end = jnp.int32(0)
    for s in range(count):
        end = end + lengths_ref[0, s]
        seg = seg + (places >= end).astype(jnp.int32)
    return seg


def masked_copies(seg, entries, count):
    zero = jnp.zeros_like(entries)
    return [jnp.where(seg == s, entries, zero) for s in range(count)]


def one_hot_rows(seg, count):
    rows = lax.broadcasted_iota(jnp.int32, (8, seg.shape[1]), 0)
    return jnp.where((rows == seg) & (rows < count), 1.0, 0.0).astype(f32)


def masked_sum(seg, wide, count):
    height = HEAD_DIM
    total = jnp.zeros((height, wide.shape[1]), f32)
    for s in range(count):
        total = total + jnp.where(seg == s, wide[s * height : (s + 1) * height], 0.0)
    return total


def feature_rows(vectors, proj_t):
    scale = HEAD_DIM ** (-0.25)
    widened = vectors.astype(f32)
    square = (0.5 * scale * scale) * jnp.sum(widened * widened, axis=0, keepdims=True)
    return (jnp.exp(scale * dot(proj_t, vectors) - square) * (1.0 / math.sqrt(FEAT))).astype(bf16)


def attend_kernel(
    count,
    lengths_ref,
    place_ref,
    xt_ref,
    query_weight_ref,
    key_weight_ref,
    value_weight_ref,
    query_bias_ref,
    key_bias_ref,
    value_bias_ref,
    proj_ref,
    qkv_ref,
    qf_ref,
    kf_ref,
    state_ref,
    out_ref,
    den_ref,
    p0_ref,
    p1_ref,
    p2_ref,
    p3_ref,
    mixed_ref,
):
    h = pl.program_id(0)
    shards, _, local = xt_ref.shape
    heads = pl.num_programs(0)
    width = query_weight_ref.shape[0]
    spread_rows = count * HEAD_DIM

    @pl.when(h == 0)
    def _():
        for kind, (weight, bias) in enumerate(
            (
                (query_weight_ref, query_bias_ref),
                (key_weight_ref, key_bias_ref),
                (value_weight_ref, value_bias_ref),
            )
        ):
            column = jnp.broadcast_to(bias[...], (8, width)).T[:, 0:1]
            for s in range(shards):
                qkv_ref[kind * width : (kind + 1) * width, s * local : (s + 1) * local] = (
                    dot(weight[...], xt_ref[s]) + column
                ).astype(bf16)

    def rows(kind):
        begin = pl.multiple_of(kind * width + h * HEAD_DIM, HEAD_DIM)
        return qkv_ref[pl.ds(begin, HEAD_DIM), :]

    seg = segments(lengths_ref, count, (1, shards * local))
    hot = one_hot_rows(seg, count)
    proj_t = proj_ref[0].T
    q_feat = feature_rows(rows(0), proj_t)
    k_feat = feature_rows(rows(1), proj_t)
    qf_ref[0] = q_feat
    kf_ref[0] = k_feat
    wide = jnp.concatenate(
        masked_copies(seg, rows(2), count) + [jnp.concatenate([hot, hot], axis=0).astype(bf16)], axis=0
    )
    state = dot_cols(wide, k_feat)
    sums = state[spread_rows : spread_rows + 8]
    high = sums.astype(bf16).astype(f32)
    state_ref[0, :spread_rows] = state[:spread_rows].astype(bf16)
    state_ref[0, spread_rows : spread_rows + 16] = jnp.concatenate([high, high], axis=0).astype(bf16)
    state_ref[0, spread_rows + 16 :] = jnp.concatenate(
        [sums - high, jnp.zeros_like(high)], axis=0
    ).astype(bf16)
    through = dot(state_ref[0], q_feat)
    scores = through[spread_rows : spread_rows + 8] + through[spread_rows + 16 : spread_rows + 24]
    den = jnp.sum(hot * scores, axis=0, keepdims=True) + (seg >= count).astype(f32)
    out = masked_sum(seg, through, count) / den
    out_ref[...] = out
    den_ref[0] = jnp.broadcast_to(den, den_ref.shape[1:])
    mixed_ref[pl.ds(pl.multiple_of(h * HEAD_DIM, HEAD_DIM), HEAD_DIM), :] = out.astype(bf16)

    @pl.when(h == heads - 1)
    def _():
        for s, piece in enumerate((p0_ref, p1_ref, p2_ref, p3_ref)):
            piece[...] = mixed_ref[:, lanes(lax.bitwise_xor(place_ref[0], s), local)]


def attend(xt, weights, biases, proj, lengths, place):
    shards, depth, local = xt.shape
    heads, head_dim, feat = proj.shape
    total = shards * local
    count = lengths.shape[1] - 1
    width = heads * head_dim
    state_rows = count * head_dim + 32
    smem = pl.BlockSpec(memory_space=pltpu.SMEM)

    def whole(*shape):
        return pl.BlockSpec(shape, lambda h: (0,) * len(shape))

    def per_head(*shape):
        return pl.BlockSpec((1,) + shape, lambda h: (h,) + (0,) * len(shape))

    return pl.pallas_call(
        functools.partial(attend_kernel, count),
        grid=(heads,),
        in_specs=[
            smem,
            smem,
            whole(shards, depth, local),
        ]
        + [whole(width, depth)] * 3
        + [whole(1, width)] * 3
        + [per_head(head_dim, feat)],
        out_specs=[
            whole(3 * width, total),
            per_head(feat, total),
            per_head(feat, total),
            per_head(state_rows, feat),
            pl.BlockSpec((head_dim, total), lambda h: (h, 0)),
            per_head(8, total),
        ]
        + [whole(width, local)] * shards,
        out_shape=[
            jax.ShapeDtypeStruct((3 * width, total), bf16),
            jax.ShapeDtypeStruct((heads, feat, total), bf16),
            jax.ShapeDtypeStruct((heads, feat, total), bf16),
            jax.ShapeDtypeStruct((heads, state_rows, feat), bf16),
            jax.ShapeDtypeStruct((width, total), f32),
            jax.ShapeDtypeStruct((heads, 8, total), f32),
        ]
        + [jax.ShapeDtypeStruct((width, local), bf16)] * shards,
        scratch_shapes=[pltpu.VMEM((width, total), bf16)],
        compiler_params=pltpu.CompilerParams(vmem_limit_bytes=60 << 20),
        cost_estimate=cost(8),
        name="attend",
    )(lengths, place, xt, *weights, *biases, proj)


def feature_back_rows(grad_feat, feat, vectors, proj_w):
    scale = HEAD_DIM ** (-0.25)
    grad_proj = grad_feat * feat.astype(f32)
    pulled = scale * dot(proj_w, grad_proj.astype(bf16))
    return pulled - (scale * scale) * vectors.astype(f32) * jnp.sum(grad_proj, axis=0, keepdims=True)


def attend_back_kernel(
    count,
    lengths_ref,
    place_ref,
    qkv_ref,
    qf_ref,
    kf_ref,
    state_ref,
    out_ref,
    den_ref,
    g0_ref,
    g1_ref,
    g2_ref,
    g3_ref,
    proj_ref,
    weight_ref,
    sums_ref,
    grad_ref,
    send_ref,
    keep_ref,
    heads_ref,
    small_ref,
):
    h = pl.program_id(0)
    width, local = g0_ref.shape
    shards = grad_ref.shape[1] // local
    depth = weight_ref.shape[0]
    heads = pl.num_programs(0)
    spread_rows = count * HEAD_DIM

    @pl.when(h == 0)
    def _():
        for s, piece in enumerate((g0_ref, g1_ref, g2_ref, g3_ref)):
            heads_ref[:, lanes(lax.bitwise_xor(place_ref[0], s), local)] = piece[...]

    def at(kind):
        return pl.ds(pl.multiple_of(kind * width + h * HEAD_DIM, HEAD_DIM), HEAD_DIM)

    seg = segments(lengths_ref, count, (1, shards * local))
    hot = one_hot_rows(seg, count)
    query, key, value = qkv_ref[at(0), :], qkv_ref[at(1), :], qkv_ref[at(2), :]
    q_feat, k_feat = qf_ref[0], kf_ref[0]
    grad_head = heads_ref[pl.ds(pl.multiple_of(h * HEAD_DIM, HEAD_DIM), HEAD_DIM), :].astype(f32)
    den = den_ref[0, 0:1, :]
    grad_numer = (grad_head / den).astype(bf16)
    grad_den = -jnp.sum(grad_head * out_ref[...], axis=0, keepdims=True) / den
    marked = hot * grad_den
    high = marked.astype(bf16).astype(f32)
    low = marked - high
    numer_wide = jnp.concatenate(
        masked_copies(seg, grad_numer, count)
        + [
            jnp.concatenate([high, low], axis=0).astype(bf16),
            jnp.concatenate([high, jnp.zeros_like(high)], axis=0).astype(bf16),
        ],
        axis=0,
    )
    grad_state = dot_cols(numer_wide[: spread_rows + 16], q_feat)
    sums = grad_state[spread_rows : spread_rows + 8] + grad_state[spread_rows + 8 : spread_rows + 16]
    sums_high = sums.astype(bf16).astype(f32)
    grad_state = jnp.concatenate(
        [
            grad_state[:spread_rows].astype(bf16),
            jnp.concatenate([sums_high, sums - sums_high], axis=0).astype(bf16),
        ],
        axis=0,
    )
    value_wide = jnp.concatenate(
        masked_copies(seg, value, count) + [jnp.concatenate([hot, hot], axis=0).astype(bf16)], axis=0
    )
    proj_w = proj_ref[0]
    grad_qfeat = dot_rows(state_ref[0], numer_wide)
    grad_ref[at(0), :] = feature_back_rows(grad_qfeat, q_feat, query, proj_w).astype(bf16)
    grad_kfeat = dot_rows(grad_state, value_wide)
    grad_ref[at(1), :] = feature_back_rows(grad_kfeat, k_feat, key, proj_w).astype(bf16)
    grad_ref[at(2), :] = masked_sum(seg, dot(grad_state[:spread_rows], k_feat), count).astype(bf16)

    @pl.when(h == heads - 1)
    def _():
        small_ref[...] = sums_ref[...]
        totals = dot_cols(jnp.ones((8, shards * local), bf16), grad_ref[...])
        for t in range(shards):

            @pl.when(place_ref[0] == t)
            def _():
                for kind, row in enumerate(BIAS_ROWS):
                    small_ref[row : row + 1, t * width : (t + 1) * width] = totals[
                        0:1, kind * width : (kind + 1) * width
                    ]

        small = jnp.concatenate(
            [small_ref[:, begin : begin + local] for begin in range(0, depth, local)], axis=0
        )
        rows = small.shape[0]
        high = small.astype(bf16)
        low = (small - high.astype(f32)).astype(bf16)
        for s in range(shards):
            out = (keep_ref, send_ref)[s % 2].at[s // 2]
            out[:depth] = dot(
                weight_ref[...], grad_ref[:, lanes(lax.bitwise_xor(place_ref[0], s), local)]
            ).astype(bf16)
            out[depth : depth + rows] = high
            out[depth + rows :] = low


def attend_back(saved, pieces, proj, weight, sums, lengths, place):
    qkv, qf, kf, state, out, den = saved
    heads, feat, total = qf.shape
    width, local = pieces[0].shape
    shards = total // local
    depth = weight.shape[0]
    count = lengths.shape[1] - 1
    state_rows = state.shape[1]
    extra = 2 * sums.shape[0] * (depth // local)
    smem = pl.BlockSpec(memory_space=pltpu.SMEM)

    def whole(*shape):
        return pl.BlockSpec(shape, lambda h: (0,) * len(shape))

    def per_head(*shape):
        return pl.BlockSpec((1,) + shape, lambda h: (h,) + (0,) * len(shape))

    return pl.pallas_call(
        functools.partial(attend_back_kernel, count),
        grid=(heads,),
        in_specs=[
            smem,
            smem,
            whole(3 * width, total),
            per_head(feat, total),
            per_head(feat, total),
            per_head(state_rows, feat),
            pl.BlockSpec((HEAD_DIM, total), lambda h: (h, 0)),
            per_head(8, total),
        ]
        + [whole(width, local)] * shards
        + [per_head(HEAD_DIM, feat), whole(depth, 3 * width), whole(*sums.shape)],
        out_specs=[
            whole(3 * width, total),
            whole(shards // 2, depth + extra, local),
            whole(shards // 2, depth + extra, local),
        ],
        out_shape=[
            jax.ShapeDtypeStruct((3 * width, total), bf16),
            jax.ShapeDtypeStruct((shards // 2, depth + extra, local), bf16),
            jax.ShapeDtypeStruct((shards // 2, depth + extra, local), bf16),
        ],
        scratch_shapes=[pltpu.VMEM((width, total), bf16), pltpu.VMEM(sums.shape, f32)],
        compiler_params=pltpu.CompilerParams(vmem_limit_bytes=28 << 20),
        cost_estimate=cost(9),
        name="attend_back",
    )(lengths, place, qkv, qf, kf, state, out, den, *pieces, proj, weight, sums)


def slot_place(slot, half):
    k = slot // 2
    if half == 0:
        return 1 - k % 2, k // 2
    return 1 - k // 2, k % 2


def pick_blocks(own, turned_ref):
    slots = turned_ref.shape[0]
    return jnp.concatenate([turned_ref[lax.bitwise_xor(own, slot)] for slot in range(0, slots, 2)], axis=0)


def emit_slots(entries, outs, begin=0):
    height = outs[0].shape[2]
    count = entries.shape[1]
    for half in range(2):

        @pl.when(pl.program_id(0) // 2 == half)
        def _():
            for k in range(PLANE // 2):
                part, index = slot_place(2 * k, half)
                outs[2 * half + part][index, 0, :, begin : begin + count] = entries[k * height : (k + 1) * height]


def slot_outputs(shards, height, count):
    low = pl.BlockSpec((2, 1, height, count), lambda s: (0, jnp.minimum(s, 1), 0, 0))
    high = pl.BlockSpec((2, 1, height, count), lambda s: (0, jnp.maximum(s - 2, 0), 0, 0))
    shape = jax.ShapeDtypeStruct((2, shards // 2, height, count), bf16)
    return [low, low, high, high], [shape] * 4


def output_grad_kernel(own_ref, turned_ref, turned_far_ref, act_ref, act_far_ref, *outs):
    own = own_ref[0]
    grads = dot(pick_blocks(own, turned_ref), act_ref[0]) + dot(pick_blocks(own, turned_far_ref), act_far_ref[0])
    emit_slots(grads.astype(bf16), outs)


def output_grad(own, turned, turned_far, acts, acts_far):
    shards, rows, hidden = acts.shape
    slots, height, _ = turned.shape
    specs, shapes = slot_outputs(shards, height, hidden)
    whole = pl.BlockSpec((slots, height, rows), lambda s: (0, 0, 0))
    by_shard = pl.BlockSpec((1, rows, hidden), lambda s: (s, 0, 0))
    return pl.pallas_call(
        output_grad_kernel,
        grid=(shards,),
        in_specs=[pl.BlockSpec(memory_space=pltpu.SMEM), whole, whole, by_shard, by_shard],
        out_specs=specs,
        out_shape=shapes,
        compiler_params=pltpu.CompilerParams(vmem_limit_bytes=16 << 20),
        cost_estimate=cost(4),
        name="output_grad",
    )(own, turned, turned_far, acts, acts_far)


def hidden_grad_kernel(
    own_ref,
    first_ref,
    first_far_ref,
    grad_pre_ref,
    grad_pre_far_ref,
    branch_ref,
    branch_far_ref,
    mixed_ref,
    mixed_far_ref,
    *outs,
):
    own = own_ref[0]
    hidden = grad_pre_ref.shape[2]
    grads = dot(pick_blocks(own, first_ref), grad_pre_ref[0]) + dot(
        pick_blocks(own, first_far_ref), grad_pre_far_ref[0]
    )
    emit_slots(grads.astype(bf16), outs)
    grads = dot_cols(pick_blocks(own, branch_ref), mixed_ref[0]) + dot_cols(
        pick_blocks(own, branch_far_ref), mixed_far_ref[0]
    )
    emit_slots(grads.astype(bf16), outs, hidden)


def hidden_grad(own, first, first_far, grad_pre, grad_pre_far, branch, branch_far, mixed, mixed_far):
    shards, rows, hidden = grad_pre.shape
    slots, height, _ = first.shape
    width = mixed.shape[1]
    specs, shapes = slot_outputs(shards, height, hidden + width)
    whole = pl.BlockSpec((slots, height, rows), lambda s: (0, 0, 0))
    by_shard = pl.BlockSpec((1, rows, hidden), lambda s: (s, 0, 0))
    piece = pl.BlockSpec((1, width, rows), lambda s: (s, 0, 0))
    return pl.pallas_call(
        hidden_grad_kernel,
        grid=(shards,),
        in_specs=[
            pl.BlockSpec(memory_space=pltpu.SMEM),
            whole,
            whole,
            by_shard,
            by_shard,
            whole,
            whole,
            piece,
            piece,
        ],
        out_specs=specs,
        out_shape=shapes,
        compiler_params=pltpu.CompilerParams(vmem_limit_bytes=16 << 20),
        cost_estimate=cost(5),
        name="hidden_grad",
    )(own, first, first_far, grad_pre, grad_pre_far, branch, branch_far, mixed, mixed_far)


def qkv_grad_kernel(own_ref, xt_ref, grad_ref, even_ref, odd_ref, hold_ref):
    shards, _, local = xt_ref.shape
    grads = sum(
        dot_cols(xt_ref[d], grad_ref[:, d * local : (d + 1) * local]) for d in range(shards)
    )
    hold_ref[...] = grads.astype(bf16).reshape(hold_ref.shape)
    rows = even_ref.shape[4]
    for slot in range(hold_ref.shape[0]):
        target = odd_ref if slot % 2 else even_ref
        block = hold_ref[lax.bitwise_xor(own_ref[0], slot)]
        for half in range(2):
            target[(half,) + slot_place(slot, half) + (0,)] = block[half * rows : (half + 1) * rows]


def qkv_grad(own, slots, xt, grads):
    shards, depth, local = xt.shape
    count = grads.shape[0]
    vmem = pl.BlockSpec(memory_space=pltpu.VMEM)
    shape = jax.ShapeDtypeStruct((2, 2, slots // 4, 1, depth // slots // 2, count), bf16)
    return pl.pallas_call(
        qkv_grad_kernel,
        in_specs=[pl.BlockSpec(memory_space=pltpu.SMEM), vmem, vmem],
        out_specs=[vmem, vmem],
        out_shape=[shape, shape],
        scratch_shapes=[pltpu.VMEM((slots, depth // slots, count), bf16)],
        compiler_params=pltpu.CompilerParams(vmem_limit_bytes=16 << 20),
        cost_estimate=cost(2),
        name="qkv_grad",
    )(own, xt, grads)


def norm_rows(resid):
    center = resid - jnp.mean(resid, axis=-1, keepdims=True)
    inverse = lax.rsqrt(jnp.mean(center * center, axis=-1, keepdims=True) + eps)
    return center * inverse, inverse


HELD = [(0, (0, 1, 2, 3)), (2, (0, 1, 2, 3)), (4, (0, 1, 2, 3)), (6, (0, 1)), (6, (2, 3))]
HELD = HELD + [(mask ^ 1, shards) for mask, shards in HELD]


def place_copies(own, held, begin, rows, target, sems):
    columns = held[0].shape[2]
    copies = [[] for _ in range(target.shape[0])]
    for piece, (mask, shards) in zip(held, HELD):
        source = lax.bitwise_xor(own, mask)
        chip = lax.shift_right_logical(source, 1)
        core = lax.bitwise_and(source, 1)
        for index, s in enumerate(shards):
            copies[s].append(
                pltpu.make_async_copy(
                    piece.at[index, pl.ds(begin, rows), :],
                    target.at[s, chip, :, lanes(core, columns)],
                    sems.at[s, mask],
                )
            )
    return copies


def start_all(copies):
    for entries in copies:
        for copy in entries:
            copy.start()


def wait_all(entries):
    for copy in entries:
        copy.wait()


def ffn_up_kernel(
    own_ref,
    tokens_ref,
    p0_ref,
    p1_ref,
    p2_ref,
    p3_ref,
    mixer_bias_ref,
    gain_ref,
    shift_ref,
    *refs,
):
    held, refs = refs[: len(HELD)], refs[len(HELD) :]
    parts, refs = refs[:4], refs[4:]
    (
        normed_ref,
        inverse_ref,
        turned_ref,
        mixed_ref,
        act_ref,
        slope_ref,
        mixer_ref,
        hidden_ref,
        bias_ref,
        mixer_sem,
        hidden_sem,
        bias_sem,
    ) = refs
    own = own_ref[0]
    shards, chips, mixer_rows, depth = mixer_ref.shape
    hidden_rows = hidden_ref.shape[2]
    mixer_copies = place_copies(own, held, hidden_rows, mixer_rows, mixer_ref, mixer_sem)
    hidden_copies = place_copies(own, held, 0, hidden_rows, hidden_ref, hidden_sem)
    bias_rows = parts[0].shape[0] - 16
    bias_copies = [
        pltpu.make_async_copy(part.at[bias_rows : bias_rows + 16], bias_ref.at[s], bias_sem.at[s])
        for s, part in enumerate(parts)
    ]
    start_all(mixer_copies)
    start_all(hidden_copies)
    start_all([bias_copies])
    resid = tokens_ref[...].astype(f32) + mixer_bias_ref[...]
    for s, piece in enumerate((p0_ref, p1_ref, p2_ref, p3_ref)):
        mixed_ref[s] = piece[...]
        wait_all(mixer_copies[s])
        resid = resid + dot_rows(piece[...], mixer_ref[s].reshape(chips * mixer_rows, depth))
    normed, inverse = norm_rows(resid)
    normed_ref[...] = normed
    inverse_ref[...] = jnp.broadcast_to(inverse, inverse_ref.shape)
    first_low = (normed * gain_ref[...] + shift_ref[...]).astype(bf16)
    turned_ref[...] = first_low.T
    for s in range(shards):
        wait_all(hidden_copies[s] + [bias_copies[s]])
        bias = unpack_bias(bias_ref[s])
        pre = dot(first_low, hidden_ref[s].reshape(chips * hidden_rows, hidden_ref.shape[3])) + bias
        phi = 0.5 * (1.0 + lax.erf(pre * math.sqrt(0.5)))
        act_ref[s] = (pre * phi).astype(bf16)
        slope_ref[s] = (
            phi + pre * jnp.exp(-0.5 * pre * pre) * (1.0 / math.sqrt(2.0 * math.pi))
        ).astype(bf16)


def ffn_up(own, tokens, pieces, mixer_bias, gain, shift_by, parts, held, mixer_rows):
    rows, depth = tokens.shape
    shards = len(pieces)
    chips = PLANE // 2
    hidden = 2 * held[0].shape[2]
    hidden_rows = held[0].shape[1] - mixer_rows
    vmem = pl.BlockSpec(memory_space=pltpu.VMEM)
    return pl.pallas_call(
        ffn_up_kernel,
        in_specs=[pl.BlockSpec(memory_space=pltpu.SMEM)]
        + [vmem] * (1 + shards + 3)
        + [pl.BlockSpec(memory_space=pltpu.HBM)] * (len(HELD) + shards),
        out_specs=[vmem] * 6,
        out_shape=[
            jax.ShapeDtypeStruct((rows, depth), f32),
            jax.ShapeDtypeStruct((rows, 128), f32),
            jax.ShapeDtypeStruct((depth, rows), bf16),
            jax.ShapeDtypeStruct((shards,) + pieces[0].shape, bf16),
            jax.ShapeDtypeStruct((shards, rows, hidden), bf16),
            jax.ShapeDtypeStruct((shards, rows, hidden), bf16),
        ],
        scratch_shapes=[
            pltpu.VMEM((shards, chips, mixer_rows, depth), bf16),
            pltpu.VMEM((shards, chips, hidden_rows, hidden), bf16),
            pltpu.VMEM((shards, 16, held[0].shape[2]), bf16),
            pltpu.SemaphoreType.DMA((shards, PLANE)),
            pltpu.SemaphoreType.DMA((shards, PLANE)),
            pltpu.SemaphoreType.DMA((shards,)),
        ],
        compiler_params=pltpu.CompilerParams(vmem_limit_bytes=28 << 20),
        cost_estimate=cost(8),
        name="ffn_up",
    )(own, tokens, *pieces, mixer_bias, gain, shift_by, *held, *parts)


def norm_rows_back(scaled, normed, inverse):
    return inverse * (
        scaled
        - jnp.mean(scaled, axis=-1, keepdims=True)
        - normed * jnp.mean(scaled * normed, axis=-1, keepdims=True)
    )


def column_sum(entries):
    return jnp.sum(entries, axis=0, keepdims=True)


def ffn_down_kernel(
    own_ref,
    normed_ref,
    inverse_ref,
    act_ref,
    slope_ref,
    cotangent_ref,
    first_gain_ref,
    first_shift_ref,
    output_bias_ref,
    gain_ref,
    shift_ref,
    *refs,
):
    held, refs = refs[: len(HELD)], refs[len(HELD) :]
    held_out, refs = refs[: len(HELD)], refs[len(HELD) :]
    (
        layer_ref,
        resid_ref,
        b0_ref,
        b1_ref,
        b2_ref,
        b3_ref,
        grad_ffn_ref,
        grad_pre_ref,
        grad_branch_ref,
        sums_ref,
        mixer_ref,
        hidden_ref,
        output_ref,
        mixer_sem,
        hidden_sem,
        output_sem,
    ) = refs
    own, place = own_ref[0], own_ref[1]
    shards, chips, mixer_rows, depth = mixer_ref.shape
    hidden_rows = hidden_ref.shape[2]
    hidden = hidden_ref.shape[3]
    output_copies = place_copies(own, held_out, 0, output_ref.shape[2], output_ref, output_sem)
    hidden_copies = place_copies(own, held, 0, hidden_rows, hidden_ref, hidden_sem)
    mixer_copies = place_copies(own, held, hidden_rows, mixer_rows, mixer_ref, mixer_sem)
    start_all(output_copies)
    start_all(hidden_copies)
    start_all(mixer_copies)
    normed_one = normed_ref[...]
    resid = normed_one * first_gain_ref[...] + first_shift_ref[...] + output_bias_ref[...]
    for s in range(shards):
        wait_all(output_copies[s])
        resid = resid + dot(act_ref[s], output_ref[s].reshape(hidden, depth))
    normed, inverse = norm_rows(resid)
    layer_ref[...] = (normed * gain_ref[...] + shift_ref[...]).astype(bf16)
    grad_out = cotangent_ref[...].astype(f32)
    sums_ref[0:1] = column_sum(grad_out * normed)
    sums_ref[1:2] = column_sum(grad_out)
    grad_two = norm_rows_back(grad_out * gain_ref[...], normed, inverse)
    grad_ffn = grad_two.astype(bf16)
    grad_ffn_ref[...] = grad_ffn.T
    sums_ref[2:3] = column_sum(grad_ffn.astype(f32))
    grad_first = grad_two
    for s in range(shards):
        grad_pre = (
            dot_cols(grad_ffn, output_ref[s].reshape(hidden, depth)) * slope_ref[s].astype(f32)
        ).astype(bf16)
        grad_pre_ref[s] = grad_pre
        sums_ref[pl.ds(8 + lax.bitwise_xor(place, s), 1)] = column_sum(grad_pre.astype(f32))
        wait_all(hidden_copies[s])
        grad_first = grad_first + dot_cols(grad_pre, hidden_ref[s].reshape(depth, hidden))
    sums_ref[3:4] = column_sum(grad_first * normed_one)
    sums_ref[4:5] = column_sum(grad_first)
    grad_one = norm_rows_back(grad_first * first_gain_ref[...], normed_one, inverse_ref[:, 0:1])
    resid_ref[...] = grad_one
    grad_branch = grad_one.astype(bf16)
    branch_turned = grad_branch.T
    grad_branch_ref[...] = branch_turned
    sums_ref[5:6] = column_sum(grad_branch.astype(f32))
    sums_ref[6:8] = jnp.zeros((2, depth), f32)
    sums_ref[8 + shards :] = jnp.zeros((8 - shards, depth), f32)
    for s, back in enumerate((b0_ref, b1_ref, b2_ref, b3_ref)):
        wait_all(mixer_copies[s])
        back[...] = dot(mixer_ref[s].reshape(chips * mixer_rows, depth), branch_turned).astype(bf16)


def ffn_down(own, normed, inverse, acts, slopes, cotangent, vectors, held, held_out, mixer_rows):
    rows, depth = normed.shape
    shards, _, hidden = acts.shape
    chips = PLANE // 2
    hidden_rows = held[0].shape[1] - mixer_rows
    output_rows = held_out[0].shape[1]
    vmem = pl.BlockSpec(memory_space=pltpu.VMEM)
    width = chips * mixer_rows
    return pl.pallas_call(
        ffn_down_kernel,
        in_specs=[pl.BlockSpec(memory_space=pltpu.SMEM)]
        + [vmem] * 10
        + [pl.BlockSpec(memory_space=pltpu.HBM)] * (2 * len(HELD)),
        out_specs=[vmem] * (6 + shards),
        out_shape=[
            jax.ShapeDtypeStruct((rows, depth), bf16),
            jax.ShapeDtypeStruct((rows, depth), f32),
        ]
        + [jax.ShapeDtypeStruct((width, rows), bf16)] * shards
        + [
            jax.ShapeDtypeStruct((depth, rows), bf16),
            jax.ShapeDtypeStruct((shards, rows, hidden), bf16),
            jax.ShapeDtypeStruct((depth, rows), bf16),
            jax.ShapeDtypeStruct((16, depth), f32),
        ],
        scratch_shapes=[
            pltpu.VMEM((shards, chips, mixer_rows, depth), bf16),
            pltpu.VMEM((shards, chips, hidden_rows, hidden), bf16),
            pltpu.VMEM((shards, chips, output_rows, depth), bf16),
            pltpu.SemaphoreType.DMA((shards, PLANE)),
            pltpu.SemaphoreType.DMA((shards, PLANE)),
            pltpu.SemaphoreType.DMA((shards, PLANE)),
        ],
        compiler_params=pltpu.CompilerParams(vmem_limit_bytes=36 << 20),
        cost_estimate=cost(15),
        name="ffn_down",
    )(own, normed, inverse, acts, slopes, cotangent, *vectors, *held, *held_out)


def fold_kernel(depth, keep_ref, far_ref, mine_ref, other_ref):
    rows = (keep_ref.shape[1] - depth) // 2
    for s, out in enumerate((mine_ref, other_ref)):
        out[:depth] = (keep_ref[s, :depth].astype(f32) + far_ref[s, :depth].astype(f32)).astype(bf16)
        small = sum(
            ref[s, depth : depth + rows].astype(f32) + ref[s, depth + rows :].astype(f32) for ref in (keep_ref, far_ref)
        )
        high = small.astype(bf16)
        out[depth : depth + rows] = high
        out[depth + rows :] = (small - high.astype(f32)).astype(bf16)


def fold(depth, keep, far):
    vmem = pl.BlockSpec(memory_space=pltpu.VMEM)
    return pl.pallas_call(
        functools.partial(fold_kernel, depth),
        in_specs=[vmem] * 2,
        out_specs=[vmem] * 2,
        out_shape=[jax.ShapeDtypeStruct(keep.shape[1:], bf16)] * 2,
        compiler_params=pltpu.CompilerParams(vmem_limit_bytes=16 << 20),
        cost_estimate=cost(2),
        name="fold",
    )(keep, far)


def join_cores_kernel(near_ref, far_ref, *outs):
    for half in range(2):
        for part in range(2):
            outs[2 * half + part][...] = (
                near_ref[half, part].astype(f32) + far_ref[half, part].astype(f32)
            ).astype(bf16)


def join_cores(near, far):
    vmem = pl.BlockSpec(memory_space=pltpu.VMEM)
    return pl.pallas_call(
        join_cores_kernel,
        in_specs=[vmem] * 2,
        out_specs=[vmem] * 4,
        out_shape=[jax.ShapeDtypeStruct(near.shape[2:], bf16)] * 4,
        compiler_params=pltpu.CompilerParams(vmem_limit_bytes=16 << 20),
        cost_estimate=cost(2),
        name="join_cores",
    )(near, far)


def finish_tokens_kernel(resid_ref, mine_ref, far_ref, out_ref, small_ref):
    depth = resid_ref.shape[1]
    rows = small_ref.shape[0]
    total = mine_ref[:depth].astype(f32) + far_ref[:depth].astype(f32)
    out_ref[...] = resid_ref[...] + total.T
    small_ref[...] = sum(
        ref[depth : depth + rows].astype(f32) + ref[depth + rows :].astype(f32) for ref in (mine_ref, far_ref)
    )


def finish_tokens(resid, mine, far):
    local, depth = resid.shape
    rows = (mine.shape[0] - depth) // 2
    vmem = pl.BlockSpec(memory_space=pltpu.VMEM)
    return pl.pallas_call(
        finish_tokens_kernel,
        in_specs=[vmem] * 3,
        out_specs=[vmem] * 2,
        out_shape=[jax.ShapeDtypeStruct(resid.shape, f32), jax.ShapeDtypeStruct((rows, local), f32)],
        compiler_params=pltpu.CompilerParams(vmem_limit_bytes=16 << 20),
        cost_estimate=cost(1),
        name="finish_tokens",
    )(resid, mine, far)


def finish_hidden_kernel(a_ref, b_ref, hidden_ref, mixer_ref):
    total = a_ref[...].astype(f32) + b_ref[...].astype(f32)
    hidden = hidden_ref.shape[1]
    hidden_ref[...] = total[:, :hidden]
    mixer_ref[...] = total[:, hidden:].T


def finish_hidden(entries, hidden):
    rows, columns = entries[0].shape
    vmem = pl.BlockSpec(memory_space=pltpu.VMEM)
    return pl.pallas_call(
        finish_hidden_kernel,
        in_specs=[vmem] * 2,
        out_specs=[vmem] * 2,
        out_shape=[
            jax.ShapeDtypeStruct((rows, hidden), f32),
            jax.ShapeDtypeStruct((columns - hidden, rows), f32),
        ],
        compiler_params=pltpu.CompilerParams(vmem_limit_bytes=60 << 20),
        cost_estimate=cost(1),
        name="finish_hidden",
    )(*entries)


def finish_qkv_kernel(a_ref, b_ref, c_ref, d_ref, query_ref, key_ref, value_ref):
    rows, width = a_ref.shape[0], query_ref.shape[1]
    low = a_ref[...].astype(f32) + b_ref[...].astype(f32)
    high = c_ref[...].astype(f32) + d_ref[...].astype(f32)
    for kind, out in enumerate((query_ref, key_ref, value_ref)):
        out[:rows] = low[:, kind * width : (kind + 1) * width]
        out[rows:] = high[:, kind * width : (kind + 1) * width]


def finish_qkv(entries):
    rows, columns = entries[0].shape
    vmem = pl.BlockSpec(memory_space=pltpu.VMEM)
    return pl.pallas_call(
        finish_qkv_kernel,
        in_specs=[vmem] * 4,
        out_specs=[vmem] * 3,
        out_shape=[jax.ShapeDtypeStruct((2 * rows, columns // 3), f32)] * 3,
        compiler_params=pltpu.CompilerParams(vmem_limit_bytes=60 << 20),
        cost_estimate=cost(1),
        name="finish_qkv",
    )(*entries)


BIAS_ROWS = (6, 7, 12)


def swap(values, mask):
    size = lax.axis_size("dp")
    return lax.ppermute(values, "dp", [(i, i ^ mask) for i in range(size)])


def cross(values, mask):
    size = lax.axis_size("tensor")
    return lax.ppermute(values, "tensor", [(i, i ^ mask) for i in range(size)])


def after(values, *others):
    return lax.optimization_barrier((values, others))[0]


def spread_shards(payload):
    return [payload] + [cross(payload, s) for s in range(1, lax.axis_size("tensor"))]


def spread_plane(parts, before=(), between=()):
    stack = after(jnp.stack(parts), *before)
    over_x, over_y = after((swap(stack, 2), swap(stack, 4)), *between)
    return stack, over_x, over_y, swap(over_x[:2], 4), swap(over_y[2:], 2)


def both_cores(held, before=()):
    first = after(held[:3], *before)
    return list(held) + [swap(entry, 1) for entry in first] + [swap(entry, 1) for entry in held[3:]]


def add_low(*entries):
    return sum(entry.astype(f32) for entry in entries).astype(bf16)


def sum_first(near, before=(), between=()):
    send_low, keep_low, send_high, keep_high = near
    send_low, send_high = after((send_low, send_high), *before)
    low, high = after((swap(send_low, 2), swap(send_high, 4)), *between)
    return (
        [add_low(keep_low[0], low[0]), add_low(keep_high[0], high[0])],
        [add_low(keep_low[1], low[1]), add_low(keep_high[1], high[1])],
    )


def sum_second(stay, send, between=()):
    low, high = after((swap(send[0], 4), swap(send[1], 2)), *between)
    return [add_low(stay[0], low), add_low(stay[1], high)]


def scatter_all(halves, axis):
    parts = []
    for half in range(2):
        blocks = []
        for i in range(PLANE):
            part, index = slot_place(i, half)
            blocks.append(halves[i % 2][2 * half + part][index])
        parts.append(jnp.stack(blocks, axis=1))
    whole = jnp.concatenate(parts, axis=axis)
    whole = whole.reshape(whole.shape[:1] + (-1,) + whole.shape[-1:])
    return lax.psum_scatter(whole, "dp", scatter_dimension=1, tiled=True)


def pair_shards(grads):
    return after(jnp.stack([grads[1], grads[3]]))


def join_shards(grads, pair, between=()):
    near = after(cross(pair, 1), *between)
    mine, other = add_low(grads[0], near[0]), add_low(grads[2], near[1])
    return mine, cross(other, 2)


def by_shard(halves):
    return [half[s] for half in halves for s in range(half.shape[0])]


def small_sum(values):
    size = lax.axis_size("dp")
    if size != PLANE:
        values = lax.psum(values, "dp")
    else:
        for mask in (1, 2, 4):
            values = values + swap(values, mask)
    return values


def body(
    tokens,
    lengths,
    query_weight,
    query_bias,
    key_weight,
    key_bias,
    value_weight,
    value_bias,
    feature_proj,
    mixer_weight,
    mixer_bias,
    first_gain,
    first_shift,
    hidden_weight,
    hidden_bias,
    output_weight,
    output_bias,
    second_gain,
    second_shift,
    cotangent,
):
    depth = tokens.shape[1]
    shards = lax.axis_size("tensor")
    place = lax.axis_index("tensor").astype(jnp.int32)
    plane = (lax.axis_index("dp") % PLANE).astype(jnp.int32)
    width = query_weight.shape[1]
    hidden = hidden_weight.shape[1]
    mixer_rows = mixer_weight.shape[0] // (PLANE // 2)
    own = jnp.stack([plane, place])
    slot_of = plane[None] if lax.axis_size("dp") == PLANE else jnp.zeros((1,), jnp.int32)

    def row(vector):
        return vector.reshape(1, -1)

    def blocks(turned):
        return turned.reshape(PLANE, turned.shape[0] // PLANE, turned.shape[1])

    own_xt, payload, payload_out = pack(
        own, tokens, hidden_bias.reshape(-1, 128), hidden_weight, mixer_weight, output_weight
    )
    parts = spread_shards(payload)
    weights = (query_weight.T, key_weight.T, value_weight.T)
    qkv_weight = prepare(after(weights, payload))
    xt = lax.all_gather(after(own_xt, qkv_weight), "tensor", axis=0, tiled=False)
    rows = payload.shape[0] - 16
    around = spread_plane([part[:rows] for part in parts])
    parts_out = spread_shards(after(payload_out, *parts))
    around = around[:3] + after(around[3:], *parts_out)
    held = both_cores(around, around[3:])
    *saved, p0, p1, p2, p3 = attend(
        after(xt, *around),
        weights,
        [row(query_bias), row(key_bias), row(value_bias)],
        feature_proj,
        lengths,
        place[None],
    )
    around_out = spread_plane(parts_out, around, (p0,))
    pieces = [p0] + [cross(p, s) for s, p in ((1, p1), (2, p2), (3, p3))]
    held_out = both_cores(around_out, pieces)
    normed, inverse, turned, mixed, acts, slopes = ffn_up(
        own, tokens, pieces, row(mixer_bias), row(first_gain), row(first_shift), parts, held, mixer_rows
    )
    acts_far, turned_far, mixed_far = swap(acts, 1), swap(turned, 1), swap(mixed, 1)
    held_out = after(held_out, turned_far, mixed_far)
    vectors = [row(v) for v in (first_gain, first_shift, output_bias, second_gain, second_shift)]
    layer_out, grad_resid, b0, b1, b2, b3, grad_ffn, grad_pre, grad_branch, sums = ffn_down(
        own, normed, inverse, acts, slopes, cotangent, vectors, held, held_out, mixer_rows
    )
    back = [b0] + [cross(b, s) for s, b in ((1, b1), (2, b2), (3, b3))]
    output_work = (blocks(grad_ffn), blocks(swap(grad_ffn, 1)), acts, acts_far)
    hidden_work = (
        blocks(turned),
        blocks(turned_far),
        grad_pre,
        swap(grad_pre, 1),
        blocks(grad_branch),
        blocks(swap(grad_branch, 1)),
        mixed,
        mixed_far,
    )
    fast = lax.axis_size("dp") == PLANE
    if fast:
        near_output = output_grad(slot_of, *output_work)
        near_output = after(near_output, hidden_work)
        near_hidden = hidden_grad(slot_of, *hidden_work)
        back = after(back, near_output, near_hidden)
    grad_qkv, send, keep = attend_back(
        saved, back, feature_proj, qkv_weight, sums, lengths, place[None]
    )
    far = cross(send, 1)
    if fast:
        even, odd = qkv_grad(slot_of, PLANE, xt, grad_qkv)
        stay_output, send_output = sum_first(near_output, between=(even,))
        stay_hidden, send_hidden = sum_first(near_hidden, between=send_output)
        near_qkv = join_cores(even, after(swap(odd, 1), send_hidden))
        mine, other = fold(depth, keep, after(far, near_qkv))
        far = cross(other, 2)
        grad_output = by_shard(sum_second(stay_output, send_output, between=(other,)))
        pair_output = pair_shards(grad_output)
        grad_hidden = by_shard(sum_second(stay_hidden, send_hidden, between=(pair_output,)))
        pair_hidden = pair_shards(grad_hidden)
        stay_qkv, send_qkv = sum_first(near_qkv, between=(pair_hidden,))
        grad_output = join_shards(grad_output, pair_output, send_qkv)
        low, high = swap(send_qkv[0], 4), swap(send_qkv[1], 2)
        grad_weights = finish_qkv([entry[0] for entry in (stay_qkv[0], low, stay_qkv[1], high)])
        grad_hidden = join_shards(grad_hidden, pair_hidden, grad_weights)
    else:
        zero, one = jnp.zeros((1,), jnp.int32), jnp.ones((1,), jnp.int32)
        mine, other = fold(depth, keep, far)
        far = cross(other, 2)
        grad_output = scatter_all([output_grad(slot, *output_work) for slot in (zero, one)], 0)
        grad_output = by_shard([0.5 * grad_output])
        grad_output = join_shards(grad_output, pair_shards(grad_output))
        grad_hidden = scatter_all([hidden_grad(slot, *hidden_work) for slot in (zero, one)], 0)
        grad_hidden = by_shard([0.5 * grad_hidden])
        grad_hidden = join_shards(grad_hidden, pair_shards(grad_hidden))
        grad_weight = scatter_all(
            [
                [entry[half, part] for half in range(2) for part in range(2)]
                for entry in qkv_grad(zero, PLANE, xt, grad_qkv)
            ],
            2,
        )[0].astype(f32)
        grad_weights = [grad_weight[:, kind * width : (kind + 1) * width] for kind in range(3)]
    tokens_grad, small = finish_tokens(grad_resid, mine, far)
    small = small_sum(small)
    small = after(small.reshape(-1, 16, small.shape[1]).transpose(1, 0, 2).reshape(16, -1))
    grad_output = sum(entry.astype(f32) for entry in grad_output).T
    grad_hidden, grad_mixer = finish_hidden(grad_hidden, hidden)
    return (
        layer_out,
        tokens_grad,
        grad_weights[0],
        small[6],
        grad_weights[1],
        small[7],
        grad_weights[2],
        small[12],
        grad_mixer,
        small[5],
        small[3],
        small[4],
        grad_hidden,
        small[8 : 8 + shards].reshape(-1),
        grad_output,
        small[2],
        small[0],
        small[1],
    )


def solution(mesh):
    placed = (
        P(("dp", "tensor"), None),
        P("dp", None),
        P(None, "tensor"),
        P("tensor"),
        P(None, "tensor"),
        P("tensor"),
        P(None, "tensor"),
        P("tensor"),
        P("tensor", None, None),
        P("tensor", None),
        P(),
        P(),
        P(),
        P(None, "tensor"),
        P("tensor"),
        P("tensor", None),
        P(),
        P(),
        P(),
        P(("dp", "tensor"), None),
    )
    return jax.shard_map(
        body,
        mesh=mesh,
        in_specs=placed,
        out_specs=(
            P(("dp", "tensor"), None),
            P(("dp", "tensor"), None),
            P("dp", "tensor"),
            P(),
            P("dp", "tensor"),
            P(),
            P("dp", "tensor"),
            P(),
            P("tensor", "dp"),
            P(),
            P(),
            P(),
            P("dp", "tensor"),
            P(),
            P("tensor", "dp"),
            P(),
            P(),
            P(),
        ),
        check_vma=False,
    )
```

time: 288 us -> 228 us (0.79)
  other arithmetic: 25.1 us -> 4.9 us
  waiting for transfers between devices: 103 us -> 86.1 us
  Pallas kernels: 67.3 us -> 53.1 us
  local copies, waits for them, and re-layouts: 18.7 us -> 9.87 us
    convert_element_type x14 -> x11, other arithmetic: 18.9 us -> 3.25 us  [add_low(): return sum((entry.astype(f32) for entry in entries)).astype(bf16)]
    ppermute x21 -> x18, waiting for transfers between devices: 56.8 us -> 46.2 us  [cross(): return lax.ppermute(values, 'tensor', [(i, i ^ mask) for i in range(size)])]
    ppermute x35 -> x40, waiting for transfers between devices: 46.3 us -> 39.9 us  [swap(): return lax.ppermute(values, 'dp', [(i, i ^ mask) for i in range(size)])]
    ppermute x35 -> x40, starting transfers between devices: 26.5 us -> 32.4 us  [swap(): return lax.ppermute(values, 'dp', [(i, i ^ mask) for i in range(size)])]
    ppermute x21 -> x18, starting transfers between devices: 31.3 us -> 26.5 us  [cross(): return lax.ppermute(values, 'tensor', [(i, i ^ mask) for i in range(size)])]
    reshape x7 -> x6, local copies, waits for them, and re-layouts: 4.75 us -> 0.02 us  [row(): return vector.reshape(1, -1)]
    pallas_call x1 -> x6, Pallas kernels: 2.9 us -> 7.59 us  [the longest x1 2.6 us: prepare(): pl.pallas_call(prepare_kernel, in_specs=[vmem] * 3, out_specs=vmem, out_s...]
    pallas_call x1, Pallas kernels: 15.6 us -> 11.2 us  [ffn_down(): pl.pallas_call(ffn_down_kernel, in_specs=[pl.BlockSpec(memory_space=pltpu...]
  transfers between devices with their start and end apart: 58 -> 59, of which waited for: 23 -> 20; matrix products, arithmetic and copies ran while one was open for 13% -> 3% of each run, Pallas kernels for 15% -> 21%
where the time goes in v1:
time: 228 us
  waiting for transfers between devices  86.1 us (38%)
  starting transfers between devices  59 us (26%)
  Pallas kernels  53.1 us (23%)
  between operations  14.8 us (6%)
  local copies, waits for them, and re-layouts  9.87 us (4%)
  other arithmetic  4.9 us (2%)
    ppermute x18, waiting for transfers between devices, cross(): return lax.ppermute(values, 'tensor', [(i, i ^ mask) for i in range(size)])  46.2 us
    ppermute x40, waiting for transfers between devices, swap(): return lax.ppermute(values, 'dp', [(i, i ^ mask) for i in range(size)])  39.9 us
    ppermute x40, starting transfers between devices, swap(): return lax.ppermute(values, 'dp', [(i, i ^ mask) for i in range(size)])  32.4 us
    ppermute x18, starting transfers between devices, cross(): return lax.ppermute(values, 'tensor', [(i, i ^ mask) for i in range(size)])  26.5 us
    pallas_call x1, Pallas kernels, ffn_down(): pl.pallas_call(ffn_down_kernel, in_specs=[pl.BlockSpec(memory_space=pltpu...  11.2 us
    pallas_call x1, Pallas kernels, attend(): pl.pallas_call(functools.partial(attend_kernel, count), grid=(heads,), in...  9.6 us
    pallas_call x1, Pallas kernels, attend_back(): pl.pallas_call(functools.partial(attend_back_kernel, count), grid=(heads,...  7.52 us
    unnamed x67, local copies, waits for them, and re-layouts  6.29 us
  transfers between devices with their start and end apart: 59, of which 20 were waited for; matrix products, arithmetic and copies ran while one was open for 3% of the time, Pallas kernels for 21%

profile of v1, /device:TPU:0, one launch (start us, length us, event | category | flops | bytes accessed | tf_op | source)
XLA Modules:
  0.0 227.8 jit_solution(15442492829586635781)
XLA Ops:
  7.8 2.7 %pack.1 = (bf16[768,256]{1,0:T(8,128)(2,1)}, bf16[256,384]{1,0:T(8,128)(2,1)}, bf16[192,384]{1,0:T(8,128)(2,1)}) custom-call(s32[2]{0:T(128)} %pad_add_fusion.own_ref, f32[6,128]{1,0:T(8,128)} %bitcast.107, bf16[256,768]{1,0:T(8,128)(2,1)} %tokens_ref.3, bf16[768,768]{1,0:T(8,128)(2,1)} %hidden_ref.1, bf16[192,768]{1,0:T(8,128)(2,1)} %mixer_ref.1, ...), custom_call_target="tpu_custom_call" | custom-call | flops 27000000512 | tf_op jit(solution)/shard_map/pack/pallas_call | solution.py:76
  10.6 5.1 %collective-permute-start.2 = (bf16[256,384]{1,0:T(8,128)(2,1)}, bf16[256,384]{1,0:T(8,128)(2,1)S(1)}, u32[]{:S(2)}, u32[]{:S(2)}) collective-permute-start(bf16[256,384]{1,0:T(8,128)(2,1)} %get-tuple-element.131.refs_10_), channel_id=1, source_target_pairs={{0,3},{1,2},{2,1},{3,0},{4,7},{5,6},{6,5},{7,4},{8,11},{9,10},{10,... | collective-permute-start | bytes 589832 | tf_op jit(solution)/shard_map/ppermute | solution.py:985
  16.3 2.6 %prepare.1.weight_ref = bf16[768,576]{1,0:T(8,128)(2,1)} custom-call(bf16[192,768]{1,0:T(8,128)(2,1)} %bitcast.99, bf16[192,768]{1,0:T(8,128)(2,1)} %bitcast.101, bf16[192,768]{1,0:T(8,128)(2,1)} %bitcast.103), custom_call_target="tpu_custom_call" | custom-call | flops 35999997952 | tf_op jit(solution)/shard_map/prepare/pallas_call | solution.py:105
  19.0 2.8 %collective-permute-done.2.refs_13_ = bf16[256,384]{1,0:T(8,128)(2,1)S(1)} collective-permute-done((bf16[256,384]{1,0:T(8,128)(2,1)}, bf16[256,384]{1,0:T(8,128)(2,1)S(1)}, u32[]{:S(2)}, u32[]{:S(2)}) %collective-permute-start.2) | collective-permute-done | bytes 196640 | tf_op jit(solution)/shard_map/ppermute | solution.py:985
  21.8 13.3 %collective-permute-done.1.refs_12_ = bf16[256,384]{1,0:T(8,128)(2,1)S(1)} collective-permute-done((bf16[256,384]{1,0:T(8,128)(2,1)}, bf16[256,384]{1,0:T(8,128)(2,1)S(1)}, u32[]{:S(2)}, u32[]{:S(2)}) %collective-permute-start.1) | collective-permute-done | bytes 196640 | tf_op jit(solution)/shard_map/ppermute | solution.py:985
  36.0 2.5 %collective-permute-start.4 = (bf16[4,240,384]{2,1,0:T(8,128)(2,1)S(1)}, bf16[4,240,384]{2,1,0:T(8,128)(2,1)S(1)}, u32[]{:S(2)}, u32[]{:S(2)}) collective-permute-start(bf16[4,240,384]{2,1,0:T(8,128)(2,1)S(1)} %pad_maximum_fusion.refs_0_), channel_id=1, source_target_pairs={{0,16},{4,20},{8,24},{12,28},{16,0},{20,4},{24,8},{28,12},{1,17},{... | collective-permute-start | bytes 2211848 | tf_op jit(solution)/shard_map/ppermute | solution.py:980
  40.1 11.2 %collective-permute-done.4.refs_2_ = bf16[4,240,384]{2,1,0:T(8,128)(2,1)S(1)} collective-permute-done((bf16[4,240,384]{2,1,0:T(8,128)(2,1)S(1)}, bf16[4,240,384]{2,1,0:T(8,128)(2,1)S(1)}, u32[]{:S(2)}, u32[]{:S(2)}) %collective-permute-start.4) | collective-permute-done | bytes 737312 | tf_op jit(solution)/shard_map/ppermute | solution.py:980
  51.3 3.5 %collective-permute-done.3.refs_1_ = bf16[4,240,384]{2,1,0:T(8,128)(2,1)S(1)} collective-permute-done((bf16[4,240,384]{2,1,0:T(8,128)(2,1)S(1)}, bf16[4,240,384]{2,1,0:T(8,128)(2,1)S(1)}, u32[]{:S(2)}, u32[]{:S(2)}) %collective-permute-start.3) | collective-permute-done | bytes 737312 | tf_op jit(solution)/shard_map/ppermute | solution.py:980
  56.9 6.6 %collective-permute-start.9 = (bf16[192,384]{1,0:T(8,128)(2,1)S(1)}, bf16[192,384]{1,0:T(8,128)(2,1)S(1)}, u32[]{:S(2)}, u32[]{:S(2)}) collective-permute-start(bf16[192,384]{1,0:T(8,128)(2,1)S(1)} %copy-done.23), channel_id=1, source_target_pairs={{0,3},{1,2},{2,1},{3,0},{4,7},{5,6},{6,5},{7,4},{8,11},{9,10},{10,... | collective-permute-start | bytes 442376 | tf_op jit(solution)/shard_map/ppermute | solution.py:985
  64.0 2.7 %collective-permute-done.9 = bf16[192,384]{1,0:T(8,128)(2,1)S(1)} collective-permute-done((bf16[192,384]{1,0:T(8,128)(2,1)S(1)}, bf16[192,384]{1,0:T(8,128)(2,1)S(1)}, u32[]{:S(2)}, u32[]{:S(2)}) %collective-permute-start.9) | collective-permute-done | bytes 147488 | tf_op jit(solution)/shard_map/ppermute | solution.py:985
  66.7 3.9 %collective-permute-done.8 = bf16[192,384]{1,0:T(8,128)(2,1)S(1)} collective-permute-done((bf16[192,384]{1,0:T(8,128)(2,1)S(1)}, bf16[192,384]{1,0:T(8,128)(2,1)S(1)}, u32[]{:S(2)}, u32[]{:S(2)}) %collective-permute-start.8) | collective-permute-done | bytes 147488 | tf_op jit(solution)/shard_map/ppermute | solution.py:985
  74.9 9.6 %attend.1 = (bf16[576,1024]{1,0:T(8,128)(2,1)}, bf16[3,256,1024]{2,1,0:T(8,128)(2,1)}, bf16[3,256,1024]{2,1,0:T(8,128)(2,1)}, bf16[3,416,256]{2,1,0:T(8,128)(2,1...) custom-call(s32[1,7]{1,0:T(1,128)} %lengths_ref.3, ...), custom_call_target="tpu_custom_call" | custom-call | flops 71999995904 | tf_op jit(solution)/shard_map/attend/pallas_call | solution.py:251
  84.5 2.2 collective-permute-done.19.refs_12_
  99.9 6.2 %ffn_up.1 = (f32[256,768]{1,0:T(8,128)S(1)}, f32[256,128]{1,0:T(8,128)S(1)}, bf16[768,256]{1,0:T(8,128)(2,1)S(1)}, bf16[4,192,256]{2,1,0:T(8,128)(2,1)S(1)}, bf1...) custom-call(s32[2]{0:T(128)S(1)} %copy-done.14, bf16[256,768]{1,0:T(8,128)(2,1)S(1)} %copy-done.4, ...), custom_call_target="tpu_custom_call" | custom-call | flops 71999995904 | tf_op jit(solution)/shard_map/ffn_up/pallas_call | solution.py:696
  111.9 11.2 %ffn_down.1 = (bf16[256,768]{1,0:T(8,128)(2,1)}, f32[256,768]{1,0:T(8,128)S(1)}, bf16[192,256]{1,0:T(8,128)(2,1)S(1)}, bf16[192,256]{1,0:T(8,128)(2,1)S(1)}, bf1...) custom-call(s32[2]{0:T(128)S(1)} %copy-done.14, ...), custom_call_target="tpu_custom_call" | custom-call | flops 134999998464 | tf_op jit(solution)/shard_map/ffn_down/pallas_call | solution.py:826
  128.2 2.4 %output_grad.1 = (bf16[2,2,96,768]{3,2,1,0:T(8,128)(2,1)S(1)}, bf16[2,2,96,768]{3,2,1,0:T(8,128)(2,1)S(1)}, bf16[2,2,96,768]{3,2,1,0:T(8,128)(2,1)S(1)}, bf16[2,2,96,768]{3,2,1,0:T(8,128)(2,1)S(1)}) custom-call(s32[1]{0:T(128)} %bitcast.own_ref, bf16[8,96,256]{2,1,0:T(8,128)(2,1)S(1)} %bitcast.88, bf16[8,96,256]{2,1,0:T(8,128)(2,1)S(1)} %bitcast.90, ...), custom_call_target="tpu_custom_call" | custom-call | flops 35999997952 | tf_op jit(solution)/shard_map/output_grad/pallas_call | solution.py:491
  134.1 4.5 %hidden_grad.1 = (bf16[2,2,96,960]{3,2,1,0:T(8,128)(2,1)S(1)}, bf16[2,2,96,960]{3,2,1,0:T(8,128)(2,1)S(1)}, bf16[2,2,96,960]{3,2,1,0:T(8,128)(2,1)S(1)}, bf16[2,2,96,960]{3,2,1,0:T(8,128)(2,1)S(1)}) custom-call(s32[1]{0:T(128)} %bitcast.own_ref, bf16[8,96,256]{2,1,0:T(8,128)(2,1)S(1)} %bitcast.85, bf16[8,96,256]{2,1,0:T(8,128)(2,1)S(1)} %bitcast.86, ...), custom_call_target="tpu_custom_call" | custom-call | flops 44999999488 | tf_op jit(solution)/shard_map/hidden_grad/pallas_call | solution.py:535
  140.5 7.5 %attend_back.1 = (bf16[576,1024]{1,0:T(8,128)(2,1)S(1)}, bf16[2,864,256]{2,1,0:T(8,128)(2,1)S(1)}, bf16[2,864,256]{2,1,0:T(8,128)(2,1)S(1)}) custom-call(s32[1,7]{1,0:T(1,128)S(1)} %copy-done.13, s32[1]{0:T(128)} %bitcast.1.place_ref, bf16[576,1024]{1,0:T(8,128)(2,1)S(1)} %copy-done.18, bf16[3,256,1024]{2,1,0:T(8,128)(2,1)S(1)} %copy-done.16, ...), custom_call_target="tpu_custom_call" | custom-call | flops 80999997440 | tf_op jit(solution)/shard_map/attend_back/pallas_call | solution.py:416
  152.2 12.7 %collective-permute-done.38 = bf16[2,2,96,960]{3,2,1,0:T(8,128)(2,1)S(1)} collective-permute-done((bf16[2,2,96,960]{3,2,1,0:T(8,128)(2,1)S(1)}, bf16[2,2,96,960]{3,2,1,0:T(8,128)(2,1)S(1)}, u32[]{:S(2)}, u32[]{:S(2)}) %collective-permute-start.38) | collective-permute-done | bytes 737312 | tf_op jit(solution)/shard_map/ppermute | solution.py:980
  168.9 2.8 %collective-permute-done.36.far_ref = bf16[2,864,256]{2,1,0:T(8,128)(2,1)S(1)} collective-permute-done((bf16[2,864,256]{2,1,0:T(8,128)(2,1)S(1)}, bf16[2,864,256]{2,1,0:T(8,128)(2,1)S(1)}, u32[]{:S(2)}, u32[]{:S(2)}) %collective-permute-start.36) | collective-permute-done | bytes 884768 | tf_op jit(solution)/shard_map/ppermute | solution.py:985
  176.8 2.8 %collective-permute-done.46 = bf16[2,96,960]{2,1,0:T(8,128)(2,1)S(1)} collective-permute-done((bf16[2,96,960]{2,1,0:T(8,128)(2,1)S(1)}, bf16[2,96,960]{2,1,0:T(8,128)(2,1)S(1)}, u32[]{:S(2)}, u32[]{:S(2)}) %collective-permute-start.46) | collective-permute-done | bytes 368672 | tf_op jit(solution)/shard_map/ppermute | solution.py:980
  186.9 9.0 %collective-permute-done.42.far_ref = bf16[864,256]{1,0:T(8,128)(2,1)S(1)} collective-permute-done((bf16[864,256]{1,0:T(8,128)(2,1)S(1)}, bf16[864,256]{1,0:T(8,128)(2,1)S(1)}, u32[]{:S(2)}, u32[]{:S(2)}) %collective-permute-start.42) | collective-permute-done | bytes 442400 | tf_op jit(solution)/shard_map/ppermute | solution.py:985
  200.9 2.7 %collective-permute-done.52 = f32[48,256]{1,0:T(8,128)S(1)} collective-permute-done((f32[48,256]{1,0:T(8,128)S(1)}, f32[48,256]{1,0:T(8,128)S(1)}, u32[]{:S(2)}, u32[]{:S(2)}) %collective-permute-start.52) | collective-permute-done | bytes 49184 | tf_op jit(solution)/shard_map/ppermute | solution.py:980
  206.1 8.2 %collective-permute-done.57 = bf16[96,768]{1,0:T(8,128)(2,1)S(1)} collective-permute-done((bf16[96,768]{1,0:T(8,128)(2,1)S(1)}, bf16[96,768]{1,0:T(8,128)(2,1)S(1)}, u32[]{:S(2)}, u32[]{:S(2)}) %collective-permute-start.57) | collective-permute-done | bytes 147488 | tf_op jit(solution)/shard_map/ppermute | solution.py:985
  (218 shorter events, 74.5 us)
Async XLA Ops:
  7.2 67.1 %all-gather.3.cloned.1.call-start = ((), (), s32[]{:S(2)}) async-start(), calls=%async_computation | async-start | bytes 1966080 | tf_op jit(solution)/shard_map/all_gather | solution.py:1107
  15.7 19.4 %collective-permute-start.1 = (bf16[256,384]{1,0:T(8,128)(2,1)}, bf16[256,384]{1,0:T(8,128)(2,1)S(1)}, u32[]{:S(2)}, u32[]{:S(2)}) collective-permute-start(bf16[256,384]{1,0:T(8,128)(2,1)} %get-tuple-element.131.refs_10_), channel_id=1, source_target_pairs={{0,2},{1,3},{2,0},{3,1},{4,6},{5,7},{6,4},{7,5},{8,10},{9,11},{10,... | collective-permute-start | bytes 589832 | tf_op jit(solution)/shard_map/ppermute | solution.py:985
  15.7 19.4 %collective-permute-start = (bf16[256,384]{1,0:T(8,128)(2,1)}, bf16[256,384]{1,0:T(8,128)(2,1)S(1)}, u32[]{:S(2)}, u32[]{:S(2)}) collective-permute-start(bf16[256,384]{1,0:T(8,128)(2,1)} %get-tuple-element.131.refs_10_), channel_id=1, source_target_pairs={{0,1},{1,0},{2,3},{3,2},{4,5},{5,4},{6,7},{7,6},{8,9},{9,8},{10,11... | collective-permute-start | bytes 589832 | tf_op jit(solution)/shard_map/ppermute | solution.py:985
  36.0 15.3 %collective-permute-start.4 = (bf16[4,240,384]{2,1,0:T(8,128)(2,1)S(1)}, bf16[4,240,384]{2,1,0:T(8,128)(2,1)S(1)}, u32[]{:S(2)}, u32[]{:S(2)}) collective-permute-start(bf16[4,240,384]{2,1,0:T(8,128)(2,1)S(1)} %pad_maximum_fusion.refs_0_), channel_id=1, source_target_pairs={{0,16},{4,20},{8,24},{12,28},{16,0},{20,4},{24,8},{28,12},{1,17},{... | collective-permute-start | bytes 2211848 | tf_op jit(solution)/shard_map/ppermute | solution.py:980
  38.4 16.4 %collective-permute-start.3 = (bf16[4,240,384]{2,1,0:T(8,128)(2,1)S(1)}, bf16[4,240,384]{2,1,0:T(8,128)(2,1)S(1)}, u32[]{:S(2)}, u32[]{:S(2)}) collective-permute-start(bf16[4,240,384]{2,1,0:T(8,128)(2,1)S(1)} %pad_maximum_fusion.refs_0_), channel_id=1, source_target_pairs={{0,8},{4,12},{8,0},{12,4},{16,24},{20,28},{24,16},{28,20},{1,9},{5... | collective-permute-start | bytes 2211848 | tf_op jit(solution)/shard_map/ppermute | solution.py:980
  54.9 15.6 %collective-permute-start.6 = (bf16[2,240,384]{2,1,0:T(8,128)(2,1)S(1)}, bf16[2,240,384]{2,1,0:T(8,128)(2,1)}, u32[]{:S(2)}, u32[]{:S(2)}) collective-permute-start(bf16[2,240,384]{2,1,0:T(8,128)(2,1)S(1)} %slice.167), channel_id=1, source_target_pairs={{0,8},{4,12},{8,0},{12,4},{16,24},{20,28},{24,16},{28,20},{1,9},{5... | collective-permute-start | bytes 1105928 | tf_op jit(solution)/shard_map/ppermute | solution.py:980
  71.2 15.5 %collective-permute-start.19 = (bf16[4,192,384]{2,1,0:T(8,128)(2,1)S(1)}, bf16[4,192,384]{2,1,0:T(8,128)(2,1)}, u32[]{:S(2)}, u32[]{:S(2)}) collective-permute-start(bf16[4,192,384]{2,1,0:T(8,128)(2,1)S(1)} %pad_maximum_fusion.1.refs_10_), channel_id=1, source_target_pairs={{0,16},{4,20},{8,24},{12,28},{16,0},{20,4},{24,8},{28,12},{1,17},{... | collective-permute-start | bytes 1769480 | tf_op jit(solution)/shard_map/ppermute | solution.py:980
  72.8 15.1 %collective-permute-start.18 = (bf16[4,192,384]{2,1,0:T(8,128)(2,1)S(1)}, bf16[4,192,384]{2,1,0:T(8,128)(2,1)}, u32[]{:S(2)}, u32[]{:S(2)}) collective-permute-start(bf16[4,192,384]{2,1,0:T(8,128)(2,1)S(1)} %pad_maximum_fusion.1.refs_10_), channel_id=1, source_target_pairs={{0,8},{4,12},{8,0},{12,4},{16,24},{20,28},{24,16},{28,20},{1,9},{5... | collective-permute-start | bytes 1769480 | tf_op jit(solution)/shard_map/ppermute | solution.py:980
  74.3 15.4 %collective-permute-start.13 = (bf16[4,240,384]{2,1,0:T(8,128)(2,1)S(1)}, bf16[4,240,384]{2,1,0:T(8,128)(2,1)}, u32[]{:S(2)}, u32[]{:S(2)}) collective-permute-start(bf16[4,240,384]{2,1,0:T(8,128)(2,1)S(1)} %pad_maximum_fusion.refs_0_), channel_id=1, source_target_pairs={{0,4},{4,0},{8,12},{12,8},{16,20},{20,16},{24,28},{28,24},{1,5},{5... | collective-permute-start | bytes 2211848 | tf_op jit(solution)/shard_map/ppermute | solution.py:980
  74.3 19.4 %collective-permute-start.14 = (bf16[4,240,384]{2,1,0:T(8,128)(2,1)S(1)}, bf16[4,240,384]{2,1,0:T(8,128)(2,1)}, u32[]{:S(2)}, u32[]{:S(2)}) collective-permute-start(bf16[4,240,384]{2,1,0:T(8,128)(2,1)S(1)} %collective-permute-done.3.refs_1_), channel_id=1, source_target_pairs={{0,4},{4,0},{8,12},{12,8},{16,20},{20,16},{24,28},{28,24},{1,5},{5... | collective-permute-start | bytes 2211848 | tf_op jit(solution)/shard_map/ppermute | solution.py:980
  74.8 20.0 %collective-permute-start.15 = (bf16[4,240,384]{2,1,0:T(8,128)(2,1)S(1)}, bf16[4,240,384]{2,1,0:T(8,128)(2,1)}, u32[]{:S(2)}, u32[]{:S(2)}) collective-permute-start(bf16[4,240,384]{2,1,0:T(8,128)(2,1)S(1)} %collective-permute-done.4.refs_2_), channel_id=1, source_target_pairs={{0,4},{4,0},{8,12},{12,8},{16,20},{20,16},{24,28},{28,24},{1,5},{5... | collective-permute-start | bytes 2211848 | tf_op jit(solution)/shard_map/ppermute | solution.py:980
  111.2 16.5 %collective-permute-start.33 = (bf16[4,256,768]{2,1,0:T(8,128)(2,1)S(1)}, bf16[4,256,768]{2,1,0:T(8,128)(2,1)S(1)}, u32[]{:S(2)}, u32[]{:S(2)}) collective-permute-start(bf16[4,256,768]{2,1,0:T(8,128)(2,1)S(1)} %get-tuple-element.152.act_ref), channel_id=1, source_target_pairs={{0,4},{4,0},{8,12},{12,8},{16,20},{20,16},{24,28},{28,24},{1,5},{5... | collective-permute-start | bytes 4718600 | tf_op jit(solution)/shard_map/ppermute | solution.py:980
  123.3 15.2 %collective-permute-start.29 = (bf16[192,256]{1,0:T(8,128)(2,1)S(1)}, bf16[192,256]{1,0:T(8,128)(2,1)S(1)}, u32[]{:S(2)}, u32[]{:S(2)}) collective-permute-start(bf16[192,256]{1,0:T(8,128)(2,1)S(1)} %get-tuple-element.181), channel_id=1, source_target_pairs={{0,1},{1,0},{2,3},{3,2},{4,5},{5,4},{6,7},{7,6},{8,9},{9,8},{10,11... | collective-permute-start | bytes 294920 | tf_op jit(solution)/shard_map/ppermute | solution.py:985
  131.8 17.9 %collective-permute-start.40 = (bf16[2,2,96,768]{3,2,1,0:T(8,128)(2,1)S(1)}, bf16[2,2,96,768]{3,2,1,0:T(8,128)(2,1)S(1)}, u32[]{:S(2)}, u32[]{:S(2)}) collective-permute-start(bf16[2,2,96,768]{3,2,1,0:T(8,128)(2,1)S(1)} %get-tuple-element.211), channel_id=1, source_target_pairs={{0,8},{4,12},{8,0},{12,4},{16,24},{20,28},{24,16},{28,20},{1,9},{5... | collective-permute-start | bytes 1769480 | tf_op jit(solution)/shard_map/ppermute | solution.py:980
  133.3 17.2 %collective-permute-start.41 = (bf16[2,2,96,768]{3,2,1,0:T(8,128)(2,1)S(1)}, bf16[2,2,96,768]{3,2,1,0:T(8,128)(2,1)S(1)}, u32[]{:S(2)}, u32[]{:S(2)}) collective-permute-start(bf16[2,2,96,768]{3,2,1,0:T(8,128)(2,1)S(1)} %get-tuple-element.212), channel_id=1, source_target_pairs={{0,16},{4,20},{8,24},{12,28},{16,0},{20,4},{24,8},{28,12},{1,17},{... | collective-permute-start | bytes 1769480 | tf_op jit(solution)/shard_map/ppermute | solution.py:980
  138.6 26.3 %collective-permute-start.38 = (bf16[2,2,96,960]{3,2,1,0:T(8,128)(2,1)S(1)}, bf16[2,2,96,960]{3,2,1,0:T(8,128)(2,1)S(1)}, u32[]{:S(2)}, u32[]{:S(2)}) collective-permute-start(bf16[2,2,96,960]{3,2,1,0:T(8,128)(2,1)S(1)} %get-tuple-element.209), channel_id=1, source_target_pairs={{0,8},{4,12},{8,0},{12,4},{16,24},{20,28},{24,16},{28,20},{1,9},{5... | collective-permute-start | bytes 2211848 | tf_op jit(solution)/shard_map/ppermute | solution.py:980
  140.0 26.4 %collective-permute-start.39 = (bf16[2,2,96,960]{3,2,1,0:T(8,128)(2,1)S(1)}, bf16[2,2,96,960]{3,2,1,0:T(8,128)(2,1)S(1)}, u32[]{:S(2)}, u32[]{:S(2)}) collective-permute-start(bf16[2,2,96,960]{3,2,1,0:T(8,128)(2,1)S(1)} %get-tuple-element.210), channel_id=1, source_target_pairs={{0,16},{4,20},{8,24},{12,28},{16,0},{20,4},{24,8},{28,12},{1,17},{... | collective-permute-start | bytes 2211848 | tf_op jit(solution)/shard_map/ppermute | solution.py:980
  149.6 17.9 %collective-permute-start.37 = (bf16[2,2,2,1,48,576]{5,4,3,2,1,0:T(8,128)(2,1)S(1)}, bf16[2,2,2,1,48,576]{5,4,3,2,1,0:T(8,128)(2,1)S(1)}, u32[]{:S(2)}, u32[]{:S(2)}) collective-permute-start(bf16[2,2,2,1,48,576]{5,4,3,2,1,0:T(8,128)(2,1)S(1)} %get-tuple-element.208), channel_id=1, source_target_pairs={{0,4},{4,0},{8,12},{12,8},{16,20},{20,16},{24,28},{28,24},{1,5},{5... | collective-permute-start | bytes 1327112 | tf_op jit(solution)/shard_map/ppermute | solution.py:980
  149.6 22.1 %collective-permute-start.36 = (bf16[2,864,256]{2,1,0:T(8,128)(2,1)S(1)}, bf16[2,864,256]{2,1,0:T(8,128)(2,1)S(1)}, u32[]{:S(2)}, u32[]{:S(2)}) collective-permute-start(bf16[2,864,256]{2,1,0:T(8,128)(2,1)S(1)} %get-tuple-element.205), channel_id=1, source_target_pairs={{0,1},{1,0},{2,3},{3,2},{4,5},{5,4},{6,7},{7,6},{8,9},{9,8},{10,11... | collective-permute-start | bytes 2654216 | tf_op jit(solution)/shard_map/ppermute | solution.py:985
  150.6 22.8 %collective-permute-start.48 = (bf16[2,96,768]{2,1,0:T(8,128)(2,1)S(1)}, bf16[2,96,768]{2,1,0:T(8,128)(2,1)S(1)}, u32[]{:S(2)}, u32[]{:S(2)}) collective-permute-start(bf16[2,96,768]{2,1,0:T(8,128)(2,1)S(1)} %fusion.9), channel_id=1, source_target_pairs={{0,8},{4,12},{8,0},{12,4},{16,24},{20,28},{24,16},{28,20},{1,9},{5... | collective-permute-start | bytes 884744 | tf_op jit(solution)/shard_map/ppermute | solution.py:980
  167.5 14.5 %collective-permute-start.45 = (bf16[2,96,960]{2,1,0:T(8,128)(2,1)S(1)}, bf16[2,96,960]{2,1,0:T(8,128)(2,1)S(1)}, u32[]{:S(2)}, u32[]{:S(2)}) collective-permute-start(bf16[2,96,960]{2,1,0:T(8,128)(2,1)S(1)} %fusion.4), channel_id=1, source_target_pairs={{0,16},{4,20},{8,24},{12,28},{16,0},{20,4},{24,8},{28,12},{1,17},{... | collective-permute-start | bytes 1105928 | tf_op jit(solution)/shard_map/ppermute | solution.py:980
  174.8 21.1 %collective-permute-start.42 = (bf16[864,256]{1,0:T(8,128)(2,1)S(1)}, bf16[864,256]{1,0:T(8,128)(2,1)S(1)}, u32[]{:S(2)}, u32[]{:S(2)}) collective-permute-start(bf16[864,256]{1,0:T(8,128)(2,1)S(1)} %get-tuple-element.224), channel_id=1, source_target_pairs={{0,2},{1,3},{2,0},{3,1},{4,6},{5,7},{6,4},{7,5},{8,10},{9,11},{10,... | collective-permute-start | bytes 1327112 | tf_op jit(solution)/shard_map/ppermute | solution.py:985
  179.6 19.8 %collective-permute-start.56 = (bf16[2,96,768]{2,1,0:T(8,128)(2,1)S(1)}, bf16[2,96,768]{2,1,0:T(8,128)(2,1)S(1)}, u32[]{:S(2)}, u32[]{:S(2)}) collective-permute-start(bf16[2,96,768]{2,1,0:T(8,128)(2,1)S(1)} %pad_maximum_fusion.3), channel_id=1, source_target_pairs={{0,1},{1,0},{2,3},{3,2},{4,5},{5,4},{6,7},{7,6},{8,9},{9,8},{10,11... | collective-permute-start | bytes 884744 | tf_op jit(solution)/shard_map/ppermute | solution.py:985
  182.5 22.5 %collective-permute-start.54 = (bf16[2,96,960]{2,1,0:T(8,128)(2,1)S(1)}, bf16[2,96,960]{2,1,0:T(8,128)(2,1)S(1)}, u32[]{:S(2)}, u32[]{:S(2)}) collective-permute-start(bf16[2,96,960]{2,1,0:T(8,128)(2,1)S(1)} %pad_maximum_fusion.2), channel_id=1, source_target_pairs={{0,1},{1,0},{2,3},{3,2},{4,5},{5,4},{6,7},{7,6},{8,9},{9,8},{10,11... | collective-permute-start | bytes 1105928 | tf_op jit(solution)/shard_map/ppermute | solution.py:985
  (68 other events, 586.6 us)
Sparse Core Ops, SparseCore 0:
  19.1 44.5 all-gather.2

commit v2 on v1

--- a/solution.py
+++ b/solution.py
@@ -35,7 +35,7 @@
 
 
 def pack_kernel(
-    own_ref, bias_ref, tokens_ref, hidden_ref, mixer_ref, output_ref, xt_ref, first_ref, second_ref, held_ref, sems
+    own_ref, bias_ref, tokens_ref, hidden_ref, mixer_ref, output_ref, first_ref, second_ref, turned_ref, held_ref, sems
 ):
     rows, columns = second_ref.shape
     chip = lax.shift_right_logical(own_ref[0], 1)
@@ -54,15 +54,15 @@
         copy(output_ref, rows, second_ref, sems.at[2]),
     ]
     fetch = pltpu.make_async_copy(tokens_ref, held_ref, sems.at[3])
+    start_all([copies])
     fetch.start()
-    start_all([copies])
     wide = jnp.concatenate([bias_ref[...], jnp.zeros((16 - bias_ref.shape[0], 128), f32)], axis=0)
     for index in range(3):
         part = wide.astype(bf16)
         wide = wide - part.astype(f32)
         first_ref[rows + mixer_rows :, index * 128 : (index + 1) * 128] = part
     fetch.wait()
-    xt_ref[...] = held_ref[...].T
+    turned_ref[...] = held_ref[...].T
     wait_all(copies)
 
 
@@ -78,9 +78,9 @@
         in_specs=[pl.BlockSpec(memory_space=pltpu.SMEM), vmem] + [pl.BlockSpec(memory_space=pltpu.HBM)] * 4,
         out_specs=[vmem] * 3,
         out_shape=[
-            jax.ShapeDtypeStruct((depth, local), bf16),
             jax.ShapeDtypeStruct((first_rows, columns), bf16),
             jax.ShapeDtypeStruct((rows, columns), bf16),
+            jax.ShapeDtypeStruct((depth, local), bf16),
         ],
         scratch_shapes=[pltpu.VMEM((local, depth), bf16), pltpu.SemaphoreType.DMA((4,))],
         compiler_params=pltpu.CompilerParams(vmem_limit_bytes=60 << 20),
@@ -107,7 +107,7 @@
         in_specs=[vmem] * 3,
         out_specs=vmem,
         out_shape=jax.ShapeDtypeStruct((depth, 3 * width), bf16),
-        compiler_params=pltpu.CompilerParams(vmem_limit_bytes=60 << 20),
+        compiler_params=pltpu.CompilerParams(vmem_limit_bytes=8 << 20),
         cost_estimate=cost(4),
         name="prepare",
     )(*weights)
@@ -156,7 +156,10 @@
     count,
     lengths_ref,
     place_ref,
-    xt_ref,
+    x0_ref,
+    x1_ref,
+    x2_ref,
+    x3_ref,
     query_weight_ref,
     key_weight_ref,
     value_weight_ref,
@@ -177,7 +180,8 @@
     mixed_ref,
 ):
     h = pl.program_id(0)
-    shards, _, local = xt_ref.shape
+    tokens = (x0_ref, x1_ref, x2_ref, x3_ref)
+    shards, local = len(tokens), x0_ref.shape[1]
     heads = pl.num_programs(0)
     width = query_weight_ref.shape[0]
     spread_rows = count * HEAD_DIM
@@ -193,8 +197,8 @@
         ):
             column = jnp.broadcast_to(bias[...], (8, width)).T[:, 0:1]
             for s in range(shards):
-                qkv_ref[kind * width : (kind + 1) * width, s * local : (s + 1) * local] = (
-                    dot(weight[...], xt_ref[s]) + column
+                qkv_ref[kind * width : (kind + 1) * width, lanes(lax.bitwise_xor(place_ref[0], s), local)] = (
+                    dot(weight[...], tokens[s][...]) + column
                 ).astype(bf16)
 
     def rows(kind):
@@ -233,8 +237,8 @@
             piece[...] = mixed_ref[:, lanes(lax.bitwise_xor(place_ref[0], s), local)]
 
 
-def attend(xt, weights, biases, proj, lengths, place):
-    shards, depth, local = xt.shape
+def attend(tokens, weights, biases, proj, lengths, place):
+    shards, local, depth = len(tokens), tokens[0].shape[1], weights[0].shape[1]
     heads, head_dim, feat = proj.shape
     total = shards * local
     count = lengths.shape[1] - 1
@@ -254,8 +258,8 @@
         in_specs=[
             smem,
             smem,
-            whole(shards, depth, local),
         ]
+        + [whole(depth, local)] * shards
         + [whole(width, depth)] * 3
         + [whole(1, width)] * 3
         + [per_head(head_dim, feat)],
@@ -278,10 +282,10 @@
         ]
         + [jax.ShapeDtypeStruct((width, local), bf16)] * shards,
         scratch_shapes=[pltpu.VMEM((width, total), bf16)],
-        compiler_params=pltpu.CompilerParams(vmem_limit_bytes=60 << 20),
+        compiler_params=pltpu.CompilerParams(vmem_limit_bytes=30 << 20),
         cost_estimate=cost(8),
         name="attend",
-    )(lengths, place, xt, *weights, *biases, proj)
+    )(lengths, place, *tokens, *weights, *biases, proj)
 
 
 def feature_back_rows(grad_feat, feat, vectors, proj_w):
@@ -554,10 +558,12 @@
     )(own, first, first_far, grad_pre, grad_pre_far, branch, branch_far, mixed, mixed_far)
 
 
-def qkv_grad_kernel(own_ref, xt_ref, grad_ref, even_ref, odd_ref, hold_ref):
-    shards, _, local = xt_ref.shape
+def qkv_grad_kernel(own_ref, place_ref, x0_ref, x1_ref, x2_ref, x3_ref, grad_ref, even_ref, odd_ref, hold_ref):
+    local = x0_ref.shape[1]
+    depth = hold_ref.shape[0] * hold_ref.shape[1]
     grads = sum(
-        dot_cols(xt_ref[d], grad_ref[:, d * local : (d + 1) * local]) for d in range(shards)
+        dot_cols(block[:depth], grad_ref[:, lanes(lax.bitwise_xor(place_ref[0], s), local)])
+        for s, block in enumerate((x0_ref, x1_ref, x2_ref, x3_ref))
     )
     hold_ref[...] = grads.astype(bf16).reshape(hold_ref.shape)
     rows = even_ref.shape[4]
@@ -568,21 +574,20 @@
             target[(half,) + slot_place(slot, half) + (0,)] = block[half * rows : (half + 1) * rows]
 
 
-def qkv_grad(own, slots, xt, grads):
-    shards, depth, local = xt.shape
+def qkv_grad(own, place, slots, depth, tokens, grads):
     count = grads.shape[0]
     vmem = pl.BlockSpec(memory_space=pltpu.VMEM)
     shape = jax.ShapeDtypeStruct((2, 2, slots // 4, 1, depth // slots // 2, count), bf16)
     return pl.pallas_call(
         qkv_grad_kernel,
-        in_specs=[pl.BlockSpec(memory_space=pltpu.SMEM), vmem, vmem],
+        in_specs=[pl.BlockSpec(memory_space=pltpu.SMEM)] * 2 + [vmem] * (len(tokens) + 1),
         out_specs=[vmem, vmem],
         out_shape=[shape, shape],
         scratch_shapes=[pltpu.VMEM((slots, depth // slots, count), bf16)],
         compiler_params=pltpu.CompilerParams(vmem_limit_bytes=16 << 20),
         cost_estimate=cost(2),
         name="qkv_grad",
-    )(own, xt, grads)
+    )(own, place, *tokens, grads)
 
 
 def norm_rows(resid):
@@ -597,19 +602,18 @@
 
 def place_copies(own, held, begin, rows, target, sems):
     columns = held[0].shape[2]
-    copies = [[] for _ in range(target.shape[0])]
-    for piece, (mask, shards) in zip(held, HELD):
+    copies = []
+    for index, (piece, (mask, shards)) in enumerate(zip(held, HELD)):
         source = lax.bitwise_xor(own, mask)
         chip = lax.shift_right_logical(source, 1)
         core = lax.bitwise_and(source, 1)
-        for index, s in enumerate(shards):
-            copies[s].append(
-                pltpu.make_async_copy(
-                    piece.at[index, pl.ds(begin, rows), :],
-                    target.at[s, chip, :, lanes(core, columns)],
-                    sems.at[s, mask],
-                )
+        copies.append(
+            pltpu.make_async_copy(
+                piece.at[:, pl.ds(begin, rows), :],
+                target.at[shards[0] : shards[-1] + 1, chip, :, lanes(core, columns)],
+                sems.at[index],
             )
+        )
     return copies
 
 
@@ -662,13 +666,12 @@
         pltpu.make_async_copy(part.at[bias_rows : bias_rows + 16], bias_ref.at[s], bias_sem.at[s])
         for s, part in enumerate(parts)
     ]
-    start_all(mixer_copies)
-    start_all(hidden_copies)
-    start_all([bias_copies])
+    start_all([mixer_copies, bias_copies, hidden_copies])
     resid = tokens_ref[...].astype(f32) + mixer_bias_ref[...]
     for s, piece in enumerate((p0_ref, p1_ref, p2_ref, p3_ref)):
         mixed_ref[s] = piece[...]
-        wait_all(mixer_copies[s])
+        if s == 0:
+            wait_all(mixer_copies)
         resid = resid + dot_rows(piece[...], mixer_ref[s].reshape(chips * mixer_rows, depth))
     normed, inverse = norm_rows(resid)
     normed_ref[...] = normed
@@ -676,7 +679,8 @@
     first_low = (normed * gain_ref[...] + shift_ref[...]).astype(bf16)
     turned_ref[...] = first_low.T
     for s in range(shards):
-        wait_all(hidden_copies[s] + [bias_copies[s]])
+        if s == 0:
+            wait_all(hidden_copies + bias_copies)
         bias = unpack_bias(bias_ref[s])
         pre = dot(first_low, hidden_ref[s].reshape(chips * hidden_rows, hidden_ref.shape[3])) + bias
         phi = 0.5 * (1.0 + lax.erf(pre * math.sqrt(0.5)))
@@ -697,7 +701,7 @@
         ffn_up_kernel,
         in_specs=[pl.BlockSpec(memory_space=pltpu.SMEM)]
         + [vmem] * (1 + shards + 3)
-        + [pl.BlockSpec(memory_space=pltpu.HBM)] * (len(HELD) + shards),
+        + [pl.BlockSpec(memory_space=pl.ANY)] * (len(HELD) + shards),
         out_specs=[vmem] * 6,
         out_shape=[
             jax.ShapeDtypeStruct((rows, depth), f32),
@@ -711,8 +715,8 @@
             pltpu.VMEM((shards, chips, mixer_rows, depth), bf16),
             pltpu.VMEM((shards, chips, hidden_rows, hidden), bf16),
             pltpu.VMEM((shards, 16, held[0].shape[2]), bf16),
-            pltpu.SemaphoreType.DMA((shards, PLANE)),
-            pltpu.SemaphoreType.DMA((shards, PLANE)),
+            pltpu.SemaphoreType.DMA((len(HELD),)),
+            pltpu.SemaphoreType.DMA((len(HELD),)),
             pltpu.SemaphoreType.DMA((shards,)),
         ],
         compiler_params=pltpu.CompilerParams(vmem_limit_bytes=28 << 20),
@@ -774,13 +778,11 @@
     output_copies = place_copies(own, held_out, 0, output_ref.shape[2], output_ref, output_sem)
     hidden_copies = place_copies(own, held, 0, hidden_rows, hidden_ref, hidden_sem)
     mixer_copies = place_copies(own, held, hidden_rows, mixer_rows, mixer_ref, mixer_sem)
-    start_all(output_copies)
-    start_all(hidden_copies)
-    start_all(mixer_copies)
+    start_all([output_copies, hidden_copies, mixer_copies])
     normed_one = normed_ref[...]
     resid = normed_one * first_gain_ref[...] + first_shift_ref[...] + output_bias_ref[...]
+    wait_all(output_copies)
     for s in range(shards):
-        wait_all(output_copies[s])
         resid = resid + dot(act_ref[s], output_ref[s].reshape(hidden, depth))
     normed, inverse = norm_rows(resid)
     layer_ref[...] = (normed * gain_ref[...] + shift_ref[...]).astype(bf16)
@@ -798,7 +800,8 @@
         ).astype(bf16)
         grad_pre_ref[s] = grad_pre
         sums_ref[pl.ds(8 + lax.bitwise_xor(place, s), 1)] = column_sum(grad_pre.astype(f32))
-        wait_all(hidden_copies[s])
+        if s == 0:
+            wait_all(hidden_copies)
         grad_first = grad_first + dot_cols(grad_pre, hidden_ref[s].reshape(depth, hidden))
     sums_ref[3:4] = column_sum(grad_first * normed_one)
     sums_ref[4:5] = column_sum(grad_first)
@@ -811,7 +814,8 @@
     sums_ref[6:8] = jnp.zeros((2, depth), f32)
     sums_ref[8 + shards :] = jnp.zeros((8 - shards, depth), f32)
     for s, back in enumerate((b0_ref, b1_ref, b2_ref, b3_ref)):
-        wait_all(mixer_copies[s])
+        if s == 0:
+            wait_all(mixer_copies)
         back[...] = dot(mixer_ref[s].reshape(chips * mixer_rows, depth), branch_turned).astype(bf16)
 
 
@@ -827,7 +831,7 @@
         ffn_down_kernel,
         in_specs=[pl.BlockSpec(memory_space=pltpu.SMEM)]
         + [vmem] * 10
-        + [pl.BlockSpec(memory_space=pltpu.HBM)] * (2 * len(HELD)),
+        + [pl.BlockSpec(memory_space=pl.ANY)] * (2 * len(HELD)),
         out_specs=[vmem] * (6 + shards),
         out_shape=[
             jax.ShapeDtypeStruct((rows, depth), bf16),
@@ -844,9 +848,9 @@
             pltpu.VMEM((shards, chips, mixer_rows, depth), bf16),
             pltpu.VMEM((shards, chips, hidden_rows, hidden), bf16),
             pltpu.VMEM((shards, chips, output_rows, depth), bf16),
-            pltpu.SemaphoreType.DMA((shards, PLANE)),
-            pltpu.SemaphoreType.DMA((shards, PLANE)),
-            pltpu.SemaphoreType.DMA((shards, PLANE)),
+            pltpu.SemaphoreType.DMA((len(HELD),)),
+            pltpu.SemaphoreType.DMA((len(HELD),)),
+            pltpu.SemaphoreType.DMA((len(HELD),)),
         ],
         compiler_params=pltpu.CompilerParams(vmem_limit_bytes=36 << 20),
         cost_estimate=cost(15),
@@ -873,7 +877,7 @@
         in_specs=[vmem] * 2,
         out_specs=[vmem] * 2,
         out_shape=[jax.ShapeDtypeStruct(keep.shape[1:], bf16)] * 2,
-        compiler_params=pltpu.CompilerParams(vmem_limit_bytes=16 << 20),
+        compiler_params=pltpu.CompilerParams(vmem_limit_bytes=8 << 20),
         cost_estimate=cost(2),
         name="fold",
     )(keep, far)
@@ -894,7 +898,7 @@
         in_specs=[vmem] * 2,
         out_specs=[vmem] * 4,
         out_shape=[jax.ShapeDtypeStruct(near.shape[2:], bf16)] * 4,
-        compiler_params=pltpu.CompilerParams(vmem_limit_bytes=16 << 20),
+        compiler_params=pltpu.CompilerParams(vmem_limit_bytes=8 << 20),
         cost_estimate=cost(2),
         name="join_cores",
     )(near, far)
@@ -919,7 +923,7 @@
         in_specs=[vmem] * 3,
         out_specs=[vmem] * 2,
         out_shape=[jax.ShapeDtypeStruct(resid.shape, f32), jax.ShapeDtypeStruct((rows, local), f32)],
-        compiler_params=pltpu.CompilerParams(vmem_limit_bytes=16 << 20),
+        compiler_params=pltpu.CompilerParams(vmem_limit_bytes=8 << 20),
         cost_estimate=cost(1),
         name="finish_tokens",
     )(resid, mine, far)
@@ -943,7 +947,7 @@
             jax.ShapeDtypeStruct((rows, hidden), f32),
             jax.ShapeDtypeStruct((columns - hidden, rows), f32),
         ],
-        compiler_params=pltpu.CompilerParams(vmem_limit_bytes=60 << 20),
+        compiler_params=pltpu.CompilerParams(vmem_limit_bytes=8 << 20),
         cost_estimate=cost(1),
         name="finish_hidden",
     )(*entries)
@@ -966,7 +970,7 @@
         in_specs=[vmem] * 4,
         out_specs=[vmem] * 3,
         out_shape=[jax.ShapeDtypeStruct((2 * rows, columns // 3), f32)] * 3,
-        compiler_params=pltpu.CompilerParams(vmem_limit_bytes=60 << 20),
+        compiler_params=pltpu.CompilerParams(vmem_limit_bytes=8 << 20),
         cost_estimate=cost(1),
         name="finish_qkv",
     )(*entries)
@@ -989,19 +993,21 @@
     return lax.optimization_barrier((values, others))[0]
 
 
-def spread_shards(payload):
-    return [payload] + [cross(payload, s) for s in range(1, lax.axis_size("tensor"))]
-
-
-def spread_plane(parts, before=(), between=()):
-    stack = after(jnp.stack(parts), *before)
+def from_neighbours(payload):
+    return cross(payload, 1), cross(payload, 2)
+
+
+def all_shards(payload, near, far):
+    return [payload, near, far, cross(far, 1)]
+
+
+def spread_plane(stack, between=()):
     over_x, over_y = after((swap(stack, 2), swap(stack, 4)), *between)
-    return stack, over_x, over_y, swap(over_x[:2], 4), swap(over_y[2:], 2)
-
-
-def both_cores(held, before=()):
-    first = after(held[:3], *before)
-    return list(held) + [swap(entry, 1) for entry in first] + [swap(entry, 1) for entry in held[3:]]
+    return [stack, over_x, over_y, swap(over_x[:2], 4), swap(over_y[2:], 2)]
+
+
+def other_core(held, before=()):
+    return [swap(entry, 1) for entry in after(held, *before)]
 
 
 def add_low(*entries):
@@ -1098,29 +1104,36 @@
     def blocks(turned):
         return turned.reshape(PLANE, turned.shape[0] // PLANE, turned.shape[1])
 
-    own_xt, payload, payload_out = pack(
+    payload, payload_out, turned = pack(
         own, tokens, hidden_bias.reshape(-1, 128), hidden_weight, mixer_weight, output_weight
     )
-    parts = spread_shards(payload)
-    weights = (query_weight.T, key_weight.T, value_weight.T)
+    near, far = from_neighbours(payload)
+    parts = all_shards(payload, near, far)
+    near_out, far_out = from_neighbours(after(payload_out, far))
+    parts_out = all_shards(payload_out, near_out, far_out)
+    near, far = from_neighbours(after(turned, parts[3]))
+    weights = [query_weight.T, key_weight.T, value_weight.T]
     qkv_weight = prepare(after(weights, payload))
-    xt = lax.all_gather(after(own_xt, qkv_weight), "tensor", axis=0, tiled=False)
     rows = payload.shape[0] - 16
-    around = spread_plane([part[:rows] for part in parts])
-    parts_out = spread_shards(after(payload_out, *parts))
-    around = around[:3] + after(around[3:], *parts_out)
-    held = both_cores(around, around[3:])
+    stack = jnp.stack([part[:rows] for part in parts])
+    stack_far = swap(stack, 1)
+    stack_out = jnp.stack(parts_out)
+    around = spread_plane(stack, between=(near, far, qkv_weight, stack_far, stack_out))
+    tokens_all = all_shards(turned, near, far)
+    crossed = [stack_far] + other_core(around[1:3])
+    tokens_all = after(tokens_all, *crossed, *around[3:])
     *saved, p0, p1, p2, p3 = attend(
-        after(xt, *around),
+        tokens_all,
         weights,
         [row(query_bias), row(key_bias), row(value_bias)],
         feature_proj,
         lengths,
         place[None],
     )
-    around_out = spread_plane(parts_out, around, (p0,))
+    around_out = spread_plane(stack_out, between=(p0,))
     pieces = [p0] + [cross(p, s) for s, p in ((1, p1), (2, p2), (3, p3))]
-    held_out = both_cores(around_out, pieces)
+    held = around + crossed + other_core(around[3:])
+    held_out = around_out + other_core(around_out[:3], pieces) + other_core(around_out[3:])
     normed, inverse, turned, mixed, acts, slopes = ffn_up(
         own, tokens, pieces, row(mixer_bias), row(first_gain), row(first_shift), parts, held, mixer_rows
     )
@@ -1153,7 +1166,7 @@
     )
     far = cross(send, 1)
     if fast:
-        even, odd = qkv_grad(slot_of, PLANE, xt, grad_qkv)
+        even, odd = qkv_grad(slot_of, place[None], PLANE, depth, tokens_all, grad_qkv)
         stay_output, send_output = sum_first(near_output, between=(even,))
         stay_hidden, send_hidden = sum_first(near_hidden, between=send_output)
         near_qkv = join_cores(even, after(swap(odd, 1), send_hidden))
@@ -1181,7 +1194,7 @@
         grad_weight = scatter_all(
             [
                 [entry[half, part] for half in range(2) for part in range(2)]
-                for entry in qkv_grad(zero, PLANE, xt, grad_qkv)
+                for entry in qkv_grad(zero, place[None], PLANE, depth, tokens_all, grad_qkv)
             ],
             2,
         )[0].astype(f32)

time: 228 us -> 202 us (0.89)
  between operations: 14.8 us -> 1.52 us
  Pallas kernels: 53.1 us -> 42.8 us
  local copies, waits for them, and re-layouts: 9.87 us -> 6.18 us
    ppermute x18 -> x21, waiting for transfers between devices: 46.2 us -> 54.5 us  [cross(): return lax.ppermute(values, 'tensor', [(i, i ^ mask) for i in range(size)])]
    ppermute x40, waiting for transfers between devices: 39.9 us -> 33.5 us  [swap(): return lax.ppermute(values, 'dp', [(i, i ^ mask) for i in range(size)])]
    pallas_call x1, Pallas kernels: 9.6 us -> 6.74 us  [attend(): pl.pallas_call(functools.partial(attend_kernel, count), grid=(heads,), in...]
    unnamed x67 -> x79, local copies, waits for them, and re-layouts: 6.29 us -> 3.61 us
    ppermute x18 -> x21, starting transfers between devices: 26.5 us -> 27.3 us  [cross(): return lax.ppermute(values, 'tensor', [(i, i ^ mask) for i in range(size)])]
  transfers between devices with their start and end apart: 59 -> 61, of which waited for: 20 -> 23; matrix products, arithmetic and copies ran while one was open for 3% -> 2% of each run, Pallas kernels for 21% -> 19%
where the time goes in v2:
time: 202 us; the launch traced here: 201 us
  waiting for transfers between devices  87.9 us (44%)
  starting transfers between devices  60 us (30%)
  Pallas kernels  42.8 us (21%)
  local copies, waits for them, and re-layouts  6.18 us (3%)
  other arithmetic  2.97 us (1%)
    ppermute x21, waiting for transfers between devices, cross(): return lax.ppermute(values, 'tensor', [(i, i ^ mask) for i in range(size)])  54.5 us
    ppermute x40, waiting for transfers between devices, swap(): return lax.ppermute(values, 'dp', [(i, i ^ mask) for i in range(size)])  33.5 us
    ppermute x40, starting transfers between devices, swap(): return lax.ppermute(values, 'dp', [(i, i ^ mask) for i in range(size)])  32.7 us
    ppermute x21, starting transfers between devices, cross(): return lax.ppermute(values, 'tensor', [(i, i ^ mask) for i in range(size)])  27.3 us
    pallas_call x1, Pallas kernels, ffn_down(): pl.pallas_call(ffn_down_kernel, in_specs=[pl.BlockSpec(memory_space=pltpu...  9.1 us
    pallas_call x1, Pallas kernels, attend_back(): pl.pallas_call(functools.partial(attend_back_kernel, count), grid=(heads,...  7.46 us
    pallas_call x1, Pallas kernels, attend(): pl.pallas_call(functools.partial(attend_kernel, count), grid=(heads,), in...  6.74 us
    pallas_call x1, Pallas kernels, ffn_up(): pl.pallas_call(ffn_up_kernel, in_specs=[pl.BlockSpec(memory_space=pltpu.S...  4.72 us
  transfers between devices with their start and end apart: 61, of which 23 were waited for; matrix products, arithmetic and copies ran while one was open for 2% of the time, Pallas kernels for 19%

profile of v2, /device:TPU:0, one launch (start us, length us, event | category | flops | bytes accessed | tf_op | source)
XLA Modules:
  0.0 201.4 jit_solution(5894456441393279279)
XLA Ops:
  1.3 2.9 %pack.1 = (bf16[256,384]{1,0:T(8,128)(2,1)}, bf16[192,384]{1,0:T(8,128)(2,1)}, bf16[768,256]{1,0:T(8,128)(2,1)}) custom-call(s32[2]{0:T(128)} %pad_add_fusion.own_ref, f32[6,128]{1,0:T(8,128)} %bitcast.107, bf16[256,768]{1,0:T(8,128)(2,1)} %tokens_ref.3, bf16[768,768]{1,0:T(8,128)(2,1)} %hidden_ref.1, bf16[192,768]{1,0:T(8,128)(2,1)} %mixer_ref.1, ...), custom_call_target="tpu_custom_call" | custom-call | flops 27000000512 | tf_op jit(solution)/shard_map/pack/pallas_call | solution.py:76
  4.2 3.1 %collective-permute-start.5 = (bf16[256,384]{1,0:T(8,128)(2,1)}, bf16[256,384]{1,0:T(8,128)(2,1)S(1)}, u32[]{:S(2)}, u32[]{:S(2)}) collective-permute-start(bf16[256,384]{1,0:T(8,128)(2,1)} %get-tuple-element.134.refs_10_), channel_id=1, source_target_pairs={{0,1},{1,0},{2,3},{3,2},{4,5},{5,4},{6,7},{7,6},{8,9},{9,8},{10,11... | collective-permute-start | bytes 589832 | tf_op jit(solution)/shard_map/ppermute | solution.py:989
  7.3 2.6 %collective-permute-start = (bf16[256,384]{1,0:T(8,128)(2,1)}, bf16[256,384]{1,0:T(8,128)(2,1)S(1)}, u32[]{:S(2)}, u32[]{:S(2)}) collective-permute-start(bf16[256,384]{1,0:T(8,128)(2,1)} %get-tuple-element.134.refs_10_), channel_id=1, source_target_pairs={{0,2},{1,3},{2,0},{3,1},{4,6},{5,7},{6,4},{7,5},{8,10},{9,11},{10,... | collective-permute-start | bytes 589832 | tf_op jit(solution)/shard_map/ppermute | solution.py:989
  10.9 8.2 %collective-permute-done.refs_12_ = bf16[256,384]{1,0:T(8,128)(2,1)S(1)} collective-permute-done((bf16[256,384]{1,0:T(8,128)(2,1)}, bf16[256,384]{1,0:T(8,128)(2,1)S(1)}, u32[]{:S(2)}, u32[]{:S(2)}) %collective-permute-start) | collective-permute-done | bytes 196640 | tf_op jit(solution)/shard_map/ppermute | solution.py:989
  19.4 2.7 %collective-permute-start.9 = (bf16[192,384]{1,0:T(8,128)(2,1)}, bf16[192,384]{1,0:T(8,128)(2,1)S(1)}, u32[]{:S(2)}, u32[]{:S(2)}) collective-permute-start(bf16[192,384]{1,0:T(8,128)(2,1)} %get-tuple-element.140), channel_id=1, source_target_pairs={{0,1},{1,0},{2,3},{3,2},{4,5},{5,4},{6,7},{7,6},{8,9},{9,8},{10,11... | collective-permute-start | bytes 442376 | tf_op jit(solution)/shard_map/ppermute | solution.py:989
  22.2 4.8 %collective-permute-done.10 = bf16[192,384]{1,0:T(8,128)(2,1)S(1)} collective-permute-done((bf16[192,384]{1,0:T(8,128)(2,1)}, bf16[192,384]{1,0:T(8,128)(2,1)S(1)}, u32[]{:S(2)}, u32[]{:S(2)}) %collective-permute-start.10) | collective-permute-done | bytes 147488 | tf_op jit(solution)/shard_map/ppermute | solution.py:989
  27.4 4.1 %collective-permute-done.1.refs_13_ = bf16[256,384]{1,0:T(8,128)(2,1)S(1)} collective-permute-done((bf16[256,384]{1,0:T(8,128)(2,1)S(1)}, bf16[256,384]{1,0:T(8,128)(2,1)S(1)}, u32[]{:S(2)}, u32[]{:S(2)}) %collective-permute-start.1) | collective-permute-done | bytes 196640 | tf_op jit(solution)/shard_map/ppermute | solution.py:989
  31.5 3.3 %collective-permute-start.3 = (bf16[768,256]{1,0:T(8,128)(2,1)}, bf16[768,256]{1,0:T(8,128)(2,1)S(1)}, u32[]{:S(2)}, u32[]{:S(2)}) collective-permute-start(bf16[768,256]{1,0:T(8,128)(2,1)} %get-tuple-element.145.x0_ref), channel_id=1, source_target_pairs={{0,2},{1,3},{2,0},{3,1},{4,6},{5,7},{6,4},{7,5},{8,10},{9,11},{10,... | collective-permute-start | bytes 1179656 | tf_op jit(solution)/shard_map/ppermute | solution.py:989
  38.7 10.0 %collective-permute-done.3.x2_ref = bf16[768,256]{1,0:T(8,128)(2,1)S(1)} collective-permute-done((bf16[768,256]{1,0:T(8,128)(2,1)}, bf16[768,256]{1,0:T(8,128)(2,1)S(1)}, u32[]{:S(2)}, u32[]{:S(2)}) %collective-permute-start.3) | collective-permute-done | bytes 393248 | tf_op jit(solution)/shard_map/ppermute | solution.py:989
  55.5 7.2 %collective-permute-done.15.refs_4_ = bf16[2,240,384]{2,1,0:T(8,128)(2,1)S(1)} collective-permute-done((bf16[2,240,384]{2,1,0:T(8,128)(2,1)S(1)}, bf16[2,240,384]{2,1,0:T(8,128)(2,1)S(1)}, u32[]{:S(2)}, u32[]{:S(2)}) %collective-permute-start.15) | collective-permute-done | bytes 368672 | tf_op jit(solution)/shard_map/ppermute | solution.py:984
  66.4 6.7 %attend.1 = (bf16[576,1024]{1,0:T(8,128)(2,1)S(1)}, bf16[3,256,1024]{2,1,0:T(8,128)(2,1)S(1)}, bf16[3,256,1024]{2,1,0:T(8,128)(2,1)S(1)}, bf16[3,416,256]{2,1,0:...) custom-call(s32[1,7]{1,0:T(1,128)S(1)} %copy-done.25, ...), custom_call_target="tpu_custom_call" | custom-call | flops 71999995904 | tf_op jit(solution)/shard_map/attend/pallas_call | solution.py:255
  74.6 2.3 %collective-permute-done.22.refs_12_ = bf16[4,192,384]{2,1,0:T(8,128)(2,1)S(1)} collective-permute-done((bf16[4,192,384]{2,1,0:T(8,128)(2,1)S(1)}, bf16[4,192,384]{2,1,0:T(8,128)(2,1)S(1)}, u32[]{:S(2)}, u32[]{:S(2)}) %collective-permute-start.22) | collective-permute-done | bytes 589856 | tf_op jit(solution)/shard_map/ppermute | solution.py:984
  82.9 2.8 %collective-permute-done.17.p2_ref = bf16[192,256]{1,0:T(8,128)(2,1)S(1)} collective-permute-done((bf16[192,256]{1,0:T(8,128)(2,1)S(1)}, bf16[192,256]{1,0:T(8,128)(2,1)S(1)}, u32[]{:S(2)}, u32[]{:S(2)}) %collective-permute-start.17) | collective-permute-done | bytes 98336 | tf_op jit(solution)/shard_map/ppermute | solution.py:989
  85.7 4.7 %ffn_up.1 = (f32[256,768]{1,0:T(8,128)S(1)}, f32[256,128]{1,0:T(8,128)S(1)}, bf16[768,256]{1,0:T(8,128)(2,1)S(1)}, bf16[4,192,256]{2,1,0:T(8,128)(2,1)S(1)}, bf1...) custom-call(s32[2]{0:T(128)S(1)} %copy-done.27, bf16[256,768]{1,0:T(8,128)(2,1)S(1)} %copy-done.1, ...), custom_call_target="tpu_custom_call" | custom-call | flops 71999995904 | tf_op jit(solution)/shard_map/ffn_up/pallas_call | solution.py:700
  97.1 9.1 %ffn_down.1 = (bf16[256,768]{1,0:T(8,128)(2,1)}, f32[256,768]{1,0:T(8,128)S(1)}, bf16[192,256]{1,0:T(8,128)(2,1)S(1)}, bf16[192,256]{1,0:T(8,128)(2,1)S(1)}, bf1...) custom-call(s32[2]{0:T(128)S(1)} %copy-done.27, ...), custom_call_target="tpu_custom_call" | custom-call | flops 134999998464 | tf_op jit(solution)/shard_map/ffn_down/pallas_call | solution.py:830
  111.4 2.4 %output_grad.1 = (bf16[2,2,96,768]{3,2,1,0:T(8,128)(2,1)S(1)}, bf16[2,2,96,768]{3,2,1,0:T(8,128)(2,1)S(1)}, bf16[2,2,96,768]{3,2,1,0:T(8,128)(2,1)S(1)}, bf16[2,2,96,768]{3,2,1,0:T(8,128)(2,1)S(1)}) custom-call(s32[1]{0:T(128)} %bitcast.own_ref, bf16[8,96,256]{2,1,0:T(8,128)(2,1)S(1)} %bitcast.85, bf16[8,96,256]{2,1,0:T(8,128)(2,1)S(1)} %bitcast.87, ...), custom_call_target="tpu_custom_call" | custom-call | flops 35999997952 | tf_op jit(solution)/shard_map/output_grad/pallas_call | solution.py:495
  117.9 4.5 %hidden_grad.1 = (bf16[2,2,96,960]{3,2,1,0:T(8,128)(2,1)S(1)}, bf16[2,2,96,960]{3,2,1,0:T(8,128)(2,1)S(1)}, bf16[2,2,96,960]{3,2,1,0:T(8,128)(2,1)S(1)}, bf16[2,2,96,960]{3,2,1,0:T(8,128)(2,1)S(1)}) custom-call(s32[1]{0:T(128)} %bitcast.own_ref, bf16[8,96,256]{2,1,0:T(8,128)(2,1)S(1)} %bitcast.82, bf16[8,96,256]{2,1,0:T(8,128)(2,1)S(1)} %bitcast.83, ...), custom_call_target="tpu_custom_call" | custom-call | flops 44999999488 | tf_op jit(solution)/shard_map/hidden_grad/pallas_call | solution.py:539
  123.6 7.5 %attend_back.1 = (bf16[576,1024]{1,0:T(8,128)(2,1)S(1)}, bf16[2,864,256]{2,1,0:T(8,128)(2,1)S(1)}, bf16[2,864,256]{2,1,0:T(8,128)(2,1)S(1)}) custom-call(s32[1,7]{1,0:T(1,128)S(1)} %copy-done.26, s32[1]{0:T(128)} %bitcast.1.place_ref, bf16[576,1024]{1,0:T(8,128)(2,1)S(1)} %copy-done.31, bf16[3,256,1024]{2,1,0:T(8,128)(2,1)S(1)} %get-tuple-element.181.qf_ref, ...), custom_call_target="tpu_custom_call" | custom-call | flops 80999997440 | tf_op jit(solution)/shard_map/attend_back/pallas_call | solution.py:420
  135.2 12.7 %collective-permute-done.41 = bf16[2,2,96,960]{3,2,1,0:T(8,128)(2,1)S(1)} collective-permute-done((bf16[2,2,96,960]{3,2,1,0:T(8,128)(2,1)S(1)}, bf16[2,2,96,960]{3,2,1,0:T(8,128)(2,1)S(1)}, u32[]{:S(2)}, u32[]{:S(2)}) %collective-permute-start.41) | collective-permute-done | bytes 737312 | tf_op jit(solution)/shard_map/ppermute | solution.py:984
  151.9 2.8 %collective-permute-done.39.far_ref = bf16[2,864,256]{2,1,0:T(8,128)(2,1)S(1)} collective-permute-done((bf16[2,864,256]{2,1,0:T(8,128)(2,1)S(1)}, bf16[2,864,256]{2,1,0:T(8,128)(2,1)S(1)}, u32[]{:S(2)}, u32[]{:S(2)}) %collective-permute-start.39) | collective-permute-done | bytes 884768 | tf_op jit(solution)/shard_map/ppermute | solution.py:989
  160.1 2.5 %collective-permute-done.49 = bf16[2,96,960]{2,1,0:T(8,128)(2,1)S(1)} collective-permute-done((bf16[2,96,960]{2,1,0:T(8,128)(2,1)S(1)}, bf16[2,96,960]{2,1,0:T(8,128)(2,1)S(1)}, u32[]{:S(2)}, u32[]{:S(2)}) %collective-permute-start.49) | collective-permute-done | bytes 368672 | tf_op jit(solution)/shard_map/ppermute | solution.py:984
  169.6 10.1 %collective-permute-done.45.far_ref = bf16[864,256]{1,0:T(8,128)(2,1)S(1)} collective-permute-done((bf16[864,256]{1,0:T(8,128)(2,1)S(1)}, bf16[864,256]{1,0:T(8,128)(2,1)S(1)}, u32[]{:S(2)}, u32[]{:S(2)}) %collective-permute-start.45) | collective-permute-done | bytes 442400 | tf_op jit(solution)/shard_map/ppermute | solution.py:989
  183.9 2.4 %collective-permute-done.55 = f32[48,256]{1,0:T(8,128)S(1)} collective-permute-done((f32[48,256]{1,0:T(8,128)S(1)}, f32[48,256]{1,0:T(8,128)S(1)}, u32[]{:S(2)}, u32[]{:S(2)}) %collective-permute-start.55) | collective-permute-done | bytes 49184 | tf_op jit(solution)/shard_map/ppermute | solution.py:984
  188.3 8.2 %collective-permute-done.60 = bf16[96,768]{1,0:T(8,128)(2,1)S(1)} collective-permute-done((bf16[96,768]{1,0:T(8,128)(2,1)S(1)}, bf16[96,768]{1,0:T(8,128)(2,1)S(1)}, u32[]{:S(2)}, u32[]{:S(2)}) %collective-permute-start.60) | collective-permute-done | bytes 147488 | tf_op jit(solution)/shard_map/ppermute | solution.py:989
  (233 shorter events, 72.3 us)
Async XLA Ops:
  4.2 17.9 %collective-permute-start.5 = (bf16[256,384]{1,0:T(8,128)(2,1)}, bf16[256,384]{1,0:T(8,128)(2,1)S(1)}, u32[]{:S(2)}, u32[]{:S(2)}) collective-permute-start(bf16[256,384]{1,0:T(8,128)(2,1)} %get-tuple-element.134.refs_10_), channel_id=1, source_target_pairs={{0,1},{1,0},{2,3},{3,2},{4,5},{5,4},{6,7},{7,6},{8,9},{9,8},{10,11... | collective-permute-start | bytes 589832 | tf_op jit(solution)/shard_map/ppermute | solution.py:989
  19.4 17.2 %collective-permute-start.9 = (bf16[192,384]{1,0:T(8,128)(2,1)}, bf16[192,384]{1,0:T(8,128)(2,1)S(1)}, u32[]{:S(2)}, u32[]{:S(2)}) collective-permute-start(bf16[192,384]{1,0:T(8,128)(2,1)} %get-tuple-element.140), channel_id=1, source_target_pairs={{0,1},{1,0},{2,3},{3,2},{4,5},{5,4},{6,7},{7,6},{8,9},{9,8},{10,11... | collective-permute-start | bytes 442376 | tf_op jit(solution)/shard_map/ppermute | solution.py:989
  31.5 17.2 %collective-permute-start.3 = (bf16[768,256]{1,0:T(8,128)(2,1)}, bf16[768,256]{1,0:T(8,128)(2,1)S(1)}, u32[]{:S(2)}, u32[]{:S(2)}) collective-permute-start(bf16[768,256]{1,0:T(8,128)(2,1)} %get-tuple-element.145.x0_ref), channel_id=1, source_target_pairs={{0,2},{1,3},{2,0},{3,1},{4,6},{5,7},{6,4},{7,5},{8,10},{9,11},{10,... | collective-permute-start | bytes 1179656 | tf_op jit(solution)/shard_map/ppermute | solution.py:989
  34.8 15.1 %collective-permute-start.2 = (bf16[768,256]{1,0:T(8,128)(2,1)}, bf16[768,256]{1,0:T(8,128)(2,1)S(1)}, u32[]{:S(2)}, u32[]{:S(2)}) collective-permute-start(bf16[768,256]{1,0:T(8,128)(2,1)} %get-tuple-element.145.x0_ref), channel_id=1, source_target_pairs={{0,1},{1,0},{2,3},{3,2},{4,5},{5,4},{6,7},{7,6},{8,9},{9,8},{10,11... | collective-permute-start | bytes 1179656 | tf_op jit(solution)/shard_map/ppermute | solution.py:989
  35.0 14.9 %collective-permute-start.8 = (bf16[4,240,384]{2,1,0:T(8,128)(2,1)S(1)}, bf16[4,240,384]{2,1,0:T(8,128)(2,1)S(1)}, u32[]{:S(2)}, u32[]{:S(2)}) collective-permute-start(bf16[4,240,384]{2,1,0:T(8,128)(2,1)S(1)} %pad_maximum_fusion.refs_0_), channel_id=1, source_target_pairs={{0,16},{4,20},{8,24},{12,28},{16,0},{20,4},{24,8},{28,12},{1,17},{... | collective-permute-start | bytes 2211848 | tf_op jit(solution)/shard_map/ppermute | solution.py:984
  50.6 15.1 %collective-permute-start.12 = (bf16[4,240,384]{2,1,0:T(8,128)(2,1)S(1)}, bf16[4,240,384]{2,1,0:T(8,128)(2,1)S(1)}, u32[]{:S(2)}, u32[]{:S(2)}) collective-permute-start(bf16[4,240,384]{2,1,0:T(8,128)(2,1)S(1)} %collective-permute-done.7.refs_1_), channel_id=1, source_target_pairs={{0,4},{4,0},{8,12},{12,8},{16,20},{20,16},{24,28},{28,24},{1,5},{5... | collective-permute-start | bytes 2211848 | tf_op jit(solution)/shard_map/ppermute | solution.py:984
  50.6 15.6 %collective-permute-start.13 = (bf16[4,240,384]{2,1,0:T(8,128)(2,1)S(1)}, bf16[4,240,384]{2,1,0:T(8,128)(2,1)S(1)}, u32[]{:S(2)}, u32[]{:S(2)}) collective-permute-start(bf16[4,240,384]{2,1,0:T(8,128)(2,1)S(1)} %collective-permute-done.8.refs_2_), channel_id=1, source_target_pairs={{0,4},{4,0},{8,12},{12,8},{16,20},{20,16},{24,28},{28,24},{1,5},{5... | collective-permute-start | bytes 2211848 | tf_op jit(solution)/shard_map/ppermute | solution.py:984
  51.2 14.6 %collective-permute-start.4 = (bf16[768,256]{1,0:T(8,128)(2,1)S(1)}, bf16[768,256]{1,0:T(8,128)(2,1)S(1)}, u32[]{:S(2)}, u32[]{:S(2)}) collective-permute-start(bf16[768,256]{1,0:T(8,128)(2,1)S(1)} %collective-permute-done.3.x2_ref), channel_id=1, source_target_pairs={{0,1},{1,0},{2,3},{3,2},{4,5},{5,4},{6,7},{7,6},{8,9},{9,8},{10,11... | collective-permute-start | bytes 1179656 | tf_op jit(solution)/shard_map/ppermute | solution.py:989
  65.7 15.0 %collective-permute-start.19 = (bf16[2,240,384]{2,1,0:T(8,128)(2,1)S(1)}, bf16[2,240,384]{2,1,0:T(8,128)(2,1)S(1)}, u32[]{:S(2)}, u32[]{:S(2)}) collective-permute-start(bf16[2,240,384]{2,1,0:T(8,128)(2,1)S(1)} %collective-permute-done.14.refs_3_), channel_id=1, source_target_pairs={{0,4},{4,0},{8,12},{12,8},{16,20},{20,16},{24,28},{28,24},{1,5},{5... | collective-permute-start | bytes 1105928 | tf_op jit(solution)/shard_map/ppermute | solution.py:984
  65.8 16.5 %collective-permute-start.20 = (bf16[2,240,384]{2,1,0:T(8,128)(2,1)S(1)}, bf16[2,240,384]{2,1,0:T(8,128)(2,1)S(1)}, u32[]{:S(2)}, u32[]{:S(2)}) collective-permute-start(bf16[2,240,384]{2,1,0:T(8,128)(2,1)S(1)} %collective-permute-done.15.refs_4_), channel_id=1, source_target_pairs={{0,4},{4,0},{8,12},{12,8},{16,20},{20,16},{24,28},{28,24},{1,5},{5... | collective-permute-start | bytes 1105928 | tf_op jit(solution)/shard_map/ppermute | solution.py:984
  96.7 14.2 %collective-permute-start.36 = (bf16[4,256,768]{2,1,0:T(8,128)(2,1)S(1)}, bf16[4,256,768]{2,1,0:T(8,128)(2,1)S(1)}, u32[]{:S(2)}, u32[]{:S(2)}) collective-permute-start(bf16[4,256,768]{2,1,0:T(8,128)(2,1)S(1)} %get-tuple-element.157.act_ref), channel_id=1, source_target_pairs={{0,4},{4,0},{8,12},{12,8},{16,20},{20,16},{24,28},{28,24},{1,5},{5... | collective-permute-start | bytes 4718600 | tf_op jit(solution)/shard_map/ppermute | solution.py:984
  106.4 15.9 %collective-permute-start.32 = (bf16[192,256]{1,0:T(8,128)(2,1)S(1)}, bf16[192,256]{1,0:T(8,128)(2,1)S(1)}, u32[]{:S(2)}, u32[]{:S(2)}) collective-permute-start(bf16[192,256]{1,0:T(8,128)(2,1)S(1)} %get-tuple-element.187), channel_id=1, source_target_pairs={{0,1},{1,0},{2,3},{3,2},{4,5},{5,4},{6,7},{7,6},{8,9},{9,8},{10,11... | collective-permute-start | bytes 294920 | tf_op jit(solution)/shard_map/ppermute | solution.py:989
  108.1 14.3 %collective-permute-start.33 = (bf16[192,256]{1,0:T(8,128)(2,1)S(1)}, bf16[192,256]{1,0:T(8,128)(2,1)S(1)}, u32[]{:S(2)}, u32[]{:S(2)}) collective-permute-start(bf16[192,256]{1,0:T(8,128)(2,1)S(1)} %get-tuple-element.188), channel_id=1, source_target_pairs={{0,2},{1,3},{2,0},{3,1},{4,6},{5,7},{6,4},{7,5},{8,10},{9,11},{10,... | collective-permute-start | bytes 294920 | tf_op jit(solution)/shard_map/ppermute | solution.py:989
  114.8 17.9 %collective-permute-start.43 = (bf16[2,2,96,768]{3,2,1,0:T(8,128)(2,1)S(1)}, bf16[2,2,96,768]{3,2,1,0:T(8,128)(2,1)S(1)}, u32[]{:S(2)}, u32[]{:S(2)}) collective-permute-start(bf16[2,2,96,768]{3,2,1,0:T(8,128)(2,1)S(1)} %get-tuple-element.217), channel_id=1, source_target_pairs={{0,8},{4,12},{8,0},{12,4},{16,24},{20,28},{24,16},{28,20},{1,9},{5... | collective-permute-start | bytes 1769480 | tf_op jit(solution)/shard_map/ppermute | solution.py:984
  116.3 17.2 %collective-permute-start.44 = (bf16[2,2,96,768]{3,2,1,0:T(8,128)(2,1)S(1)}, bf16[2,2,96,768]{3,2,1,0:T(8,128)(2,1)S(1)}, u32[]{:S(2)}, u32[]{:S(2)}) collective-permute-start(bf16[2,2,96,768]{3,2,1,0:T(8,128)(2,1)S(1)} %get-tuple-element.218), channel_id=1, source_target_pairs={{0,16},{4,20},{8,24},{12,28},{16,0},{20,4},{24,8},{28,12},{1,17},{... | collective-permute-start | bytes 1769480 | tf_op jit(solution)/shard_map/ppermute | solution.py:984
  122.4 25.5 %collective-permute-start.41 = (bf16[2,2,96,960]{3,2,1,0:T(8,128)(2,1)S(1)}, bf16[2,2,96,960]{3,2,1,0:T(8,128)(2,1)S(1)}, u32[]{:S(2)}, u32[]{:S(2)}) collective-permute-start(bf16[2,2,96,960]{3,2,1,0:T(8,128)(2,1)S(1)} %get-tuple-element.215), channel_id=1, source_target_pairs={{0,8},{4,12},{8,0},{12,4},{16,24},{20,28},{24,16},{28,20},{1,9},{5... | collective-permute-start | bytes 2211848 | tf_op jit(solution)/shard_map/ppermute | solution.py:984
  123.0 26.4 %collective-permute-start.42 = (bf16[2,2,96,960]{3,2,1,0:T(8,128)(2,1)S(1)}, bf16[2,2,96,960]{3,2,1,0:T(8,128)(2,1)S(1)}, u32[]{:S(2)}, u32[]{:S(2)}) collective-permute-start(bf16[2,2,96,960]{3,2,1,0:T(8,128)(2,1)S(1)} %get-tuple-element.216), channel_id=1, source_target_pairs={{0,16},{4,20},{8,24},{12,28},{16,0},{20,4},{24,8},{28,12},{1,17},{... | collective-permute-start | bytes 2211848 | tf_op jit(solution)/shard_map/ppermute | solution.py:984
  132.6 18.6 %collective-permute-start.40 = (bf16[2,2,2,1,48,576]{5,4,3,2,1,0:T(8,128)(2,1)S(1)}, bf16[2,2,2,1,48,576]{5,4,3,2,1,0:T(8,128)(2,1)S(1)}, u32[]{:S(2)}, u32[]{:S(2)}) collective-permute-start(bf16[2,2,2,1,48,576]{5,4,3,2,1,0:T(8,128)(2,1)S(1)} %get-tuple-element.214), channel_id=1, source_target_pairs={{0,4},{4,0},{8,12},{12,8},{16,20},{20,16},{24,28},{28,24},{1,5},{5... | collective-permute-start | bytes 1327112 | tf_op jit(solution)/shard_map/ppermute | solution.py:984
  132.7 22.1 %collective-permute-start.39 = (bf16[2,864,256]{2,1,0:T(8,128)(2,1)S(1)}, bf16[2,864,256]{2,1,0:T(8,128)(2,1)S(1)}, u32[]{:S(2)}, u32[]{:S(2)}) collective-permute-start(bf16[2,864,256]{2,1,0:T(8,128)(2,1)S(1)} %get-tuple-element.211), channel_id=1, source_target_pairs={{0,1},{1,0},{2,3},{3,2},{4,5},{5,4},{6,7},{7,6},{8,9},{9,8},{10,11... | collective-permute-start | bytes 2654216 | tf_op jit(solution)/shard_map/ppermute | solution.py:989
  133.6 22.8 %collective-permute-start.51 = (bf16[2,96,768]{2,1,0:T(8,128)(2,1)S(1)}, bf16[2,96,768]{2,1,0:T(8,128)(2,1)S(1)}, u32[]{:S(2)}, u32[]{:S(2)}) collective-permute-start(bf16[2,96,768]{2,1,0:T(8,128)(2,1)S(1)} %fusion.9), channel_id=1, source_target_pairs={{0,8},{4,12},{8,0},{12,4},{16,24},{20,28},{24,16},{28,20},{1,9},{5... | collective-permute-start | bytes 884744 | tf_op jit(solution)/shard_map/ppermute | solution.py:984
  158.0 21.6 %collective-permute-start.45 = (bf16[864,256]{1,0:T(8,128)(2,1)S(1)}, bf16[864,256]{1,0:T(8,128)(2,1)S(1)}, u32[]{:S(2)}, u32[]{:S(2)}) collective-permute-start(bf16[864,256]{1,0:T(8,128)(2,1)S(1)} %get-tuple-element.230), channel_id=1, source_target_pairs={{0,2},{1,3},{2,0},{3,1},{4,6},{5,7},{6,4},{7,5},{8,10},{9,11},{10,... | collective-permute-start | bytes 1327112 | tf_op jit(solution)/shard_map/ppermute | solution.py:989
  162.7 19.1 %collective-permute-start.59 = (bf16[2,96,768]{2,1,0:T(8,128)(2,1)S(1)}, bf16[2,96,768]{2,1,0:T(8,128)(2,1)S(1)}, u32[]{:S(2)}, u32[]{:S(2)}) collective-permute-start(bf16[2,96,768]{2,1,0:T(8,128)(2,1)S(1)} %pad_maximum_fusion.3), channel_id=1, source_target_pairs={{0,1},{1,0},{2,3},{3,2},{4,5},{5,4},{6,7},{7,6},{8,9},{9,8},{10,11... | collective-permute-start | bytes 884744 | tf_op jit(solution)/shard_map/ppermute | solution.py:989
  165.6 22.1 %collective-permute-start.57 = (bf16[2,96,960]{2,1,0:T(8,128)(2,1)S(1)}, bf16[2,96,960]{2,1,0:T(8,128)(2,1)S(1)}, u32[]{:S(2)}, u32[]{:S(2)}) collective-permute-start(bf16[2,96,960]{2,1,0:T(8,128)(2,1)S(1)} %pad_maximum_fusion.2), channel_id=1, source_target_pairs={{0,1},{1,0},{2,3},{3,2},{4,5},{5,4},{6,7},{7,6},{8,9},{9,8},{10,11... | collective-permute-start | bytes 1105928 | tf_op jit(solution)/shard_map/ppermute | solution.py:989
  166.4 14.4 %collective-permute-start.53 = (bf16[1,48,576]{2,1,0:T(8,128)(2,1)S(1)}, bf16[1,48,576]{2,1,0:T(8,128)(2,1)S(1)}, u32[]{:S(2)}, u32[]{:S(2)}) collective-permute-start(bf16[1,48,576]{2,1,0:T(8,128)(2,1)S(1)} %get-tuple-element.259), channel_id=1, source_target_pairs={{0,8},{4,12},{8,0},{12,4},{16,24},{20,28},{24,16},{28,20},{1,9},{5... | collective-permute-start | bytes 165896 | tf_op jit(solution)/shard_map/ppermute | solution.py:984
  (76 other events, 914.7 us)

commit v3 on v2

--- a/solution.py
+++ b/solution.py
@@ -107,7 +107,7 @@
         in_specs=[vmem] * 3,
         out_specs=vmem,
         out_shape=jax.ShapeDtypeStruct((depth, 3 * width), bf16),
-        compiler_params=pltpu.CompilerParams(vmem_limit_bytes=8 << 20),
+        compiler_params=pltpu.CompilerParams(vmem_limit_bytes=4 << 20),
         cost_estimate=cost(4),
         name="prepare",
     )(*weights)
@@ -282,7 +282,7 @@
         ]
         + [jax.ShapeDtypeStruct((width, local), bf16)] * shards,
         scratch_shapes=[pltpu.VMEM((width, total), bf16)],
-        compiler_params=pltpu.CompilerParams(vmem_limit_bytes=30 << 20),
+        compiler_params=pltpu.CompilerParams(vmem_limit_bytes=16 << 20),
         cost_estimate=cost(8),
         name="attend",
     )(lengths, place, *tokens, *weights, *biases, proj)
@@ -443,7 +443,7 @@
             jax.ShapeDtypeStruct((shards // 2, depth + extra, local), bf16),
         ],
         scratch_shapes=[pltpu.VMEM((width, total), bf16), pltpu.VMEM(sums.shape, f32)],
-        compiler_params=pltpu.CompilerParams(vmem_limit_bytes=28 << 20),
+        compiler_params=pltpu.CompilerParams(vmem_limit_bytes=18 << 20),
         cost_estimate=cost(9),
         name="attend_back",
     )(lengths, place, qkv, qf, kf, state, out, den, *pieces, proj, weight, sums)
@@ -498,7 +498,7 @@
         in_specs=[pl.BlockSpec(memory_space=pltpu.SMEM), whole, whole, by_shard, by_shard],
         out_specs=specs,
         out_shape=shapes,
-        compiler_params=pltpu.CompilerParams(vmem_limit_bytes=16 << 20),
+        compiler_params=pltpu.CompilerParams(vmem_limit_bytes=8 << 20),
         cost_estimate=cost(4),
         name="output_grad",
     )(own, turned, turned_far, acts, acts_far)
@@ -552,7 +552,7 @@
         ],
         out_specs=specs,
         out_shape=shapes,
-        compiler_params=pltpu.CompilerParams(vmem_limit_bytes=16 << 20),
+        compiler_params=pltpu.CompilerParams(vmem_limit_bytes=10 << 20),
         cost_estimate=cost(5),
         name="hidden_grad",
     )(own, first, first_far, grad_pre, grad_pre_far, branch, branch_far, mixed, mixed_far)
@@ -584,7 +584,7 @@
         out_specs=[vmem, vmem],
         out_shape=[shape, shape],
         scratch_shapes=[pltpu.VMEM((slots, depth // slots, count), bf16)],
-        compiler_params=pltpu.CompilerParams(vmem_limit_bytes=16 << 20),
+        compiler_params=pltpu.CompilerParams(vmem_limit_bytes=9 << 20),
         cost_estimate=cost(2),
         name="qkv_grad",
     )(own, place, *tokens, grads)
@@ -719,7 +719,7 @@
             pltpu.SemaphoreType.DMA((len(HELD),)),
             pltpu.SemaphoreType.DMA((shards,)),
         ],
-        compiler_params=pltpu.CompilerParams(vmem_limit_bytes=28 << 20),
+        compiler_params=pltpu.CompilerParams(vmem_limit_bytes=17 << 20),
         cost_estimate=cost(8),
         name="ffn_up",
     )(own, tokens, *pieces, mixer_bias, gain, shift_by, *held, *parts)
@@ -852,7 +852,7 @@
             pltpu.SemaphoreType.DMA((len(HELD),)),
             pltpu.SemaphoreType.DMA((len(HELD),)),
         ],
-        compiler_params=pltpu.CompilerParams(vmem_limit_bytes=36 << 20),
+        compiler_params=pltpu.CompilerParams(vmem_limit_bytes=24 << 20),
         cost_estimate=cost(15),
         name="ffn_down",
     )(own, normed, inverse, acts, slopes, cotangent, *vectors, *held, *held_out)
@@ -877,7 +877,7 @@
         in_specs=[vmem] * 2,
         out_specs=[vmem] * 2,
         out_shape=[jax.ShapeDtypeStruct(keep.shape[1:], bf16)] * 2,
-        compiler_params=pltpu.CompilerParams(vmem_limit_bytes=8 << 20),
+        compiler_params=pltpu.CompilerParams(vmem_limit_bytes=6 << 20),
         cost_estimate=cost(2),
         name="fold",
     )(keep, far)
@@ -898,7 +898,7 @@
         in_specs=[vmem] * 2,
         out_specs=[vmem] * 4,
         out_shape=[jax.ShapeDtypeStruct(near.shape[2:], bf16)] * 4,
-        compiler_params=pltpu.CompilerParams(vmem_limit_bytes=8 << 20),
+        compiler_params=pltpu.CompilerParams(vmem_limit_bytes=4 << 20),
         cost_estimate=cost(2),
         name="join_cores",
     )(near, far)
@@ -923,7 +923,7 @@
         in_specs=[vmem] * 3,
         out_specs=[vmem] * 2,
         out_shape=[jax.ShapeDtypeStruct(resid.shape, f32), jax.ShapeDtypeStruct((rows, local), f32)],
-        compiler_params=pltpu.CompilerParams(vmem_limit_bytes=8 << 20),
+        compiler_params=pltpu.CompilerParams(vmem_limit_bytes=6 << 20),
         cost_estimate=cost(1),
         name="finish_tokens",
     )(resid, mine, far)
@@ -947,7 +947,7 @@
             jax.ShapeDtypeStruct((rows, hidden), f32),
             jax.ShapeDtypeStruct((columns - hidden, rows), f32),
         ],
-        compiler_params=pltpu.CompilerParams(vmem_limit_bytes=8 << 20),
+        compiler_params=pltpu.CompilerParams(vmem_limit_bytes=4 << 20),
         cost_estimate=cost(1),
         name="finish_hidden",
     )(*entries)
@@ -970,7 +970,7 @@
         in_specs=[vmem] * 4,
         out_specs=[vmem] * 3,
         out_shape=[jax.ShapeDtypeStruct((2 * rows, columns // 3), f32)] * 3,
-        compiler_params=pltpu.CompilerParams(vmem_limit_bytes=8 << 20),
+        compiler_params=pltpu.CompilerParams(vmem_limit_bytes=3 << 20),
         cost_estimate=cost(1),
         name="finish_qkv",
     )(*entries)

time: 202 us -> 201 us (level)
  transfers between devices with their start and end apart: 61 -> 61, of which waited for: 23 -> 23; matrix products, arithmetic and copies ran while one was open for 2% -> 2% of each run, Pallas kernels for 19% -> 20%
where the time goes in v3:
time: 201 us
  waiting for transfers between devices  88.6 us (44%)
  starting transfers between devices  60.4 us (30%)
  Pallas kernels  42.8 us (21%)
  local copies, waits for them, and re-layouts  4.26 us (2%)
  other arithmetic  2.97 us (1%)
    ppermute x21, waiting for transfers between devices, cross(): return lax.ppermute(values, 'tensor', [(i, i ^ mask) for i in range(size)])  54.2 us
    ppermute x40, waiting for transfers between devices, swap(): return lax.ppermute(values, 'dp', [(i, i ^ mask) for i in range(size)])  34.5 us
    ppermute x40, starting transfers between devices, swap(): return lax.ppermute(values, 'dp', [(i, i ^ mask) for i in range(size)])  32.9 us
    ppermute x21, starting transfers between devices, cross(): return lax.ppermute(values, 'tensor', [(i, i ^ mask) for i in range(size)])  27.5 us
    pallas_call x1, Pallas kernels, ffn_down(): pl.pallas_call(ffn_down_kernel, in_specs=[pl.BlockSpec(memory_space=pltpu...  9.1 us
    pallas_call x1, Pallas kernels, attend_back(): pl.pallas_call(functools.partial(attend_back_kernel, count), grid=(heads,...  7.51 us
    pallas_call x1, Pallas kernels, attend(): pl.pallas_call(functools.partial(attend_kernel, count), grid=(heads,), in...  6.73 us
    pallas_call x1, Pallas kernels, ffn_up(): pl.pallas_call(ffn_up_kernel, in_specs=[pl.BlockSpec(memory_space=pltpu.S...  4.73 us
  transfers between devices with their start and end apart: 61, of which 23 were waited for; matrix products, arithmetic and copies ran while one was open for 2% of the time, Pallas kernels for 20%

profile of v3, /device:TPU:0, one launch (start us, length us, event | category | flops | bytes accessed | tf_op | source)
XLA Modules:
  0.0 200.6 jit_solution(4211738189988027437)
XLA Ops:
  1.3 2.9 %pack.1 = (bf16[256,384]{1,0:T(8,128)(2,1)}, bf16[192,384]{1,0:T(8,128)(2,1)}, bf16[768,256]{1,0:T(8,128)(2,1)}) custom-call(s32[2]{0:T(128)} %pad_add_fusion.own_ref, f32[6,128]{1,0:T(8,128)} %bitcast.107, bf16[256,768]{1,0:T(8,128)(2,1)} %tokens_ref.3, bf16[768,768]{1,0:T(8,128)(2,1)} %hidden_ref.1, bf16[192,768]{1,0:T(8,128)(2,1)} %mixer_ref.1, ...), custom_call_target="tpu_custom_call" | custom-call | flops 27000000512 | tf_op jit(solution)/shard_map/pack/pallas_call | solution.py:76
  4.2 3.1 %collective-permute-start.5 = (bf16[256,384]{1,0:T(8,128)(2,1)}, bf16[256,384]{1,0:T(8,128)(2,1)S(1)}, u32[]{:S(2)}, u32[]{:S(2)}) collective-permute-start(bf16[256,384]{1,0:T(8,128)(2,1)} %get-tuple-element.134.refs_10_), channel_id=1, source_target_pairs={{0,1},{1,0},{2,3},{3,2},{4,5},{5,4},{6,7},{7,6},{8,9},{9,8},{10,11... | collective-permute-start | bytes 589832 | tf_op jit(solution)/shard_map/ppermute | solution.py:989
  7.3 2.6 %collective-permute-start = (bf16[256,384]{1,0:T(8,128)(2,1)}, bf16[256,384]{1,0:T(8,128)(2,1)S(1)}, u32[]{:S(2)}, u32[]{:S(2)}) collective-permute-start(bf16[256,384]{1,0:T(8,128)(2,1)} %get-tuple-element.134.refs_10_), channel_id=1, source_target_pairs={{0,2},{1,3},{2,0},{3,1},{4,6},{5,7},{6,4},{7,5},{8,10},{9,11},{10,... | collective-permute-start | bytes 589832 | tf_op jit(solution)/shard_map/ppermute | solution.py:989
  10.9 8.2 %collective-permute-done.refs_12_ = bf16[256,384]{1,0:T(8,128)(2,1)S(1)} collective-permute-done((bf16[256,384]{1,0:T(8,128)(2,1)}, bf16[256,384]{1,0:T(8,128)(2,1)S(1)}, u32[]{:S(2)}, u32[]{:S(2)}) %collective-permute-start) | collective-permute-done | bytes 196640 | tf_op jit(solution)/shard_map/ppermute | solution.py:989
  19.4 2.7 %collective-permute-start.9 = (bf16[192,384]{1,0:T(8,128)(2,1)}, bf16[192,384]{1,0:T(8,128)(2,1)S(1)}, u32[]{:S(2)}, u32[]{:S(2)}) collective-permute-start(bf16[192,384]{1,0:T(8,128)(2,1)} %get-tuple-element.140), channel_id=1, source_target_pairs={{0,1},{1,0},{2,3},{3,2},{4,5},{5,4},{6,7},{7,6},{8,9},{9,8},{10,11... | collective-permute-start | bytes 442376 | tf_op jit(solution)/shard_map/ppermute | solution.py:989
  22.2 4.8 %collective-permute-done.10 = bf16[192,384]{1,0:T(8,128)(2,1)S(1)} collective-permute-done((bf16[192,384]{1,0:T(8,128)(2,1)}, bf16[192,384]{1,0:T(8,128)(2,1)S(1)}, u32[]{:S(2)}, u32[]{:S(2)}) %collective-permute-start.10) | collective-permute-done | bytes 147488 | tf_op jit(solution)/shard_map/ppermute | solution.py:989
  27.4 4.1 %collective-permute-done.1.refs_13_ = bf16[256,384]{1,0:T(8,128)(2,1)S(1)} collective-permute-done((bf16[256,384]{1,0:T(8,128)(2,1)S(1)}, bf16[256,384]{1,0:T(8,128)(2,1)S(1)}, u32[]{:S(2)}, u32[]{:S(2)}) %collective-permute-start.1) | collective-permute-done | bytes 196640 | tf_op jit(solution)/shard_map/ppermute | solution.py:989
  31.5 3.3 %collective-permute-start.3 = (bf16[768,256]{1,0:T(8,128)(2,1)}, bf16[768,256]{1,0:T(8,128)(2,1)S(1)}, u32[]{:S(2)}, u32[]{:S(2)}) collective-permute-start(bf16[768,256]{1,0:T(8,128)(2,1)} %get-tuple-element.145.x0_ref), channel_id=1, source_target_pairs={{0,2},{1,3},{2,0},{3,1},{4,6},{5,7},{6,4},{7,5},{8,10},{9,11},{10,... | collective-permute-start | bytes 1179656 | tf_op jit(solution)/shard_map/ppermute | solution.py:989
  38.7 10.0 %collective-permute-done.3.x2_ref = bf16[768,256]{1,0:T(8,128)(2,1)S(1)} collective-permute-done((bf16[768,256]{1,0:T(8,128)(2,1)}, bf16[768,256]{1,0:T(8,128)(2,1)S(1)}, u32[]{:S(2)}, u32[]{:S(2)}) %collective-permute-start.3) | collective-permute-done | bytes 393248 | tf_op jit(solution)/shard_map/ppermute | solution.py:989
  55.5 7.2 %collective-permute-done.15.refs_4_ = bf16[2,240,384]{2,1,0:T(8,128)(2,1)S(1)} collective-permute-done((bf16[2,240,384]{2,1,0:T(8,128)(2,1)S(1)}, bf16[2,240,384]{2,1,0:T(8,128)(2,1)S(1)}, u32[]{:S(2)}, u32[]{:S(2)}) %collective-permute-start.15) | collective-permute-done | bytes 368672 | tf_op jit(solution)/shard_map/ppermute | solution.py:984
  66.4 6.7 %attend.1 = (bf16[576,1024]{1,0:T(8,128)(2,1)S(1)}, bf16[3,256,1024]{2,1,0:T(8,128)(2,1)S(1)}, bf16[3,256,1024]{2,1,0:T(8,128)(2,1)S(1)}, bf16[3,416,256]{2,1,0:...) custom-call(s32[1,7]{1,0:T(1,128)S(1)} %copy-done.23, ...), custom_call_target="tpu_custom_call" | custom-call | flops 71999995904 | tf_op jit(solution)/shard_map/attend/pallas_call | solution.py:255
  73.5 3.4 %collective-permute-done.22.refs_12_ = bf16[4,192,384]{2,1,0:T(8,128)(2,1)S(1)} collective-permute-done((bf16[4,192,384]{2,1,0:T(8,128)(2,1)S(1)}, bf16[4,192,384]{2,1,0:T(8,128)(2,1)S(1)}, u32[]{:S(2)}, u32[]{:S(2)}) %collective-permute-start.22) | collective-permute-done | bytes 589856 | tf_op jit(solution)/shard_map/ppermute | solution.py:984
  82.9 2.7 %collective-permute-done.17.p2_ref = bf16[192,256]{1,0:T(8,128)(2,1)S(1)} collective-permute-done((bf16[192,256]{1,0:T(8,128)(2,1)S(1)}, bf16[192,256]{1,0:T(8,128)(2,1)S(1)}, u32[]{:S(2)}, u32[]{:S(2)}) %collective-permute-start.17) | collective-permute-done | bytes 98336 | tf_op jit(solution)/shard_map/ppermute | solution.py:989
  85.7 4.7 %ffn_up.1 = (f32[256,768]{1,0:T(8,128)S(1)}, f32[256,128]{1,0:T(8,128)S(1)}, bf16[768,256]{1,0:T(8,128)(2,1)S(1)}, bf16[4,192,256]{2,1,0:T(8,128)(2,1)S(1)}, bf1...) custom-call(s32[2]{0:T(128)S(1)} %copy-done.25, bf16[256,768]{1,0:T(8,128)(2,1)S(1)} %copy-done.1, ...), custom_call_target="tpu_custom_call" | custom-call | flops 71999995904 | tf_op jit(solution)/shard_map/ffn_up/pallas_call | solution.py:700
  96.3 9.1 %ffn_down.1 = (bf16[256,768]{1,0:T(8,128)(2,1)}, f32[256,768]{1,0:T(8,128)S(1)}, bf16[192,256]{1,0:T(8,128)(2,1)S(1)}, bf16[192,256]{1,0:T(8,128)(2,1)S(1)}, bf1...) custom-call(s32[2]{0:T(128)S(1)} %copy-done.25, ...), custom_call_target="tpu_custom_call" | custom-call | flops 134999998464 | tf_op jit(solution)/shard_map/ffn_down/pallas_call | solution.py:830
  110.5 2.4 %output_grad.1 = (bf16[2,2,96,768]{3,2,1,0:T(8,128)(2,1)S(1)}, bf16[2,2,96,768]{3,2,1,0:T(8,128)(2,1)S(1)}, bf16[2,2,96,768]{3,2,1,0:T(8,128)(2,1)S(1)}, bf16[2,2,96,768]{3,2,1,0:T(8,128)(2,1)S(1)}) custom-call(s32[1]{0:T(128)} %bitcast.own_ref, bf16[8,96,256]{2,1,0:T(8,128)(2,1)S(1)} %bitcast.85, bf16[8,96,256]{2,1,0:T(8,128)(2,1)S(1)} %bitcast.87, ...), custom_call_target="tpu_custom_call" | custom-call | flops 35999997952 | tf_op jit(solution)/shard_map/output_grad/pallas_call | solution.py:495
  117.0 4.4 %hidden_grad.1 = (bf16[2,2,96,960]{3,2,1,0:T(8,128)(2,1)S(1)}, bf16[2,2,96,960]{3,2,1,0:T(8,128)(2,1)S(1)}, bf16[2,2,96,960]{3,2,1,0:T(8,128)(2,1)S(1)}, bf16[2,2,96,960]{3,2,1,0:T(8,128)(2,1)S(1)}) custom-call(s32[1]{0:T(128)} %bitcast.own_ref, bf16[8,96,256]{2,1,0:T(8,128)(2,1)S(1)} %bitcast.82, bf16[8,96,256]{2,1,0:T(8,128)(2,1)S(1)} %bitcast.83, ...), custom_call_target="tpu_custom_call" | custom-call | flops 44999999488 | tf_op jit(solution)/shard_map/hidden_grad/pallas_call | solution.py:539
  122.6 7.5 %attend_back.1 = (bf16[576,1024]{1,0:T(8,128)(2,1)S(1)}, bf16[2,864,256]{2,1,0:T(8,128)(2,1)S(1)}, bf16[2,864,256]{2,1,0:T(8,128)(2,1)S(1)}) custom-call(s32[1,7]{1,0:T(1,128)S(1)} %copy-done.24, s32[1]{0:T(128)} %bitcast.1.place_ref, bf16[576,1024]{1,0:T(8,128)(2,1)S(1)} %get-tuple-element.180.qkv_ref, bf16[3,256,1024]{2,1,0:T(8,128)(2,1)S(1)} %get-tuple-element.181.qf_ref, ...), custom_call_target="tpu_custom_call" | custom-call | flops 80999997440 | tf_op jit(solution)/shard_map/attend_back/pallas_call | solution.py:420
  134.3 12.7 %collective-permute-done.41 = bf16[2,2,96,960]{3,2,1,0:T(8,128)(2,1)S(1)} collective-permute-done((bf16[2,2,96,960]{3,2,1,0:T(8,128)(2,1)S(1)}, bf16[2,2,96,960]{3,2,1,0:T(8,128)(2,1)S(1)}, u32[]{:S(2)}, u32[]{:S(2)}) %collective-permute-start.41) | collective-permute-done | bytes 737312 | tf_op jit(solution)/shard_map/ppermute | solution.py:984
  151.1 2.7 %collective-permute-done.39.far_ref = bf16[2,864,256]{2,1,0:T(8,128)(2,1)S(1)} collective-permute-done((bf16[2,864,256]{2,1,0:T(8,128)(2,1)S(1)}, bf16[2,864,256]{2,1,0:T(8,128)(2,1)S(1)}, u32[]{:S(2)}, u32[]{:S(2)}) %collective-permute-start.39) | collective-permute-done | bytes 884768 | tf_op jit(solution)/shard_map/ppermute | solution.py:989
  159.3 2.5 %collective-permute-done.49 = bf16[2,96,960]{2,1,0:T(8,128)(2,1)S(1)} collective-permute-done((bf16[2,96,960]{2,1,0:T(8,128)(2,1)S(1)}, bf16[2,96,960]{2,1,0:T(8,128)(2,1)S(1)}, u32[]{:S(2)}, u32[]{:S(2)}) %collective-permute-start.49) | collective-permute-done | bytes 368672 | tf_op jit(solution)/shard_map/ppermute | solution.py:984
  168.7 10.1 %collective-permute-done.45.far_ref = bf16[864,256]{1,0:T(8,128)(2,1)S(1)} collective-permute-done((bf16[864,256]{1,0:T(8,128)(2,1)S(1)}, bf16[864,256]{1,0:T(8,128)(2,1)S(1)}, u32[]{:S(2)}, u32[]{:S(2)}) %collective-permute-start.45) | collective-permute-done | bytes 442400 | tf_op jit(solution)/shard_map/ppermute | solution.py:989
  183.0 2.3 %collective-permute-done.55 = f32[48,256]{1,0:T(8,128)S(1)} collective-permute-done((f32[48,256]{1,0:T(8,128)S(1)}, f32[48,256]{1,0:T(8,128)S(1)}, u32[]{:S(2)}, u32[]{:S(2)}) %collective-permute-start.55) | collective-permute-done | bytes 49184 | tf_op jit(solution)/shard_map/ppermute | solution.py:984
  187.5 8.1 %collective-permute-done.60 = bf16[96,768]{1,0:T(8,128)(2,1)S(1)} collective-permute-done((bf16[96,768]{1,0:T(8,128)(2,1)S(1)}, bf16[96,768]{1,0:T(8,128)(2,1)S(1)}, u32[]{:S(2)}, u32[]{:S(2)}) %collective-permute-start.60) | collective-permute-done | bytes 147488 | tf_op jit(solution)/shard_map/ppermute | solution.py:989
  (221 shorter events, 70.8 us)
Async XLA Ops:
  4.2 17.9 %collective-permute-start.5 = (bf16[256,384]{1,0:T(8,128)(2,1)}, bf16[256,384]{1,0:T(8,128)(2,1)S(1)}, u32[]{:S(2)}, u32[]{:S(2)}) collective-permute-start(bf16[256,384]{1,0:T(8,128)(2,1)} %get-tuple-element.134.refs_10_), channel_id=1, source_target_pairs={{0,1},{1,0},{2,3},{3,2},{4,5},{5,4},{6,7},{7,6},{8,9},{9,8},{10,11... | collective-permute-start | bytes 589832 | tf_op jit(solution)/shard_map/ppermute | solution.py:989
  19.4 17.2 %collective-permute-start.9 = (bf16[192,384]{1,0:T(8,128)(2,1)}, bf16[192,384]{1,0:T(8,128)(2,1)S(1)}, u32[]{:S(2)}, u32[]{:S(2)}) collective-permute-start(bf16[192,384]{1,0:T(8,128)(2,1)} %get-tuple-element.140), channel_id=1, source_target_pairs={{0,1},{1,0},{2,3},{3,2},{4,5},{5,4},{6,7},{7,6},{8,9},{9,8},{10,11... | collective-permute-start | bytes 442376 | tf_op jit(solution)/shard_map/ppermute | solution.py:989
  31.5 17.2 %collective-permute-start.3 = (bf16[768,256]{1,0:T(8,128)(2,1)}, bf16[768,256]{1,0:T(8,128)(2,1)S(1)}, u32[]{:S(2)}, u32[]{:S(2)}) collective-permute-start(bf16[768,256]{1,0:T(8,128)(2,1)} %get-tuple-element.145.x0_ref), channel_id=1, source_target_pairs={{0,2},{1,3},{2,0},{3,1},{4,6},{5,7},{6,4},{7,5},{8,10},{9,11},{10,... | collective-permute-start | bytes 1179656 | tf_op jit(solution)/shard_map/ppermute | solution.py:989
  34.8 15.1 %collective-permute-start.2 = (bf16[768,256]{1,0:T(8,128)(2,1)}, bf16[768,256]{1,0:T(8,128)(2,1)S(1)}, u32[]{:S(2)}, u32[]{:S(2)}) collective-permute-start(bf16[768,256]{1,0:T(8,128)(2,1)} %get-tuple-element.145.x0_ref), channel_id=1, source_target_pairs={{0,1},{1,0},{2,3},{3,2},{4,5},{5,4},{6,7},{7,6},{8,9},{9,8},{10,11... | collective-permute-start | bytes 1179656 | tf_op jit(solution)/shard_map/ppermute | solution.py:989
  35.0 14.9 %collective-permute-start.8 = (bf16[4,240,384]{2,1,0:T(8,128)(2,1)S(1)}, bf16[4,240,384]{2,1,0:T(8,128)(2,1)S(1)}, u32[]{:S(2)}, u32[]{:S(2)}) collective-permute-start(bf16[4,240,384]{2,1,0:T(8,128)(2,1)S(1)} %pad_maximum_fusion.refs_0_), channel_id=1, source_target_pairs={{0,16},{4,20},{8,24},{12,28},{16,0},{20,4},{24,8},{28,12},{1,17},{... | collective-permute-start | bytes 2211848 | tf_op jit(solution)/shard_map/ppermute | solution.py:984
  50.6 15.1 %collective-permute-start.12 = (bf16[4,240,384]{2,1,0:T(8,128)(2,1)S(1)}, bf16[4,240,384]{2,1,0:T(8,128)(2,1)S(1)}, u32[]{:S(2)}, u32[]{:S(2)}) collective-permute-start(bf16[4,240,384]{2,1,0:T(8,128)(2,1)S(1)} %collective-permute-done.7.refs_1_), channel_id=1, source_target_pairs={{0,4},{4,0},{8,12},{12,8},{16,20},{20,16},{24,28},{28,24},{1,5},{5... | collective-permute-start | bytes 2211848 | tf_op jit(solution)/shard_map/ppermute | solution.py:984
  50.6 15.6 %collective-permute-start.13 = (bf16[4,240,384]{2,1,0:T(8,128)(2,1)S(1)}, bf16[4,240,384]{2,1,0:T(8,128)(2,1)S(1)}, u32[]{:S(2)}, u32[]{:S(2)}) collective-permute-start(bf16[4,240,384]{2,1,0:T(8,128)(2,1)S(1)} %collective-permute-done.8.refs_2_), channel_id=1, source_target_pairs={{0,4},{4,0},{8,12},{12,8},{16,20},{20,16},{24,28},{28,24},{1,5},{5... | collective-permute-start | bytes 2211848 | tf_op jit(solution)/shard_map/ppermute | solution.py:984
  51.2 14.6 %collective-permute-start.4 = (bf16[768,256]{1,0:T(8,128)(2,1)S(1)}, bf16[768,256]{1,0:T(8,128)(2,1)S(1)}, u32[]{:S(2)}, u32[]{:S(2)}) collective-permute-start(bf16[768,256]{1,0:T(8,128)(2,1)S(1)} %collective-permute-done.3.x2_ref), channel_id=1, source_target_pairs={{0,1},{1,0},{2,3},{3,2},{4,5},{5,4},{6,7},{7,6},{8,9},{9,8},{10,11... | collective-permute-start | bytes 1179656 | tf_op jit(solution)/shard_map/ppermute | solution.py:989
  65.7 15.0 %collective-permute-start.19 = (bf16[2,240,384]{2,1,0:T(8,128)(2,1)S(1)}, bf16[2,240,384]{2,1,0:T(8,128)(2,1)S(1)}, u32[]{:S(2)}, u32[]{:S(2)}) collective-permute-start(bf16[2,240,384]{2,1,0:T(8,128)(2,1)S(1)} %collective-permute-done.14.refs_3_), channel_id=1, source_target_pairs={{0,4},{4,0},{8,12},{12,8},{16,20},{20,16},{24,28},{28,24},{1,5},{5... | collective-permute-start | bytes 1105928 | tf_op jit(solution)/shard_map/ppermute | solution.py:984
  65.8 16.5 %collective-permute-start.20 = (bf16[2,240,384]{2,1,0:T(8,128)(2,1)S(1)}, bf16[2,240,384]{2,1,0:T(8,128)(2,1)S(1)}, u32[]{:S(2)}, u32[]{:S(2)}) collective-permute-start(bf16[2,240,384]{2,1,0:T(8,128)(2,1)S(1)} %collective-permute-done.15.refs_4_), channel_id=1, source_target_pairs={{0,4},{4,0},{8,12},{12,8},{16,20},{20,16},{24,28},{28,24},{1,5},{5... | collective-permute-start | bytes 1105928 | tf_op jit(solution)/shard_map/ppermute | solution.py:984
  95.8 14.2 %collective-permute-start.36 = (bf16[4,256,768]{2,1,0:T(8,128)(2,1)S(1)}, bf16[4,256,768]{2,1,0:T(8,128)(2,1)S(1)}, u32[]{:S(2)}, u32[]{:S(2)}) collective-permute-start(bf16[4,256,768]{2,1,0:T(8,128)(2,1)S(1)} %get-tuple-element.157.act_ref), channel_id=1, source_target_pairs={{0,4},{4,0},{8,12},{12,8},{16,20},{20,16},{24,28},{28,24},{1,5},{5... | collective-permute-start | bytes 4718600 | tf_op jit(solution)/shard_map/ppermute | solution.py:984
  105.6 15.9 %collective-permute-start.32 = (bf16[192,256]{1,0:T(8,128)(2,1)S(1)}, bf16[192,256]{1,0:T(8,128)(2,1)S(1)}, u32[]{:S(2)}, u32[]{:S(2)}) collective-permute-start(bf16[192,256]{1,0:T(8,128)(2,1)S(1)} %get-tuple-element.187), channel_id=1, source_target_pairs={{0,1},{1,0},{2,3},{3,2},{4,5},{5,4},{6,7},{7,6},{8,9},{9,8},{10,11... | collective-permute-start | bytes 294920 | tf_op jit(solution)/shard_map/ppermute | solution.py:989
  107.2 14.3 %collective-permute-start.33 = (bf16[192,256]{1,0:T(8,128)(2,1)S(1)}, bf16[192,256]{1,0:T(8,128)(2,1)S(1)}, u32[]{:S(2)}, u32[]{:S(2)}) collective-permute-start(bf16[192,256]{1,0:T(8,128)(2,1)S(1)} %get-tuple-element.188), channel_id=1, source_target_pairs={{0,2},{1,3},{2,0},{3,1},{4,6},{5,7},{6,4},{7,5},{8,10},{9,11},{10,... | collective-permute-start | bytes 294920 | tf_op jit(solution)/shard_map/ppermute | solution.py:989
  114.0 17.8 %collective-permute-start.43 = (bf16[2,2,96,768]{3,2,1,0:T(8,128)(2,1)S(1)}, bf16[2,2,96,768]{3,2,1,0:T(8,128)(2,1)S(1)}, u32[]{:S(2)}, u32[]{:S(2)}) collective-permute-start(bf16[2,2,96,768]{3,2,1,0:T(8,128)(2,1)S(1)} %get-tuple-element.217), channel_id=1, source_target_pairs={{0,8},{4,12},{8,0},{12,4},{16,24},{20,28},{24,16},{28,20},{1,9},{5... | collective-permute-start | bytes 1769480 | tf_op jit(solution)/shard_map/ppermute | solution.py:984
  115.5 17.1 %collective-permute-start.44 = (bf16[2,2,96,768]{3,2,1,0:T(8,128)(2,1)S(1)}, bf16[2,2,96,768]{3,2,1,0:T(8,128)(2,1)S(1)}, u32[]{:S(2)}, u32[]{:S(2)}) collective-permute-start(bf16[2,2,96,768]{3,2,1,0:T(8,128)(2,1)S(1)} %get-tuple-element.218), channel_id=1, source_target_pairs={{0,16},{4,20},{8,24},{12,28},{16,0},{20,4},{24,8},{28,12},{1,17},{... | collective-permute-start | bytes 1769480 | tf_op jit(solution)/shard_map/ppermute | solution.py:984
  121.5 25.5 %collective-permute-start.41 = (bf16[2,2,96,960]{3,2,1,0:T(8,128)(2,1)S(1)}, bf16[2,2,96,960]{3,2,1,0:T(8,128)(2,1)S(1)}, u32[]{:S(2)}, u32[]{:S(2)}) collective-permute-start(bf16[2,2,96,960]{3,2,1,0:T(8,128)(2,1)S(1)} %get-tuple-element.215), channel_id=1, source_target_pairs={{0,8},{4,12},{8,0},{12,4},{16,24},{20,28},{24,16},{28,20},{1,9},{5... | collective-permute-start | bytes 2211848 | tf_op jit(solution)/shard_map/ppermute | solution.py:984
  122.1 26.5 %collective-permute-start.42 = (bf16[2,2,96,960]{3,2,1,0:T(8,128)(2,1)S(1)}, bf16[2,2,96,960]{3,2,1,0:T(8,128)(2,1)S(1)}, u32[]{:S(2)}, u32[]{:S(2)}) collective-permute-start(bf16[2,2,96,960]{3,2,1,0:T(8,128)(2,1)S(1)} %get-tuple-element.216), channel_id=1, source_target_pairs={{0,16},{4,20},{8,24},{12,28},{16,0},{20,4},{24,8},{28,12},{1,17},{... | collective-permute-start | bytes 2211848 | tf_op jit(solution)/shard_map/ppermute | solution.py:984
  131.7 18.7 %collective-permute-start.40 = (bf16[2,2,2,1,48,576]{5,4,3,2,1,0:T(8,128)(2,1)S(1)}, bf16[2,2,2,1,48,576]{5,4,3,2,1,0:T(8,128)(2,1)S(1)}, u32[]{:S(2)}, u32[]{:S(2)}) collective-permute-start(bf16[2,2,2,1,48,576]{5,4,3,2,1,0:T(8,128)(2,1)S(1)} %get-tuple-element.214), channel_id=1, source_target_pairs={{0,4},{4,0},{8,12},{12,8},{16,20},{20,16},{24,28},{28,24},{1,5},{5... | collective-permute-start | bytes 1327112 | tf_op jit(solution)/shard_map/ppermute | solution.py:984
  131.8 22.1 %collective-permute-start.39 = (bf16[2,864,256]{2,1,0:T(8,128)(2,1)S(1)}, bf16[2,864,256]{2,1,0:T(8,128)(2,1)S(1)}, u32[]{:S(2)}, u32[]{:S(2)}) collective-permute-start(bf16[2,864,256]{2,1,0:T(8,128)(2,1)S(1)} %get-tuple-element.211), channel_id=1, source_target_pairs={{0,1},{1,0},{2,3},{3,2},{4,5},{5,4},{6,7},{7,6},{8,9},{9,8},{10,11... | collective-permute-start | bytes 2654216 | tf_op jit(solution)/shard_map/ppermute | solution.py:989
  132.7 22.9 %collective-permute-start.51 = (bf16[2,96,768]{2,1,0:T(8,128)(2,1)S(1)}, bf16[2,96,768]{2,1,0:T(8,128)(2,1)S(1)}, u32[]{:S(2)}, u32[]{:S(2)}) collective-permute-start(bf16[2,96,768]{2,1,0:T(8,128)(2,1)S(1)} %fusion.9), channel_id=1, source_target_pairs={{0,8},{4,12},{8,0},{12,4},{16,24},{20,28},{24,16},{28,20},{1,9},{5... | collective-permute-start | bytes 884744 | tf_op jit(solution)/shard_map/ppermute | solution.py:984
  157.1 21.7 %collective-permute-start.45 = (bf16[864,256]{1,0:T(8,128)(2,1)S(1)}, bf16[864,256]{1,0:T(8,128)(2,1)S(1)}, u32[]{:S(2)}, u32[]{:S(2)}) collective-permute-start(bf16[864,256]{1,0:T(8,128)(2,1)S(1)} %get-tuple-element.230), channel_id=1, source_target_pairs={{0,2},{1,3},{2,0},{3,1},{4,6},{5,7},{6,4},{7,5},{8,10},{9,11},{10,... | collective-permute-start | bytes 1327112 | tf_op jit(solution)/shard_map/ppermute | solution.py:989
  161.8 19.1 %collective-permute-start.59 = (bf16[2,96,768]{2,1,0:T(8,128)(2,1)S(1)}, bf16[2,96,768]{2,1,0:T(8,128)(2,1)S(1)}, u32[]{:S(2)}, u32[]{:S(2)}) collective-permute-start(bf16[2,96,768]{2,1,0:T(8,128)(2,1)S(1)} %pad_maximum_fusion.3), channel_id=1, source_target_pairs={{0,1},{1,0},{2,3},{3,2},{4,5},{5,4},{6,7},{7,6},{8,9},{9,8},{10,11... | collective-permute-start | bytes 884744 | tf_op jit(solution)/shard_map/ppermute | solution.py:989
  164.7 22.2 %collective-permute-start.57 = (bf16[2,96,960]{2,1,0:T(8,128)(2,1)S(1)}, bf16[2,96,960]{2,1,0:T(8,128)(2,1)S(1)}, u32[]{:S(2)}, u32[]{:S(2)}) collective-permute-start(bf16[2,96,960]{2,1,0:T(8,128)(2,1)S(1)} %pad_maximum_fusion.2), channel_id=1, source_target_pairs={{0,1},{1,0},{2,3},{3,2},{4,5},{5,4},{6,7},{7,6},{8,9},{9,8},{10,11... | collective-permute-start | bytes 1105928 | tf_op jit(solution)/shard_map/ppermute | solution.py:989
  165.5 14.4 %collective-permute-start.53 = (bf16[1,48,576]{2,1,0:T(8,128)(2,1)S(1)}, bf16[1,48,576]{2,1,0:T(8,128)(2,1)S(1)}, u32[]{:S(2)}, u32[]{:S(2)}) collective-permute-start(bf16[1,48,576]{2,1,0:T(8,128)(2,1)S(1)} %get-tuple-element.259), channel_id=1, source_target_pairs={{0,8},{4,12},{8,0},{12,4},{16,24},{20,28},{24,16},{28,20},{1,9},{5... | collective-permute-start | bytes 165896 | tf_op jit(solution)/shard_map/ppermute | solution.py:984
  (70 other events, 867.4 us)

commit v4 on v3

--- a/solution.py
+++ b/solution.py
@@ -878,7 +878,7 @@
         out_specs=[vmem] * 2,
         out_shape=[jax.ShapeDtypeStruct(keep.shape[1:], bf16)] * 2,
         compiler_params=pltpu.CompilerParams(vmem_limit_bytes=6 << 20),
-        cost_estimate=cost(2),
+        cost_estimate=cost(0),
         name="fold",
     )(keep, far)
 
@@ -899,7 +899,7 @@
         out_specs=[vmem] * 4,
         out_shape=[jax.ShapeDtypeStruct(near.shape[2:], bf16)] * 4,
         compiler_params=pltpu.CompilerParams(vmem_limit_bytes=4 << 20),
-        cost_estimate=cost(2),
+        cost_estimate=cost(0),
         name="join_cores",
     )(near, far)
 
@@ -924,7 +924,7 @@
         out_specs=[vmem] * 2,
         out_shape=[jax.ShapeDtypeStruct(resid.shape, f32), jax.ShapeDtypeStruct((rows, local), f32)],
         compiler_params=pltpu.CompilerParams(vmem_limit_bytes=6 << 20),
-        cost_estimate=cost(1),
+        cost_estimate=cost(0),
         name="finish_tokens",
     )(resid, mine, far)
 
@@ -948,7 +948,7 @@
             jax.ShapeDtypeStruct((columns - hidden, rows), f32),
         ],
         compiler_params=pltpu.CompilerParams(vmem_limit_bytes=4 << 20),
-        cost_estimate=cost(1),
+        cost_estimate=cost(0),
         name="finish_hidden",
     )(*entries)
 
@@ -971,7 +971,7 @@
         out_specs=[vmem] * 3,
         out_shape=[jax.ShapeDtypeStruct((2 * rows, columns // 3), f32)] * 3,
         compiler_params=pltpu.CompilerParams(vmem_limit_bytes=3 << 20),
-        cost_estimate=cost(1),
+        cost_estimate=cost(0),
         name="finish_qkv",
     )(*entries)
 

time: 201 us -> 201 us (level)
  no operation moved by 1% of the time
where the time goes in v4:
time: 201 us
  waiting for transfers between devices  88.7 us (44%)
  starting transfers between devices  60.4 us (30%)
  Pallas kernels  42.8 us (21%)
  local copies, waits for them, and re-layouts  4.26 us (2%)
  other arithmetic  2.96 us (1%)
    ppermute x21, waiting for transfers between devices, cross(): return lax.ppermute(values, 'tensor', [(i, i ^ mask) for i in range(size)])  54.2 us
    ppermute x40, waiting for transfers between devices, swap(): return lax.ppermute(values, 'dp', [(i, i ^ mask) for i in range(size)])  34.5 us
    ppermute x40, starting transfers between devices, swap(): return lax.ppermute(values, 'dp', [(i, i ^ mask) for i in range(size)])  32.9 us
    ppermute x21, starting transfers between devices, cross(): return lax.ppermute(values, 'tensor', [(i, i ^ mask) for i in range(size)])  27.5 us
    pallas_call x1, Pallas kernels, ffn_down(): pl.pallas_call(ffn_down_kernel, in_specs=[pl.BlockSpec(memory_space=pltpu...  9.1 us
    pallas_call x1, Pallas kernels, attend_back(): pl.pallas_call(functools.partial(attend_back_kernel, count), grid=(heads,...  7.51 us
    pallas_call x1, Pallas kernels, attend(): pl.pallas_call(functools.partial(attend_kernel, count), grid=(heads,), in...  6.73 us
    pallas_call x1, Pallas kernels, ffn_up(): pl.pallas_call(ffn_up_kernel, in_specs=[pl.BlockSpec(memory_space=pltpu.S...  4.73 us
  transfers between devices with their start and end apart: 61, of which 23 were waited for; matrix products, arithmetic and copies ran while one was open for 2% of the time, Pallas kernels for 20%

profile of v4, /device:TPU:0, one launch (start us, length us, event | category | flops | bytes accessed | tf_op | source)
XLA Modules:
  0.0 200.6 jit_solution(7449428200443471042)
XLA Ops:
  1.3 2.9 %pack.1 = (bf16[256,384]{1,0:T(8,128)(2,1)}, bf16[192,384]{1,0:T(8,128)(2,1)}, bf16[768,256]{1,0:T(8,128)(2,1)}) custom-call(s32[2]{0:T(128)} %pad_add_fusion.own_ref, f32[6,128]{1,0:T(8,128)} %bitcast.107, bf16[256,768]{1,0:T(8,128)(2,1)} %tokens_ref.3, bf16[768,768]{1,0:T(8,128)(2,1)} %hidden_ref.1, bf16[192,768]{1,0:T(8,128)(2,1)} %mixer_ref.1, ...), custom_call_target="tpu_custom_call" | custom-call | flops 27000000512 | tf_op jit(solution)/shard_map/pack/pallas_call | solution.py:76
  4.2 3.1 %collective-permute-start.5 = (bf16[256,384]{1,0:T(8,128)(2,1)}, bf16[256,384]{1,0:T(8,128)(2,1)S(1)}, u32[]{:S(2)}, u32[]{:S(2)}) collective-permute-start(bf16[256,384]{1,0:T(8,128)(2,1)} %get-tuple-element.134.refs_10_), channel_id=1, source_target_pairs={{0,1},{1,0},{2,3},{3,2},{4,5},{5,4},{6,7},{7,6},{8,9},{9,8},{10,11... | collective-permute-start | bytes 589832 | tf_op jit(solution)/shard_map/ppermute | solution.py:989
  7.3 2.6 %collective-permute-start = (bf16[256,384]{1,0:T(8,128)(2,1)}, bf16[256,384]{1,0:T(8,128)(2,1)S(1)}, u32[]{:S(2)}, u32[]{:S(2)}) collective-permute-start(bf16[256,384]{1,0:T(8,128)(2,1)} %get-tuple-element.134.refs_10_), channel_id=1, source_target_pairs={{0,2},{1,3},{2,0},{3,1},{4,6},{5,7},{6,4},{7,5},{8,10},{9,11},{10,... | collective-permute-start | bytes 589832 | tf_op jit(solution)/shard_map/ppermute | solution.py:989
  10.9 8.2 %collective-permute-done.refs_12_ = bf16[256,384]{1,0:T(8,128)(2,1)S(1)} collective-permute-done((bf16[256,384]{1,0:T(8,128)(2,1)}, bf16[256,384]{1,0:T(8,128)(2,1)S(1)}, u32[]{:S(2)}, u32[]{:S(2)}) %collective-permute-start) | collective-permute-done | bytes 196640 | tf_op jit(solution)/shard_map/ppermute | solution.py:989
  19.4 2.7 %collective-permute-start.9 = (bf16[192,384]{1,0:T(8,128)(2,1)}, bf16[192,384]{1,0:T(8,128)(2,1)S(1)}, u32[]{:S(2)}, u32[]{:S(2)}) collective-permute-start(bf16[192,384]{1,0:T(8,128)(2,1)} %get-tuple-element.140), channel_id=1, source_target_pairs={{0,1},{1,0},{2,3},{3,2},{4,5},{5,4},{6,7},{7,6},{8,9},{9,8},{10,11... | collective-permute-start | bytes 442376 | tf_op jit(solution)/shard_map/ppermute | solution.py:989
  22.2 4.8 %collective-permute-done.10 = bf16[192,384]{1,0:T(8,128)(2,1)S(1)} collective-permute-done((bf16[192,384]{1,0:T(8,128)(2,1)}, bf16[192,384]{1,0:T(8,128)(2,1)S(1)}, u32[]{:S(2)}, u32[]{:S(2)}) %collective-permute-start.10) | collective-permute-done | bytes 147488 | tf_op jit(solution)/shard_map/ppermute | solution.py:989
  27.4 4.1 %collective-permute-done.1.refs_13_ = bf16[256,384]{1,0:T(8,128)(2,1)S(1)} collective-permute-done((bf16[256,384]{1,0:T(8,128)(2,1)S(1)}, bf16[256,384]{1,0:T(8,128)(2,1)S(1)}, u32[]{:S(2)}, u32[]{:S(2)}) %collective-permute-start.1) | collective-permute-done | bytes 196640 | tf_op jit(solution)/shard_map/ppermute | solution.py:989
  31.5 3.3 %collective-permute-start.3 = (bf16[768,256]{1,0:T(8,128)(2,1)}, bf16[768,256]{1,0:T(8,128)(2,1)S(1)}, u32[]{:S(2)}, u32[]{:S(2)}) collective-permute-start(bf16[768,256]{1,0:T(8,128)(2,1)} %get-tuple-element.145.x0_ref), channel_id=1, source_target_pairs={{0,2},{1,3},{2,0},{3,1},{4,6},{5,7},{6,4},{7,5},{8,10},{9,11},{10,... | collective-permute-start | bytes 1179656 | tf_op jit(solution)/shard_map/ppermute | solution.py:989
  38.7 10.0 %collective-permute-done.3.x2_ref = bf16[768,256]{1,0:T(8,128)(2,1)S(1)} collective-permute-done((bf16[768,256]{1,0:T(8,128)(2,1)}, bf16[768,256]{1,0:T(8,128)(2,1)S(1)}, u32[]{:S(2)}, u32[]{:S(2)}) %collective-permute-start.3) | collective-permute-done | bytes 393248 | tf_op jit(solution)/shard_map/ppermute | solution.py:989
  55.5 7.2 %collective-permute-done.15.refs_4_ = bf16[2,240,384]{2,1,0:T(8,128)(2,1)S(1)} collective-permute-done((bf16[2,240,384]{2,1,0:T(8,128)(2,1)S(1)}, bf16[2,240,384]{2,1,0:T(8,128)(2,1)S(1)}, u32[]{:S(2)}, u32[]{:S(2)}) %collective-permute-start.15) | collective-permute-done | bytes 368672 | tf_op jit(solution)/shard_map/ppermute | solution.py:984
  66.4 6.7 %attend.1 = (bf16[576,1024]{1,0:T(8,128)(2,1)S(1)}, bf16[3,256,1024]{2,1,0:T(8,128)(2,1)S(1)}, bf16[3,256,1024]{2,1,0:T(8,128)(2,1)S(1)}, bf16[3,416,256]{2,1,0:...) custom-call(s32[1,7]{1,0:T(1,128)S(1)} %copy-done.23, ...), custom_call_target="tpu_custom_call" | custom-call | flops 71999995904 | tf_op jit(solution)/shard_map/attend/pallas_call | solution.py:255
  73.5 3.4 %collective-permute-done.22.refs_12_ = bf16[4,192,384]{2,1,0:T(8,128)(2,1)S(1)} collective-permute-done((bf16[4,192,384]{2,1,0:T(8,128)(2,1)S(1)}, bf16[4,192,384]{2,1,0:T(8,128)(2,1)S(1)}, u32[]{:S(2)}, u32[]{:S(2)}) %collective-permute-start.22) | collective-permute-done | bytes 589856 | tf_op jit(solution)/shard_map/ppermute | solution.py:984
  82.9 2.7 %collective-permute-done.17.p2_ref = bf16[192,256]{1,0:T(8,128)(2,1)S(1)} collective-permute-done((bf16[192,256]{1,0:T(8,128)(2,1)S(1)}, bf16[192,256]{1,0:T(8,128)(2,1)S(1)}, u32[]{:S(2)}, u32[]{:S(2)}) %collective-permute-start.17) | collective-permute-done | bytes 98336 | tf_op jit(solution)/shard_map/ppermute | solution.py:989
  85.7 4.7 %ffn_up.1 = (f32[256,768]{1,0:T(8,128)S(1)}, f32[256,128]{1,0:T(8,128)S(1)}, bf16[768,256]{1,0:T(8,128)(2,1)S(1)}, bf16[4,192,256]{2,1,0:T(8,128)(2,1)S(1)}, bf1...) custom-call(s32[2]{0:T(128)S(1)} %copy-done.25, bf16[256,768]{1,0:T(8,128)(2,1)S(1)} %copy-done.1, ...), custom_call_target="tpu_custom_call" | custom-call | flops 71999995904 | tf_op jit(solution)/shard_map/ffn_up/pallas_call | solution.py:700
  96.3 9.1 %ffn_down.1 = (bf16[256,768]{1,0:T(8,128)(2,1)}, f32[256,768]{1,0:T(8,128)S(1)}, bf16[192,256]{1,0:T(8,128)(2,1)S(1)}, bf16[192,256]{1,0:T(8,128)(2,1)S(1)}, bf1...) custom-call(s32[2]{0:T(128)S(1)} %copy-done.25, ...), custom_call_target="tpu_custom_call" | custom-call | flops 134999998464 | tf_op jit(solution)/shard_map/ffn_down/pallas_call | solution.py:830
  110.5 2.4 %output_grad.1 = (bf16[2,2,96,768]{3,2,1,0:T(8,128)(2,1)S(1)}, bf16[2,2,96,768]{3,2,1,0:T(8,128)(2,1)S(1)}, bf16[2,2,96,768]{3,2,1,0:T(8,128)(2,1)S(1)}, bf16[2,2,96,768]{3,2,1,0:T(8,128)(2,1)S(1)}) custom-call(s32[1]{0:T(128)} %bitcast.own_ref, bf16[8,96,256]{2,1,0:T(8,128)(2,1)S(1)} %bitcast.87, bf16[8,96,256]{2,1,0:T(8,128)(2,1)S(1)} %bitcast.89, ...), custom_call_target="tpu_custom_call" | custom-call | flops 35999997952 | tf_op jit(solution)/shard_map/output_grad/pallas_call | solution.py:495
  117.0 4.4 %hidden_grad.1 = (bf16[2,2,96,960]{3,2,1,0:T(8,128)(2,1)S(1)}, bf16[2,2,96,960]{3,2,1,0:T(8,128)(2,1)S(1)}, bf16[2,2,96,960]{3,2,1,0:T(8,128)(2,1)S(1)}, bf16[2,2,96,960]{3,2,1,0:T(8,128)(2,1)S(1)}) custom-call(s32[1]{0:T(128)} %bitcast.own_ref, bf16[8,96,256]{2,1,0:T(8,128)(2,1)S(1)} %bitcast.84, bf16[8,96,256]{2,1,0:T(8,128)(2,1)S(1)} %bitcast.85, ...), custom_call_target="tpu_custom_call" | custom-call | flops 44999999488 | tf_op jit(solution)/shard_map/hidden_grad/pallas_call | solution.py:539
  122.6 7.5 %attend_back.1 = (bf16[576,1024]{1,0:T(8,128)(2,1)S(1)}, bf16[2,864,256]{2,1,0:T(8,128)(2,1)S(1)}, bf16[2,864,256]{2,1,0:T(8,128)(2,1)S(1)}) custom-call(s32[1,7]{1,0:T(1,128)S(1)} %copy-done.24, s32[1]{0:T(128)} %bitcast.1.place_ref, bf16[576,1024]{1,0:T(8,128)(2,1)S(1)} %get-tuple-element.180.qkv_ref, bf16[3,256,1024]{2,1,0:T(8,128)(2,1)S(1)} %get-tuple-element.181.qf_ref, ...), custom_call_target="tpu_custom_call" | custom-call | flops 80999997440 | tf_op jit(solution)/shard_map/attend_back/pallas_call | solution.py:420
  134.3 12.7 %collective-permute-done.41 = bf16[2,2,96,960]{3,2,1,0:T(8,128)(2,1)S(1)} collective-permute-done((bf16[2,2,96,960]{3,2,1,0:T(8,128)(2,1)S(1)}, bf16[2,2,96,960]{3,2,1,0:T(8,128)(2,1)S(1)}, u32[]{:S(2)}, u32[]{:S(2)}) %collective-permute-start.41) | collective-permute-done | bytes 737312 | tf_op jit(solution)/shard_map/ppermute | solution.py:984
  151.1 2.7 %collective-permute-done.39.far_ref = bf16[2,864,256]{2,1,0:T(8,128)(2,1)S(1)} collective-permute-done((bf16[2,864,256]{2,1,0:T(8,128)(2,1)S(1)}, bf16[2,864,256]{2,1,0:T(8,128)(2,1)S(1)}, u32[]{:S(2)}, u32[]{:S(2)}) %collective-permute-start.39) | collective-permute-done | bytes 884768 | tf_op jit(solution)/shard_map/ppermute | solution.py:989
  159.3 2.5 %collective-permute-done.49 = bf16[2,96,960]{2,1,0:T(8,128)(2,1)S(1)} collective-permute-done((bf16[2,96,960]{2,1,0:T(8,128)(2,1)S(1)}, bf16[2,96,960]{2,1,0:T(8,128)(2,1)S(1)}, u32[]{:S(2)}, u32[]{:S(2)}) %collective-permute-start.49) | collective-permute-done | bytes 368672 | tf_op jit(solution)/shard_map/ppermute | solution.py:984
  168.7 10.1 %collective-permute-done.45.far_ref = bf16[864,256]{1,0:T(8,128)(2,1)S(1)} collective-permute-done((bf16[864,256]{1,0:T(8,128)(2,1)S(1)}, bf16[864,256]{1,0:T(8,128)(2,1)S(1)}, u32[]{:S(2)}, u32[]{:S(2)}) %collective-permute-start.45) | collective-permute-done | bytes 442400 | tf_op jit(solution)/shard_map/ppermute | solution.py:989
  183.0 2.3 %collective-permute-done.55 = f32[48,256]{1,0:T(8,128)S(1)} collective-permute-done((f32[48,256]{1,0:T(8,128)S(1)}, f32[48,256]{1,0:T(8,128)S(1)}, u32[]{:S(2)}, u32[]{:S(2)}) %collective-permute-start.55) | collective-permute-done | bytes 49184 | tf_op jit(solution)/shard_map/ppermute | solution.py:984
  187.6 8.1 %collective-permute-done.60 = bf16[96,768]{1,0:T(8,128)(2,1)S(1)} collective-permute-done((bf16[96,768]{1,0:T(8,128)(2,1)S(1)}, bf16[96,768]{1,0:T(8,128)(2,1)S(1)}, u32[]{:S(2)}, u32[]{:S(2)}) %collective-permute-start.60) | collective-permute-done | bytes 147488 | tf_op jit(solution)/shard_map/ppermute | solution.py:989
  (221 shorter events, 70.8 us)
Async XLA Ops:
  4.2 17.9 %collective-permute-start.5 = (bf16[256,384]{1,0:T(8,128)(2,1)}, bf16[256,384]{1,0:T(8,128)(2,1)S(1)}, u32[]{:S(2)}, u32[]{:S(2)}) collective-permute-start(bf16[256,384]{1,0:T(8,128)(2,1)} %get-tuple-element.134.refs_10_), channel_id=1, source_target_pairs={{0,1},{1,0},{2,3},{3,2},{4,5},{5,4},{6,7},{7,6},{8,9},{9,8},{10,11... | collective-permute-start | bytes 589832 | tf_op jit(solution)/shard_map/ppermute | solution.py:989
  19.4 17.2 %collective-permute-start.9 = (bf16[192,384]{1,0:T(8,128)(2,1)}, bf16[192,384]{1,0:T(8,128)(2,1)S(1)}, u32[]{:S(2)}, u32[]{:S(2)}) collective-permute-start(bf16[192,384]{1,0:T(8,128)(2,1)} %get-tuple-element.140), channel_id=1, source_target_pairs={{0,1},{1,0},{2,3},{3,2},{4,5},{5,4},{6,7},{7,6},{8,9},{9,8},{10,11... | collective-permute-start | bytes 442376 | tf_op jit(solution)/shard_map/ppermute | solution.py:989
  31.5 17.2 %collective-permute-start.3 = (bf16[768,256]{1,0:T(8,128)(2,1)}, bf16[768,256]{1,0:T(8,128)(2,1)S(1)}, u32[]{:S(2)}, u32[]{:S(2)}) collective-permute-start(bf16[768,256]{1,0:T(8,128)(2,1)} %get-tuple-element.145.x0_ref), channel_id=1, source_target_pairs={{0,2},{1,3},{2,0},{3,1},{4,6},{5,7},{6,4},{7,5},{8,10},{9,11},{10,... | collective-permute-start | bytes 1179656 | tf_op jit(solution)/shard_map/ppermute | solution.py:989
  34.8 15.1 %collective-permute-start.2 = (bf16[768,256]{1,0:T(8,128)(2,1)}, bf16[768,256]{1,0:T(8,128)(2,1)S(1)}, u32[]{:S(2)}, u32[]{:S(2)}) collective-permute-start(bf16[768,256]{1,0:T(8,128)(2,1)} %get-tuple-element.145.x0_ref), channel_id=1, source_target_pairs={{0,1},{1,0},{2,3},{3,2},{4,5},{5,4},{6,7},{7,6},{8,9},{9,8},{10,11... | collective-permute-start | bytes 1179656 | tf_op jit(solution)/shard_map/ppermute | solution.py:989
  35.0 14.9 %collective-permute-start.8 = (bf16[4,240,384]{2,1,0:T(8,128)(2,1)S(1)}, bf16[4,240,384]{2,1,0:T(8,128)(2,1)S(1)}, u32[]{:S(2)}, u32[]{:S(2)}) collective-permute-start(bf16[4,240,384]{2,1,0:T(8,128)(2,1)S(1)} %pad_maximum_fusion.refs_0_), channel_id=1, source_target_pairs={{0,16},{4,20},{8,24},{12,28},{16,0},{20,4},{24,8},{28,12},{1,17},{... | collective-permute-start | bytes 2211848 | tf_op jit(solution)/shard_map/ppermute | solution.py:984
  50.6 15.1 %collective-permute-start.12 = (bf16[4,240,384]{2,1,0:T(8,128)(2,1)S(1)}, bf16[4,240,384]{2,1,0:T(8,128)(2,1)S(1)}, u32[]{:S(2)}, u32[]{:S(2)}) collective-permute-start(bf16[4,240,384]{2,1,0:T(8,128)(2,1)S(1)} %collective-permute-done.7.refs_1_), channel_id=1, source_target_pairs={{0,4},{4,0},{8,12},{12,8},{16,20},{20,16},{24,28},{28,24},{1,5},{5... | collective-permute-start | bytes 2211848 | tf_op jit(solution)/shard_map/ppermute | solution.py:984
  50.6 15.6 %collective-permute-start.13 = (bf16[4,240,384]{2,1,0:T(8,128)(2,1)S(1)}, bf16[4,240,384]{2,1,0:T(8,128)(2,1)S(1)}, u32[]{:S(2)}, u32[]{:S(2)}) collective-permute-start(bf16[4,240,384]{2,1,0:T(8,128)(2,1)S(1)} %collective-permute-done.8.refs_2_), channel_id=1, source_target_pairs={{0,4},{4,0},{8,12},{12,8},{16,20},{20,16},{24,28},{28,24},{1,5},{5... | collective-permute-start | bytes 2211848 | tf_op jit(solution)/shard_map/ppermute | solution.py:984
  51.2 14.6 %collective-permute-start.4 = (bf16[768,256]{1,0:T(8,128)(2,1)S(1)}, bf16[768,256]{1,0:T(8,128)(2,1)S(1)}, u32[]{:S(2)}, u32[]{:S(2)}) collective-permute-start(bf16[768,256]{1,0:T(8,128)(2,1)S(1)} %collective-permute-done.3.x2_ref), channel_id=1, source_target_pairs={{0,1},{1,0},{2,3},{3,2},{4,5},{5,4},{6,7},{7,6},{8,9},{9,8},{10,11... | collective-permute-start | bytes 1179656 | tf_op jit(solution)/shard_map/ppermute | solution.py:989
  65.7 15.0 %collective-permute-start.19 = (bf16[2,240,384]{2,1,0:T(8,128)(2,1)S(1)}, bf16[2,240,384]{2,1,0:T(8,128)(2,1)S(1)}, u32[]{:S(2)}, u32[]{:S(2)}) collective-permute-start(bf16[2,240,384]{2,1,0:T(8,128)(2,1)S(1)} %collective-permute-done.14.refs_3_), channel_id=1, source_target_pairs={{0,4},{4,0},{8,12},{12,8},{16,20},{20,16},{24,28},{28,24},{1,5},{5... | collective-permute-start | bytes 1105928 | tf_op jit(solution)/shard_map/ppermute | solution.py:984
  65.8 16.5 %collective-permute-start.20 = (bf16[2,240,384]{2,1,0:T(8,128)(2,1)S(1)}, bf16[2,240,384]{2,1,0:T(8,128)(2,1)S(1)}, u32[]{:S(2)}, u32[]{:S(2)}) collective-permute-start(bf16[2,240,384]{2,1,0:T(8,128)(2,1)S(1)} %collective-permute-done.15.refs_4_), channel_id=1, source_target_pairs={{0,4},{4,0},{8,12},{12,8},{16,20},{20,16},{24,28},{28,24},{1,5},{5... | collective-permute-start | bytes 1105928 | tf_op jit(solution)/shard_map/ppermute | solution.py:984
  95.8 14.2 %collective-permute-start.36 = (bf16[4,256,768]{2,1,0:T(8,128)(2,1)S(1)}, bf16[4,256,768]{2,1,0:T(8,128)(2,1)S(1)}, u32[]{:S(2)}, u32[]{:S(2)}) collective-permute-start(bf16[4,256,768]{2,1,0:T(8,128)(2,1)S(1)} %get-tuple-element.157.act_ref), channel_id=1, source_target_pairs={{0,4},{4,0},{8,12},{12,8},{16,20},{20,16},{24,28},{28,24},{1,5},{5... | collective-permute-start | bytes 4718600 | tf_op jit(solution)/shard_map/ppermute | solution.py:984
  105.6 15.9 %collective-permute-start.32 = (bf16[192,256]{1,0:T(8,128)(2,1)S(1)}, bf16[192,256]{1,0:T(8,128)(2,1)S(1)}, u32[]{:S(2)}, u32[]{:S(2)}) collective-permute-start(bf16[192,256]{1,0:T(8,128)(2,1)S(1)} %get-tuple-element.187), channel_id=1, source_target_pairs={{0,1},{1,0},{2,3},{3,2},{4,5},{5,4},{6,7},{7,6},{8,9},{9,8},{10,11... | collective-permute-start | bytes 294920 | tf_op jit(solution)/shard_map/ppermute | solution.py:989
  107.2 14.3 %collective-permute-start.33 = (bf16[192,256]{1,0:T(8,128)(2,1)S(1)}, bf16[192,256]{1,0:T(8,128)(2,1)S(1)}, u32[]{:S(2)}, u32[]{:S(2)}) collective-permute-start(bf16[192,256]{1,0:T(8,128)(2,1)S(1)} %get-tuple-element.188), channel_id=1, source_target_pairs={{0,2},{1,3},{2,0},{3,1},{4,6},{5,7},{6,4},{7,5},{8,10},{9,11},{10,... | collective-permute-start | bytes 294920 | tf_op jit(solution)/shard_map/ppermute | solution.py:989
  114.0 17.8 %collective-permute-start.43 = (bf16[2,2,96,768]{3,2,1,0:T(8,128)(2,1)S(1)}, bf16[2,2,96,768]{3,2,1,0:T(8,128)(2,1)S(1)}, u32[]{:S(2)}, u32[]{:S(2)}) collective-permute-start(bf16[2,2,96,768]{3,2,1,0:T(8,128)(2,1)S(1)} %get-tuple-element.217), channel_id=1, source_target_pairs={{0,8},{4,12},{8,0},{12,4},{16,24},{20,28},{24,16},{28,20},{1,9},{5... | collective-permute-start | bytes 1769480 | tf_op jit(solution)/shard_map/ppermute | solution.py:984
  115.5 17.1 %collective-permute-start.44 = (bf16[2,2,96,768]{3,2,1,0:T(8,128)(2,1)S(1)}, bf16[2,2,96,768]{3,2,1,0:T(8,128)(2,1)S(1)}, u32[]{:S(2)}, u32[]{:S(2)}) collective-permute-start(bf16[2,2,96,768]{3,2,1,0:T(8,128)(2,1)S(1)} %get-tuple-element.218), channel_id=1, source_target_pairs={{0,16},{4,20},{8,24},{12,28},{16,0},{20,4},{24,8},{28,12},{1,17},{... | collective-permute-start | bytes 1769480 | tf_op jit(solution)/shard_map/ppermute | solution.py:984
  121.5 25.5 %collective-permute-start.41 = (bf16[2,2,96,960]{3,2,1,0:T(8,128)(2,1)S(1)}, bf16[2,2,96,960]{3,2,1,0:T(8,128)(2,1)S(1)}, u32[]{:S(2)}, u32[]{:S(2)}) collective-permute-start(bf16[2,2,96,960]{3,2,1,0:T(8,128)(2,1)S(1)} %get-tuple-element.215), channel_id=1, source_target_pairs={{0,8},{4,12},{8,0},{12,4},{16,24},{20,28},{24,16},{28,20},{1,9},{5... | collective-permute-start | bytes 2211848 | tf_op jit(solution)/shard_map/ppermute | solution.py:984
  122.1 26.5 %collective-permute-start.42 = (bf16[2,2,96,960]{3,2,1,0:T(8,128)(2,1)S(1)}, bf16[2,2,96,960]{3,2,1,0:T(8,128)(2,1)S(1)}, u32[]{:S(2)}, u32[]{:S(2)}) collective-permute-start(bf16[2,2,96,960]{3,2,1,0:T(8,128)(2,1)S(1)} %get-tuple-element.216), channel_id=1, source_target_pairs={{0,16},{4,20},{8,24},{12,28},{16,0},{20,4},{24,8},{28,12},{1,17},{... | collective-permute-start | bytes 2211848 | tf_op jit(solution)/shard_map/ppermute | solution.py:984
  131.7 18.7 %collective-permute-start.40 = (bf16[2,2,2,1,48,576]{5,4,3,2,1,0:T(8,128)(2,1)S(1)}, bf16[2,2,2,1,48,576]{5,4,3,2,1,0:T(8,128)(2,1)S(1)}, u32[]{:S(2)}, u32[]{:S(2)}) collective-permute-start(bf16[2,2,2,1,48,576]{5,4,3,2,1,0:T(8,128)(2,1)S(1)} %get-tuple-element.214), channel_id=1, source_target_pairs={{0,4},{4,0},{8,12},{12,8},{16,20},{20,16},{24,28},{28,24},{1,5},{5... | collective-permute-start | bytes 1327112 | tf_op jit(solution)/shard_map/ppermute | solution.py:984
  131.8 22.1 %collective-permute-start.39 = (bf16[2,864,256]{2,1,0:T(8,128)(2,1)S(1)}, bf16[2,864,256]{2,1,0:T(8,128)(2,1)S(1)}, u32[]{:S(2)}, u32[]{:S(2)}) collective-permute-start(bf16[2,864,256]{2,1,0:T(8,128)(2,1)S(1)} %get-tuple-element.211), channel_id=1, source_target_pairs={{0,1},{1,0},{2,3},{3,2},{4,5},{5,4},{6,7},{7,6},{8,9},{9,8},{10,11... | collective-permute-start | bytes 2654216 | tf_op jit(solution)/shard_map/ppermute | solution.py:989
  132.7 22.9 %collective-permute-start.51 = (bf16[2,96,768]{2,1,0:T(8,128)(2,1)S(1)}, bf16[2,96,768]{2,1,0:T(8,128)(2,1)S(1)}, u32[]{:S(2)}, u32[]{:S(2)}) collective-permute-start(bf16[2,96,768]{2,1,0:T(8,128)(2,1)S(1)} %fusion.9), channel_id=1, source_target_pairs={{0,8},{4,12},{8,0},{12,4},{16,24},{20,28},{24,16},{28,20},{1,9},{5... | collective-permute-start | bytes 884744 | tf_op jit(solution)/shard_map/ppermute | solution.py:984
  157.1 21.6 %collective-permute-start.45 = (bf16[864,256]{1,0:T(8,128)(2,1)S(1)}, bf16[864,256]{1,0:T(8,128)(2,1)S(1)}, u32[]{:S(2)}, u32[]{:S(2)}) collective-permute-start(bf16[864,256]{1,0:T(8,128)(2,1)S(1)} %get-tuple-element.230), channel_id=1, source_target_pairs={{0,2},{1,3},{2,0},{3,1},{4,6},{5,7},{6,4},{7,5},{8,10},{9,11},{10,... | collective-permute-start | bytes 1327112 | tf_op jit(solution)/shard_map/ppermute | solution.py:989
  161.8 19.1 %collective-permute-start.59 = (bf16[2,96,768]{2,1,0:T(8,128)(2,1)S(1)}, bf16[2,96,768]{2,1,0:T(8,128)(2,1)S(1)}, u32[]{:S(2)}, u32[]{:S(2)}) collective-permute-start(bf16[2,96,768]{2,1,0:T(8,128)(2,1)S(1)} %pad_maximum_fusion.3), channel_id=1, source_target_pairs={{0,1},{1,0},{2,3},{3,2},{4,5},{5,4},{6,7},{7,6},{8,9},{9,8},{10,11... | collective-permute-start | bytes 884744 | tf_op jit(solution)/shard_map/ppermute | solution.py:989
  164.7 22.1 %collective-permute-start.57 = (bf16[2,96,960]{2,1,0:T(8,128)(2,1)S(1)}, bf16[2,96,960]{2,1,0:T(8,128)(2,1)S(1)}, u32[]{:S(2)}, u32[]{:S(2)}) collective-permute-start(bf16[2,96,960]{2,1,0:T(8,128)(2,1)S(1)} %pad_maximum_fusion.2), channel_id=1, source_target_pairs={{0,1},{1,0},{2,3},{3,2},{4,5},{5,4},{6,7},{7,6},{8,9},{9,8},{10,11... | collective-permute-start | bytes 1105928 | tf_op jit(solution)/shard_map/ppermute | solution.py:989
  165.6 14.4 %collective-permute-start.53 = (bf16[1,48,576]{2,1,0:T(8,128)(2,1)S(1)}, bf16[1,48,576]{2,1,0:T(8,128)(2,1)S(1)}, u32[]{:S(2)}, u32[]{:S(2)}) collective-permute-start(bf16[1,48,576]{2,1,0:T(8,128)(2,1)S(1)} %get-tuple-element.259), channel_id=1, source_target_pairs={{0,8},{4,12},{8,0},{12,4},{16,24},{20,28},{24,16},{28,20},{1,9},{5... | collective-permute-start | bytes 165896 | tf_op jit(solution)/shard_map/ppermute | solution.py:984
  (70 other events, 867.4 us)
